TPU v7x, 32 devices: a whole 2x2x4 slice. The times are simulated.
32 devices in a mesh: dp: 16 (over z, y, x), mp: 2 (over core).
Axes of the slice: x: 2, y: 2, z: 4, core: 2. Of those that a mesh axis runs over, the one named last changes fastest.
Arguments:
- partial_grads: bfloat16 [16, 2, 2, 512, 1024], P('dp', None, None, None, 'mp')
- factors: bfloat16 [2, 4, 512, 1024], P('mp', None, 'dp'), as said below
- inverse_factors: bfloat16 [2, 4, 512, 1024], P('mp', None, 'dp'), as said below
- probes: bfloat16 [2, 4, 512, 512], P('mp', None, 'dp'), may hold values from -6 to 6
- slot_table: int32 [2, 4], P('mp'), may hold values from 0 to 3, as said below
Outputs:
- preconditioned: bfloat16 [2, 2, 512, 1024], P(None, None, 'dp', 'mp')
- new_factors: bfloat16 [2, 4, 512, 1024], P('mp', None, 'dp')
Inputs may be any that keep to these rules, and one draw needn't show every extreme that they name: `slot_table`: in each row the 4 entries are distinct slots; slot j belongs to owner j // 4 (an owner is a group of 16 consecutive dp devices; the starting program sends slots 2k and 2k+1 to dp device 16k for updating), and in every row some owner holds 4 blocks. `factors`: both halves of every slot are upper triangular with a positive diagonal. `inverse_factors`: both halves of every slot are upper triangular with a positive diagonal.
All inputs are finite; a program needn't handle non-finite values. Where the computation divides by a largest or mean magnitude, that divisor is 1e-20 or more.
Results may differ from a plain program's by a relative error of at most 0.011.
Values may be sent and summed in bfloat16 or wider, within the bound.
No kernel may reach another device: no remote copies, remote signals or barrier semaphores. Data moves between devices by JAX's collectives and lax.ppermute only.
A program may use at most 64 MiB of HBM per device.

v0:
```python
import functools
import math

import jax
import jax.numpy as jnp
from jax import lax
from jax.experimental import pallas as pl
from jax.experimental.pallas import tpu as pltpu
from jax.sharding import PartitionSpec as P

CLIP_RMS = 0.3
LEARN_RATE = 0.1
EPS_NORM = 1e-06
LANES = 128
CHUNKS = 2
VMEM_GRANT = 16 * 2**20
FLOAT = jnp.float32
HALF = jnp.bfloat16


VMEM_SPEC = pl.BlockSpec(memory_space=pltpu.VMEM)
SMEM_SPEC = pl.BlockSpec(memory_space=pltpu.SMEM)


def product(left_op, right_op, left_dim=1, right_dim=0):
    return lax.dot_general(
        left_op, right_op, (((left_dim,), (right_dim,)), ((), ())), preferred_element_type=FLOAT
    )


def flip(array, devices, mask):
    return lax.ppermute(array, "dp", [(i, i ^ mask) for i in range(devices)])


def pick(array, index, axis):
    return lax.dynamic_index_in_dim(array, index, axis, keepdims=False)


def unflip(pieces, own):
    stacked = jnp.stack(pieces)
    return jnp.stack([pick(stacked, own ^ k, 0) for k in range(len(pieces))])


def call(kernel, out_shape, scratch, flops, smem, *operands):
    moved = sum(x.size * x.dtype.itemsize for x in (*operands, *jax.tree.leaves(out_shape)))
    return pl.pallas_call(
        kernel,
        out_shape=out_shape,
        in_specs=[SMEM_SPEC] * smem + [VMEM_SPEC] * (len(operands) - smem),
        out_specs=jax.tree.map(lambda _: VMEM_SPEC, out_shape),
        scratch_shapes=scratch,
        cost_estimate=pl.CostEstimate(flops=flops, bytes_accessed=moved, transcendentals=0),
        compiler_params=pltpu.CompilerParams(vmem_limit_bytes=VMEM_GRANT),
    )(*operands)


class Plan:
    def __init__(self, devices, blocks, size):
        self.devices, self.blocks, self.size = devices, blocks, size
        self.group = devices // blocks
        self.rows = size // devices
        self.first = [z * (size // blocks) // LANES * LANES for z in range(blocks)]

    def spots(self):
        offset = 0
        for z in range(self.blocks):
            for what in range(5):
                first = self.first[z] if what < 4 else 0
                yield z, what, first, offset
                offset += self.size - first

    def packed(self):
        return sum(self.size - first for _, _, first, _ in self.spots())


def pack_kernel(plan, where, *refs):
    pieces, out, stack = refs[: plan.blocks], refs[-2], refs[-1]
    size = plan.size
    for k, piece in enumerate(pieces):
        stack[where[0] ^ k] = piece[...]
    for z, what, first, offset in plan.spots():
        out[:, offset : offset + size - first] = stack[z, :, what * size + first : (what + 1) * size]


def spread(plan, where, pieces, targets):
    size, rows = plan.size, plan.rows
    for z in range(1, plan.blocks):
        for target in targets[:4]:
            if target is not None and plan.first[z]:
                span = size // plan.blocks
                target[z * span : (z + 1) * span, : plan.first[z]] = jnp.zeros((span, plan.first[z]), HALF)
    for k, piece in enumerate(pieces):
        for z, what, first, offset in plan.spots():
            if targets[what] is not None:
                row = pl.multiple_of((z * plan.group + (where[1] ^ k)) * rows, rows)
                targets[what][pl.ds(row, rows), first:] = piece[:, offset : offset + size - first]


def probe_kernel(plan, where, *refs):
    pieces = refs[: plan.group]
    left, right, left_gram, right_gram, left_inv, right_inv, probe = refs[plan.group :]
    spread(plan, where, pieces, (left, right, left_inv, right_inv, probe))
    half_conjugate = product(left_inv[...], probe[...], 0, 0).astype(HALF)
    conjugate = product(half_conjugate, right_inv[...]).astype(HALF)
    left_gram[...] = product(conjugate, conjugate, 1, 1)
    right_gram[...] = product(conjugate, conjugate, 0, 0)


def gather_kernel(plan, where, *refs):
    terms, outs = refs[: plan.group], refs[plan.group :]
    for k, out in enumerate(outs):
        block = where[0] ^ k
        total = terms[0][block].astype(FLOAT)
        for term in terms[1:]:
            total = total + term[block].astype(FLOAT)
        out[...] = total.astype(HALF)


def sum_kernel(blocks, *refs):
    terms, (out, squares) = refs[:-2], refs[-2:]
    found, start = 0.0, 0
    for i in range(0, len(terms), blocks):
        total = terms[i][...].astype(FLOAT)
        for term in terms[i + 1 : i + blocks]:
            total = total + term[...].astype(FLOAT)
        out[start : start + total.shape[0]] = total.astype(HALF)
        start += total.shape[0]
        found = found + jnp.sum(jnp.sum(total * total, axis=(0, 1)))
    squares[...] = jnp.full(squares.shape, found)


def bound_of(limit, squares):
    return jnp.minimum(1.0, limit / jnp.sqrt(squares + EPS_NORM))


def whiten_kernel(plan, limit, where, *refs):
    left, right, pieces = refs[0], refs[1], refs[2 : 2 + plan.group]
    grad, left_gram, right_gram, own_clip = refs[2 + plan.group :]
    for k, piece in enumerate(pieces):
        for z in range(plan.blocks):
            row = pl.multiple_of((z * plan.group + (where[1] ^ k)) * plan.rows, plan.rows)
            grad[pl.ds(row, plan.rows), :] = piece[z]
    wide = grad[...].astype(FLOAT)
    clip = bound_of(limit, jnp.sum(wide * wide, keepdims=True))
    own_clip[...] = jnp.broadcast_to(clip, own_clip.shape)
    left_times = (clip * product(left[...], grad[...])).astype(HALF)
    whitened = product(left_times, right[...], 1, 1).astype(HALF)
    left_gram[...] = product(whitened, whitened, 1, 1)
    right_gram[...] = product(whitened, whitened, 0, 0)


def step_factor(factor, ratio, first_ref, second_ref):
    first, second = ratio * first_ref[...], second_ref[...]
    bound_value = jnp.max(jnp.abs(first + second), keepdims=True) + EPS_NORM
    row = lax.broadcasted_iota(jnp.int32, first.shape, 0)
    column = lax.broadcasted_iota(jnp.int32, first.shape, 1)
    change = jnp.where(row <= column, first - second, 0.0).astype(HALF)
    moved_rows = product(change, factor)
    return (factor.astype(FLOAT) - LEARN_RATE / bound_value * moved_rows).astype(HALF)


def finish_kernel(plan, limit, where, *refs):
    sums, refs = refs[: plan.group], refs[plan.group :]
    own_clip, left, right, grad, left_p, right_p, left_q, right_q = refs[:8]
    outs, (new_left, new_right, square, result) = refs[8:-4], refs[-4:]
    squares = sums[0][0:1, 0:1]
    for ref in sums[1:]:
        squares = squares + ref[0:1, 0:1]
    clip = bound_of(limit, squares)
    ratio = clip / own_clip[0:1, 0:1]
    ratio = ratio * ratio
    size, rows = plan.size, plan.rows
    new_left[...] = step_factor(left[...], ratio, left_p, left_q)
    new_right[...] = step_factor(right[...], ratio, right_p, right_q)
    square[...] = product(new_left[...], new_left[...], 0, 0).astype(HALF)
    precond_right = product(new_right[...], new_right[...], 0, 0).astype(HALF)

    def at(z):
        return pl.ds(pl.multiple_of((z * plan.group + where[1]) * rows, rows), rows)

    precond_left = jnp.concatenate([square[at(z), :] for z in range(plan.blocks)], axis=0)
    middle = (clip * product(precond_left, grad[...])).astype(HALF)
    result[...] = product(middle, precond_right).astype(HALF).reshape(plan.blocks, rows, size)
    for k, out in enumerate(outs):
        z = where[0] ^ k
        out[:, :size] = new_left[at(z), :]
        out[:, size : 2 * size] = new_right[at(z), :]
        out[:, 2 * size :] = result[z]


def place_kernel(plan, where, slots, old_state, *refs):
    pieces, (precond, new_state) = refs[: plan.blocks], refs[plan.blocks :]
    size = plan.size
    new_state[...] = old_state[...]
    for k, piece in enumerate(pieces):
        precond[where[0] ^ k] = piece[:, 2 * size :]
        new_state[slots[where[0] ^ k]] = piece[:, : 2 * size]


def shaped(shape, dtype=HALF):
    return jax.ShapeDtypeStruct(shape, dtype)


def body(partial_grads, factors, inverse_factors, probes, slot_table):
    devices = lax.axis_size("dp")
    halves = lax.axis_size("mp")
    me = lax.axis_index("dp")
    experts, block_rows, size, columns = partial_grads.shape[1:]
    blocks = experts * block_rows
    plan = Plan(devices, blocks, size)
    group, rows = plan.group, plan.rows
    my_block = me // group
    my_place = me % group
    where = jnp.stack([my_block, my_place]).astype(jnp.int32)
    slot_row = slot_table[0]
    in_tiles = rows % 16 == 0
    limit = CLIP_RMS * math.sqrt(blocks * size * columns * halves)

    grads = partial_grads[0].reshape(blocks, blocks, group, rows, columns)
    step = blocks // CHUNKS
    chunks = []
    for i in range(CHUNKS):
        chunk = grads[:, i * step : (i + 1) * step]
        chunks.append(
            [pick(chunk, my_place, 2)]
            + [flip(pick(chunk, my_place ^ k, 2), devices, k) for k in range(1, group)]
        )

    old_state = factors[0]
    wide = jnp.concatenate([old_state, inverse_factors[0], probes[0]], axis=2)
    chosen = jnp.take(wide, slot_row, axis=0)
    pieces = [pick(chosen, my_block, 0)] + [
        flip(pick(chosen, my_block ^ k, 0), devices, k * group) for k in range(1, blocks)
    ]
    if in_tiles:
        quarter = call(
            functools.partial(pack_kernel, plan),
            shaped((rows, plan.packed())),
            [pltpu.VMEM((blocks, rows, 5 * size), HALF)],
            0,
            1,
            where,
            *pieces,
        )
    else:
        quarter = unflip(pieces, my_block)

    terms = []
    for chunk in chunks:
        mine = call(
            functools.partial(gather_kernel, plan),
            tuple(shaped((step, rows, columns)) for _ in range(blocks)),
            [],
            0,
            1,
            where,
            *chunk,
        )
        terms += [mine[0]] + [flip(mine[k], devices, k * group) for k in range(1, blocks)]
    grad_quarter, squares = call(
        functools.partial(sum_kernel, blocks),
        (shaped((blocks, rows, columns)), shaped((8, LANES), FLOAT)),
        [],
        0,
        0,
        *terms,
    )

    states = [quarter] + [flip(quarter, devices, k) for k in range(1, group)]
    quarters = [grad_quarter] + [flip(grad_quarter, devices, k) for k in range(1, group)]

    bit = 1
    while bit < halves:
        other = lax.ppermute(squares, "mp", [(i, i ^ bit) for i in range(halves)])
        squares = squares + other
        bit *= 2
    bit = 1
    while bit < blocks:
        squares = squares + flip(squares, devices, bit * group)
        bit *= 2
    sums = [squares] + [flip(squares, devices, k) for k in range(1, group)]

    gram = shaped((size, size), FLOAT)
    square = shaped((size, size))
    matmul = 2 * size**3
    if in_tiles:
        left_q, right_q, left_c, right_c = call(
            functools.partial(probe_kernel, plan),
            (square, square, gram, gram),
            [pltpu.VMEM((size, size), HALF)] * 3,
            4 * matmul,
            1,
            where,
            *states,
        )
        gradient, left_w, right_w, own_clip = call(
            functools.partial(whiten_kernel, plan, limit),
            (shaped((size, columns)), gram, gram, shaped((8, LANES), FLOAT)),
            [],
            4 * matmul,
            1,
            where,
            left_q,
            right_q,
            *quarters,
        )
        back = call(
            functools.partial(finish_kernel, plan, limit),
            tuple(shaped((rows, 2 * size + columns)) for _ in range(blocks)),
            [pltpu.VMEM((size, size), HALF)] * 3 + [pltpu.VMEM((blocks, rows, columns), HALF)],
            5 * matmul,
            1,
            where,
            *sums,
            own_clip,
            left_q,
            right_q,
            gradient,
            left_w,
            right_w,
            left_c,
            right_c,
        )
    else:
        back = plain_block(plan, limit, my_block, my_place, sums, states, quarters)
    back = [back[0]] + [flip(back[k], devices, k * group) for k in range(1, blocks)]
    precond, new_state = call(
        functools.partial(place_kernel, plan),
        (shaped((blocks, rows, columns)), shaped(old_state.shape)),
        [],
        0,
        2,
        where,
        slot_row,
        old_state,
        *back,
    )
    return (precond.reshape(experts, block_rows, rows, columns), new_state[None])


def plain_block(plan, limit, my_block, my_place, sums, states, quarters):
    size, blocks, group, rows = plan.size, plan.blocks, plan.group, plan.rows
    state = unflip(states, my_place).transpose(1, 0, 2, 3).reshape(size, 5 * size)
    gradient = unflip(quarters, my_place).transpose(1, 0, 2, 3).reshape(size, -1)
    clip = bound_of(limit, functools.reduce(jnp.add, sums)[0:1, 0:1])
    left_q, right_q, left_inv, right_inv, probe_mat = jnp.split(state, 5, axis=1)
    half_conjugate = product(left_inv, probe_mat, 0, 0).astype(HALF)
    conjugate = product(half_conjugate, right_inv).astype(HALF)
    left_times = (clip * product(left_q, gradient)).astype(HALF)
    whitened = product(left_times, right_q, 1, 1).astype(HALF)
    new_left = step_factor(
        left_q, 1.0, product(whitened, whitened, 1, 1), product(conjugate, conjugate, 1, 1)
    )
    new_right = step_factor(
        right_q, 1.0, product(whitened, whitened, 0, 0), product(conjugate, conjugate, 0, 0)
    )
    precond_left = product(new_left, new_left, 0, 0).astype(HALF)
    precond_right = product(new_right, new_right, 0, 0).astype(HALF)

    def my_rows(array):
        return pick(array.reshape(blocks, group, rows, -1), my_place, 1)

    middle = (clip * product(my_rows(precond_left).reshape(blocks * rows, size), gradient)).astype(HALF)
    result = product(middle, precond_right).astype(HALF).reshape(blocks, rows, -1)
    back = jnp.concatenate([my_rows(new_left), my_rows(new_right), result], axis=2)
    return [pick(back, my_block ^ k, 0) for k in range(blocks)]


def solution(mesh):
    return jax.shard_map(
        body,
        mesh=mesh,
        in_specs=(
            P("dp", None, None, None, "mp"),
            P("mp", None, "dp", None),
            P("mp", None, "dp", None),
            P("mp", None, "dp", None),
            P("mp", None),
        ),
        out_specs=(P(None, None, "dp", "mp"), P("mp", None, "dp", None)),
        check_vma=False,
    )
```

profile of v0, /device:TPU:0, one launch (start us, length us, event | category | flops | bytes accessed | tf_op | source)
XLA Modules:
  0.0 92.5 jit_solution(16543104850813784477)
XLA Ops:
  4.0 3.1 %collective-permute-start.18 = (bf16[32,2560]{1,0:T(8,128)(2,1)S(1)}, bf16[32,2560]{1,0:T(8,128)(2,1)S(1)}, u32[]{:S(2)}, u32[]{:S(2)}) collective-permute-start(bf16[32,2560]{1,0:T(8,128)(2,1)S(1)} %get-tuple-element.62), channel_id=1, source_target_pairs={{0,8},{2,10},{4,12},{6,14},{8,0},{10,2},{12,4},{14,6},{16,24},{18,... | collective-permute-start | bytes 491528 | tf_op jit(solution)/shard_map/ppermute | solution.py:32
  7.1 2.6 %collective-permute-start.19 = (bf16[32,2560]{1,0:T(8,128)(2,1)S(1)}, bf16[32,2560]{1,0:T(8,128)(2,1)S(1)}, u32[]{:S(2)}, u32[]{:S(2)}) collective-permute-start(bf16[32,2560]{1,0:T(8,128)(2,1)S(1)} %get-tuple-element.61), channel_id=1, source_target_pairs={{0,16},{2,18},{4,20},{6,22},{8,24},{10,26},{12,28},{14,30},{16,0},... | collective-permute-start | bytes 491528 | tf_op jit(solution)/shard_map/ppermute | solution.py:32
  14.8 2.0 %collective-permute-start.8 = (bf16[4,2,32,512]{3,2,1,0:T(8,128)(2,1)S(1)}, bf16[4,2,32,512]{3,2,1,0:T(8,128)(2,1)S(1)}, u32[]{:S(2)}, u32[]{:S(2)}) collective-permute-start(bf16[4,2,32,512]{3,2,1,0:T(8,128)(2,1)S(1)} %get-tuple-element.52), channel_id=1, source_target_pairs={{0,6},{2,4},{4,2},{6,0},{8,14},{10,12},{12,10},{14,8},{16,22},{18,... | collective-permute-start | bytes 786440 | tf_op jit(solution)/shard_map/ppermute | solution.py:32
  16.9 4.1 %collective-permute-done.19.refs_2_ = bf16[32,2560]{1,0:T(8,128)(2,1)S(1)} collective-permute-done((bf16[32,2560]{1,0:T(8,128)(2,1)S(1)}, bf16[32,2560]{1,0:T(8,128)(2,1)S(1)}, u32[]{:S(2)}, u32[]{:S(2)}) %collective-permute-start.19) | collective-permute-done | bytes 163872 | tf_op jit(solution)/shard_map/ppermute | solution.py:32
  21.0 2.0 %collective-permute-start = (bf16[4,2,32,512]{3,2,1,0:T(8,128)(2,1)S(1)}, bf16[4,2,32,512]{3,2,1,0:T(8,128)(2,1)S(1)}, u32[]{:S(2)}, u32[]{:S(2)}) collective-permute-start(bf16[4,2,32,512]{3,2,1,0:T(8,128)(2,1)S(1)} %get-tuple-element.58), channel_id=1, source_target_pairs={{0,2},{2,0},{4,6},{6,4},{8,10},{10,8},{12,14},{14,12},{16,18},{18,... | collective-permute-start | bytes 786440 | tf_op jit(solution)/shard_map/ppermute | solution.py:32
  28.7 3.3 %collective-permute-done.refs_1_ = bf16[4,2,32,512]{3,2,1,0:T(8,128)(2,1)S(1)} collective-permute-done((bf16[4,2,32,512]{3,2,1,0:T(8,128)(2,1)S(1)}, bf16[4,2,32,512]{3,2,1,0:T(8,128)(2,1)S(1)}, u32[]{:S(2)}, u32[]{:S(2)}) %collective-permute-start) | collective-permute-done | bytes 262176 | tf_op jit(solution)/shard_map/ppermute | solution.py:32
  32.0 2.4 %collective-permute-start.23 = (bf16[32,7168]{1,0:T(8,128)(2,1)S(1)}, bf16[32,7168]{1,0:T(8,128)(2,1)S(1)}, u32[]{:S(2)}, u32[]{:S(2)}) collective-permute-start(bf16[32,7168]{1,0:T(8,128)(2,1)S(1)} %shard_map.71.refs_0_), channel_id=1, source_target_pairs={{0,6},{2,4},{4,2},{6,0},{8,14},{10,12},{12,10},{14,8},{16,22},{18,... | collective-permute-start | bytes 1376264 | tf_op jit(solution)/shard_map/ppermute | solution.py:32
  35.1 2.6 %collective-permute-done.1.refs_2_ = bf16[4,2,32,512]{3,2,1,0:T(8,128)(2,1)S(1)} collective-permute-done((bf16[4,2,32,512]{3,2,1,0:T(8,128)(2,1)S(1)}, bf16[4,2,32,512]{3,2,1,0:T(8,128)(2,1)S(1)}, u32[]{:S(2)}, u32[]{:S(2)}) %collective-permute-start.1) | collective-permute-done | bytes 262176 | tf_op jit(solution)/shard_map/ppermute | solution.py:32
  37.7 2.9 %collective-permute-start.10 = (bf16[2,32,512]{2,1,0:T(8,128)(2,1)S(1)}, bf16[2,32,512]{2,1,0:T(8,128)(2,1)S(1)}, u32[]{:S(2)}, u32[]{:S(2)}) collective-permute-start(bf16[2,32,512]{2,1,0:T(8,128)(2,1)S(1)} %get-tuple-element.32), channel_id=1, source_target_pairs={{0,16},{2,18},{4,20},{6,22},{8,24},{10,26},{12,28},{14,30},{16,0},... | collective-permute-start | bytes 196616 | tf_op jit(solution)/shard_map/ppermute | solution.py:32
  40.6 2.3 %collective-permute-start.11 = (bf16[2,32,512]{2,1,0:T(8,128)(2,1)S(1)}, bf16[2,32,512]{2,1,0:T(8,128)(2,1)S(1)}, u32[]{:S(2)}, u32[]{:S(2)}) collective-permute-start(bf16[2,32,512]{2,1,0:T(8,128)(2,1)S(1)} %get-tuple-element.33), channel_id=1, source_target_pairs={{0,24},{2,26},{4,28},{6,30},{8,16},{10,18},{12,20},{14,22},{16,8},... | collective-permute-start | bytes 196616 | tf_op jit(solution)/shard_map/ppermute | solution.py:32
  43.6 2.5 %collective-permute-start.9 = (bf16[2,32,512]{2,1,0:T(8,128)(2,1)S(1)}, bf16[2,32,512]{2,1,0:T(8,128)(2,1)S(1)}, u32[]{:S(2)}, u32[]{:S(2)}) collective-permute-start(bf16[2,32,512]{2,1,0:T(8,128)(2,1)S(1)} %get-tuple-element.31), channel_id=1, source_target_pairs={{0,8},{2,10},{4,12},{6,14},{8,0},{10,2},{12,4},{14,6},{16,24},{18,... | collective-permute-start | bytes 196616 | tf_op jit(solution)/shard_map/ppermute | solution.py:32
  46.7 2.3 %collective-permute-start.3 = (bf16[2,32,512]{2,1,0:T(8,128)(2,1)S(1)}, bf16[2,32,512]{2,1,0:T(8,128)(2,1)S(1)}, u32[]{:S(2)}, u32[]{:S(2)}) collective-permute-start(bf16[2,32,512]{2,1,0:T(8,128)(2,1)S(1)} %get-tuple-element.27), channel_id=1, source_target_pairs={{0,8},{2,10},{4,12},{6,14},{8,0},{10,2},{12,4},{14,6},{16,24},{18,... | collective-permute-start | bytes 196616 | tf_op jit(solution)/shard_map/ppermute | solution.py:32
  49.0 1.9 %collective-permute-start.4 = (bf16[2,32,512]{2,1,0:T(8,128)(2,1)S(1)}, bf16[2,32,512]{2,1,0:T(8,128)(2,1)S(1)}, u32[]{:S(2)}, u32[]{:S(2)}) collective-permute-start(bf16[2,32,512]{2,1,0:T(8,128)(2,1)S(1)} %get-tuple-element.28), channel_id=1, source_target_pairs={{0,16},{2,18},{4,20},{6,22},{8,24},{10,26},{12,28},{14,30},{16,0},... | collective-permute-start | bytes 196616 | tf_op jit(solution)/shard_map/ppermute | solution.py:32
  51.2 2.5 %collective-permute-start.5 = (bf16[2,32,512]{2,1,0:T(8,128)(2,1)S(1)}, bf16[2,32,512]{2,1,0:T(8,128)(2,1)S(1)}, u32[]{:S(2)}, u32[]{:S(2)}) collective-permute-start(bf16[2,32,512]{2,1,0:T(8,128)(2,1)S(1)} %get-tuple-element.29), channel_id=1, source_target_pairs={{0,24},{2,26},{4,28},{6,30},{8,16},{10,18},{12,20},{14,22},{16,8},... | collective-permute-start | bytes 196616 | tf_op jit(solution)/shard_map/ppermute | solution.py:32
  54.1 3.2 %collective-permute-done.5.refs_3_ = bf16[2,32,512]{2,1,0:T(8,128)(2,1)S(1)} collective-permute-done((bf16[2,32,512]{2,1,0:T(8,128)(2,1)S(1)}, bf16[2,32,512]{2,1,0:T(8,128)(2,1)S(1)}, u32[]{:S(2)}, u32[]{:S(2)}) %collective-permute-start.5) | collective-permute-done | bytes 65568 | tf_op jit(solution)/shard_map/ppermute | solution.py:32
  60.0 2.4 %collective-permute-done.13 = f32[8,128]{1,0:T(8,128)S(1)} collective-permute-done((f32[8,128]{1,0:T(8,128)S(1)}, f32[8,128]{1,0:T(8,128)S(1)}, u32[]{:S(2)}, u32[]{:S(2)}) %collective-permute-start.13) | collective-permute-done | bytes 4128 | tf_op jit(solution)/shard_map/ppermute | solution.py:32
  63.4 2.8 %collective-permute-start.24 = (bf16[4,32,512]{2,1,0:T(8,128)(2,1)S(1)}, bf16[4,32,512]{2,1,0:T(8,128)(2,1)S(1)}, u32[]{:S(2)}, u32[]{:S(2)}) collective-permute-start(bf16[4,32,512]{2,1,0:T(8,128)(2,1)S(1)} %get-tuple-element.37.refs_2_), channel_id=1, source_target_pairs={{0,2},{2,0},{4,6},{6,4},{8,10},{10,8},{12,14},{14,12},{16,18},{18,... | collective-permute-start | bytes 393224 | tf_op jit(solution)/shard_map/ppermute | solution.py:32
  68.6 3.0 %collective-permute-start.26 = (bf16[4,32,512]{2,1,0:T(8,128)(2,1)S(1)}, bf16[4,32,512]{2,1,0:T(8,128)(2,1)S(1)}, u32[]{:S(2)}, u32[]{:S(2)}) collective-permute-start(bf16[4,32,512]{2,1,0:T(8,128)(2,1)S(1)} %get-tuple-element.37.refs_2_), channel_id=1, source_target_pairs={{0,6},{2,4},{4,2},{6,0},{8,14},{10,12},{12,10},{14,8},{16,22},{18,... | collective-permute-start | bytes 393224 | tf_op jit(solution)/shard_map/ppermute | solution.py:32
  72.3 2.1 %shard_map.72 = (bf16[512,512]{1,0:T(8,128)(2,1)S(1)}, bf16[512,512]{1,0:T(8,128)(2,1)S(1)}, f32[512,512]{1,0:T(8,128)S(1)}, f32[512,512]{1,0:T(8,128)S(1)}) custom-call(s32[2]{0:T(128)S(1)} %pad_add_fusion.where, bf16[32,7168]{1,0:T(8,128)(2,1)S(1)} %shard_map.71.refs_0_, bf16[32,7168]{1,0:T(8,128)(2,1)S(1)} %collective-permute-done.21.refs_1_, ...), custom_call_target="tpu_custom_call" | custom-call | flops 1073741824 | bytes 4980744 | tf_op jit(solution)/shard_map/pallas_call | solution.py:46
  74.4 2.9 %collective-permute-start.17 = (f32[8,128]{1,0:T(8,128)S(1)}, f32[8,128]{1,0:T(8,128)S(1)}, u32[]{:S(2)}, u32[]{:S(2)}) collective-permute-start(f32[8,128]{1,0:T(8,128)S(1)} %add.66.refs_0_), channel_id=1, source_target_pairs={{0,6},{2,4},{4,2},{6,0},{8,14},{10,12},{12,10},{14,8},{16,22},{18,... | collective-permute-start | bytes 12296 | tf_op jit(solution)/shard_map/ppermute | solution.py:32
  77.3 2.2 %shard_map.73 = (bf16[512,512]{1,0:T(8,128)(2,1)S(1)}, f32[512,512]{1,0:T(8,128)S(1)}, f32[512,512]{1,0:T(8,128)S(1)}, f32[8,128]{1,0:T(8,128)S(1)}) custom-call(s32[2]{0:T(128)S(1)} %pad_add_fusion.where, bf16[512,512]{1,0:T(8,128)(2,1)S(1)} %get-tuple-element.35.refs_0_.refs_5_, bf16[512,512]{1,0:T(8,128)(2,1)S(1)} %get-tuple-element.36.refs_1_.refs_6_, ...), custom_call_target="tpu_custom_call" | custom-call | flops 1073741824 | bytes 4198408 | tf_op jit(solution)/shard_map/pallas_call | solution.py:46
  79.6 2.4 %shard_map.74 = (bf16[32,1536]{1,0:T(8,128)(2,1)S(1)}, bf16[32,1536]{1,0:T(8,128)(2,1)S(1)}, bf16[32,1536]{1,0:T(8,128)(2,1)S(1)}, bf16[32,1536]{1,0:T(8,128)(2,1)S(1)}) custom-call(s32[2]{0:T(128)S(1)} %pad_add_fusion.where, f32[8,128]{1,0:T(8,128)S(1)} %add.66.refs_0_, f32[8,128]{1,0:T(8,128)S(1)} %collective-permute-done.15.refs_1_, ...), custom_call_target="tpu_custom_call" | custom-call | flops 1342177280 | bytes 6180872 | tf_op jit(solution)/shard_map/pallas_call | solution.py:46
  82.9 1.8 %collective-permute-start.28 = (bf16[32,1536]{1,0:T(8,128)(2,1)S(1)}, bf16[32,1536]{1,0:T(8,128)(2,1)S(1)}, u32[]{:S(2)}, u32[]{:S(2)}) collective-permute-start(bf16[32,1536]{1,0:T(8,128)(2,1)S(1)} %get-tuple-element.46), channel_id=1, source_target_pairs={{0,16},{2,18},{4,20},{6,22},{8,24},{10,26},{12,28},{14,30},{16,0},... | collective-permute-start | bytes 294920 | tf_op jit(solution)/shard_map/ppermute | solution.py:32
  87.2 2.3 %collective-permute-done.28.refs_2_ = bf16[32,1536]{1,0:T(8,128)(2,1)S(1)} collective-permute-done((bf16[32,1536]{1,0:T(8,128)(2,1)S(1)}, bf16[32,1536]{1,0:T(8,128)(2,1)S(1)}, u32[]{:S(2)}, u32[]{:S(2)}) %collective-permute-start.28) | collective-permute-done | bytes 98336 | tf_op jit(solution)/shard_map/ppermute | solution.py:32
  (62 shorter events, 29.9 us)
Async XLA Ops:
  4.0 10.9 %collective-permute-start.18 = (bf16[32,2560]{1,0:T(8,128)(2,1)S(1)}, bf16[32,2560]{1,0:T(8,128)(2,1)S(1)}, u32[]{:S(2)}, u32[]{:S(2)}) collective-permute-start(bf16[32,2560]{1,0:T(8,128)(2,1)S(1)} %get-tuple-element.62), channel_id=1, source_target_pairs={{0,8},{2,10},{4,12},{6,14},{8,0},{10,2},{12,4},{14,6},{16,24},{18,... | collective-permute-start | bytes 491528 | tf_op jit(solution)/shard_map/ppermute | solution.py:32
  7.1 13.9 %collective-permute-start.19 = (bf16[32,2560]{1,0:T(8,128)(2,1)S(1)}, bf16[32,2560]{1,0:T(8,128)(2,1)S(1)}, u32[]{:S(2)}, u32[]{:S(2)}) collective-permute-start(bf16[32,2560]{1,0:T(8,128)(2,1)S(1)} %get-tuple-element.61), channel_id=1, source_target_pairs={{0,16},{2,18},{4,20},{6,22},{8,24},{10,26},{12,28},{14,30},{16,0},... | collective-permute-start | bytes 491528 | tf_op jit(solution)/shard_map/ppermute | solution.py:32
  11.5 13.0 %collective-permute-start.6 = (bf16[4,2,32,512]{3,2,1,0:T(8,128)(2,1)S(1)}, bf16[4,2,32,512]{3,2,1,0:T(8,128)(2,1)S(1)}, u32[]{:S(2)}, u32[]{:S(2)}) collective-permute-start(bf16[4,2,32,512]{3,2,1,0:T(8,128)(2,1)S(1)} %get-tuple-element.54), channel_id=1, source_target_pairs={{0,2},{2,0},{4,6},{6,4},{8,10},{10,8},{12,14},{14,12},{16,18},{18,... | collective-permute-start | bytes 786440 | tf_op jit(solution)/shard_map/ppermute | solution.py:32
  13.0 9.9 %collective-permute-start.20 = (bf16[32,2560]{1,0:T(8,128)(2,1)S(1)}, bf16[32,2560]{1,0:T(8,128)(2,1)S(1)}, u32[]{:S(2)}, u32[]{:S(2)}) collective-permute-start(bf16[32,2560]{1,0:T(8,128)(2,1)S(1)} %get-tuple-element.60), channel_id=1, source_target_pairs={{0,24},{2,26},{4,28},{6,30},{8,16},{10,18},{12,20},{14,22},{16,8},... | collective-permute-start | bytes 491528 | tf_op jit(solution)/shard_map/ppermute | solution.py:32
  13.2 12.7 %collective-permute-start.7 = (bf16[4,2,32,512]{3,2,1,0:T(8,128)(2,1)S(1)}, bf16[4,2,32,512]{3,2,1,0:T(8,128)(2,1)S(1)}, u32[]{:S(2)}, u32[]{:S(2)}) collective-permute-start(bf16[4,2,32,512]{3,2,1,0:T(8,128)(2,1)S(1)} %get-tuple-element.53), channel_id=1, source_target_pairs={{0,4},{2,6},{4,0},{6,2},{8,12},{10,14},{12,8},{14,10},{16,20},{18,... | collective-permute-start | bytes 786440 | tf_op jit(solution)/shard_map/ppermute | solution.py:32
  14.8 12.5 %collective-permute-start.8 = (bf16[4,2,32,512]{3,2,1,0:T(8,128)(2,1)S(1)}, bf16[4,2,32,512]{3,2,1,0:T(8,128)(2,1)S(1)}, u32[]{:S(2)}, u32[]{:S(2)}) collective-permute-start(bf16[4,2,32,512]{3,2,1,0:T(8,128)(2,1)S(1)} %get-tuple-element.52), channel_id=1, source_target_pairs={{0,6},{2,4},{4,2},{6,0},{8,14},{10,12},{12,10},{14,8},{16,22},{18,... | collective-permute-start | bytes 786440 | tf_op jit(solution)/shard_map/ppermute | solution.py:32
  21.0 11.0 %collective-permute-start = (bf16[4,2,32,512]{3,2,1,0:T(8,128)(2,1)S(1)}, bf16[4,2,32,512]{3,2,1,0:T(8,128)(2,1)S(1)}, u32[]{:S(2)}, u32[]{:S(2)}) collective-permute-start(bf16[4,2,32,512]{3,2,1,0:T(8,128)(2,1)S(1)} %get-tuple-element.58), channel_id=1, source_target_pairs={{0,2},{2,0},{4,6},{6,4},{8,10},{10,8},{12,14},{14,12},{16,18},{18,... | collective-permute-start | bytes 786440 | tf_op jit(solution)/shard_map/ppermute | solution.py:32
  22.9 14.7 %collective-permute-start.1 = (bf16[4,2,32,512]{3,2,1,0:T(8,128)(2,1)S(1)}, bf16[4,2,32,512]{3,2,1,0:T(8,128)(2,1)S(1)}, u32[]{:S(2)}, u32[]{:S(2)}) collective-permute-start(bf16[4,2,32,512]{3,2,1,0:T(8,128)(2,1)S(1)} %get-tuple-element.57), channel_id=1, source_target_pairs={{0,4},{2,6},{4,0},{6,2},{8,12},{10,14},{12,8},{14,10},{16,20},{18,... | collective-permute-start | bytes 786440 | tf_op jit(solution)/shard_map/ppermute | solution.py:32
  24.5 16.1 %collective-permute-start.2 = (bf16[4,2,32,512]{3,2,1,0:T(8,128)(2,1)S(1)}, bf16[4,2,32,512]{3,2,1,0:T(8,128)(2,1)S(1)}, u32[]{:S(2)}, u32[]{:S(2)}) collective-permute-start(bf16[4,2,32,512]{3,2,1,0:T(8,128)(2,1)S(1)} %get-tuple-element.56), channel_id=1, source_target_pairs={{0,6},{2,4},{4,2},{6,0},{8,14},{10,12},{12,10},{14,8},{16,22},{18,... | collective-permute-start | bytes 786440 | tf_op jit(solution)/shard_map/ppermute | solution.py:32
  25.9 42.7 %collective-permute-start.21 = (bf16[32,7168]{1,0:T(8,128)(2,1)S(1)}, bf16[32,7168]{1,0:T(8,128)(2,1)S(1)}, u32[]{:S(2)}, u32[]{:S(2)}) collective-permute-start(bf16[32,7168]{1,0:T(8,128)(2,1)S(1)} %shard_map.71.refs_0_), channel_id=1, source_target_pairs={{0,2},{2,0},{4,6},{6,4},{8,10},{10,8},{12,14},{14,12},{16,18},{18,... | collective-permute-start | bytes 1376264 | tf_op jit(solution)/shard_map/ppermute | solution.py:32
  27.3 44.3 %collective-permute-start.22 = (bf16[32,7168]{1,0:T(8,128)(2,1)S(1)}, bf16[32,7168]{1,0:T(8,128)(2,1)S(1)}, u32[]{:S(2)}, u32[]{:S(2)}) collective-permute-start(bf16[32,7168]{1,0:T(8,128)(2,1)S(1)} %shard_map.71.refs_0_), channel_id=1, source_target_pairs={{0,4},{2,6},{4,0},{6,2},{8,12},{10,14},{12,8},{14,10},{16,20},{18,... | collective-permute-start | bytes 1376264 | tf_op jit(solution)/shard_map/ppermute | solution.py:32
  32.0 39.7 %collective-permute-start.23 = (bf16[32,7168]{1,0:T(8,128)(2,1)S(1)}, bf16[32,7168]{1,0:T(8,128)(2,1)S(1)}, u32[]{:S(2)}, u32[]{:S(2)}) collective-permute-start(bf16[32,7168]{1,0:T(8,128)(2,1)S(1)} %shard_map.71.refs_0_), channel_id=1, source_target_pairs={{0,6},{2,4},{4,2},{6,0},{8,14},{10,12},{12,10},{14,8},{16,22},{18,... | collective-permute-start | bytes 1376264 | tf_op jit(solution)/shard_map/ppermute | solution.py:32
  37.7 5.9 %collective-permute-start.10 = (bf16[2,32,512]{2,1,0:T(8,128)(2,1)S(1)}, bf16[2,32,512]{2,1,0:T(8,128)(2,1)S(1)}, u32[]{:S(2)}, u32[]{:S(2)}) collective-permute-start(bf16[2,32,512]{2,1,0:T(8,128)(2,1)S(1)} %get-tuple-element.32), channel_id=1, source_target_pairs={{0,16},{2,18},{4,20},{6,22},{8,24},{10,26},{12,28},{14,30},{16,0},... | collective-permute-start | bytes 196616 | tf_op jit(solution)/shard_map/ppermute | solution.py:32
  40.6 6.1 %collective-permute-start.11 = (bf16[2,32,512]{2,1,0:T(8,128)(2,1)S(1)}, bf16[2,32,512]{2,1,0:T(8,128)(2,1)S(1)}, u32[]{:S(2)}, u32[]{:S(2)}) collective-permute-start(bf16[2,32,512]{2,1,0:T(8,128)(2,1)S(1)} %get-tuple-element.33), channel_id=1, source_target_pairs={{0,24},{2,26},{4,28},{6,30},{8,16},{10,18},{12,20},{14,22},{16,8},... | collective-permute-start | bytes 196616 | tf_op jit(solution)/shard_map/ppermute | solution.py:32
  43.6 5.4 %collective-permute-start.9 = (bf16[2,32,512]{2,1,0:T(8,128)(2,1)S(1)}, bf16[2,32,512]{2,1,0:T(8,128)(2,1)S(1)}, u32[]{:S(2)}, u32[]{:S(2)}) collective-permute-start(bf16[2,32,512]{2,1,0:T(8,128)(2,1)S(1)} %get-tuple-element.31), channel_id=1, source_target_pairs={{0,8},{2,10},{4,12},{6,14},{8,0},{10,2},{12,4},{14,6},{16,24},{18,... | collective-permute-start | bytes 196616 | tf_op jit(solution)/shard_map/ppermute | solution.py:32
  51.2 6.1 %collective-permute-start.5 = (bf16[2,32,512]{2,1,0:T(8,128)(2,1)S(1)}, bf16[2,32,512]{2,1,0:T(8,128)(2,1)S(1)}, u32[]{:S(2)}, u32[]{:S(2)}) collective-permute-start(bf16[2,32,512]{2,1,0:T(8,128)(2,1)S(1)} %get-tuple-element.29), channel_id=1, source_target_pairs={{0,24},{2,26},{4,28},{6,30},{8,16},{10,18},{12,20},{14,22},{16,8},... | collective-permute-start | bytes 196616 | tf_op jit(solution)/shard_map/ppermute | solution.py:32
  63.4 11.0 %collective-permute-start.24 = (bf16[4,32,512]{2,1,0:T(8,128)(2,1)S(1)}, bf16[4,32,512]{2,1,0:T(8,128)(2,1)S(1)}, u32[]{:S(2)}, u32[]{:S(2)}) collective-permute-start(bf16[4,32,512]{2,1,0:T(8,128)(2,1)S(1)} %get-tuple-element.37.refs_2_), channel_id=1, source_target_pairs={{0,2},{2,0},{4,6},{6,4},{8,10},{10,8},{12,14},{14,12},{16,18},{18,... | collective-permute-start | bytes 393224 | tf_op jit(solution)/shard_map/ppermute | solution.py:32
  66.9 10.4 %collective-permute-start.25 = (bf16[4,32,512]{2,1,0:T(8,128)(2,1)S(1)}, bf16[4,32,512]{2,1,0:T(8,128)(2,1)S(1)}, u32[]{:S(2)}, u32[]{:S(2)}) collective-permute-start(bf16[4,32,512]{2,1,0:T(8,128)(2,1)S(1)} %get-tuple-element.37.refs_2_), channel_id=1, source_target_pairs={{0,4},{2,6},{4,0},{6,2},{8,12},{10,14},{12,8},{14,10},{16,20},{18,... | collective-permute-start | bytes 393224 | tf_op jit(solution)/shard_map/ppermute | solution.py:32
  68.6 8.7 %collective-permute-start.26 = (bf16[4,32,512]{2,1,0:T(8,128)(2,1)S(1)}, bf16[4,32,512]{2,1,0:T(8,128)(2,1)S(1)}, u32[]{:S(2)}, u32[]{:S(2)}) collective-permute-start(bf16[4,32,512]{2,1,0:T(8,128)(2,1)S(1)} %get-tuple-element.37.refs_2_), channel_id=1, source_target_pairs={{0,6},{2,4},{4,2},{6,0},{8,14},{10,12},{12,10},{14,8},{16,22},{18,... | collective-permute-start | bytes 393224 | tf_op jit(solution)/shard_map/ppermute | solution.py:32
  71.7 7.9 %collective-permute-start.15 = (f32[8,128]{1,0:T(8,128)S(1)}, f32[8,128]{1,0:T(8,128)S(1)}, u32[]{:S(2)}, u32[]{:S(2)}) collective-permute-start(f32[8,128]{1,0:T(8,128)S(1)} %add.66.refs_0_), channel_id=1, source_target_pairs={{0,2},{2,0},{4,6},{6,4},{8,10},{10,8},{12,14},{14,12},{16,18},{18,... | collective-permute-start | bytes 12296 | tf_op jit(solution)/shard_map/ppermute | solution.py:32
  71.7 7.9 %collective-permute-start.16 = (f32[8,128]{1,0:T(8,128)S(1)}, f32[8,128]{1,0:T(8,128)S(1)}, u32[]{:S(2)}, u32[]{:S(2)}) collective-permute-start(f32[8,128]{1,0:T(8,128)S(1)} %add.66.refs_0_), channel_id=1, source_target_pairs={{0,4},{2,6},{4,0},{6,2},{8,12},{10,14},{12,8},{14,10},{16,20},{18,... | collective-permute-start | bytes 12296 | tf_op jit(solution)/shard_map/ppermute | solution.py:32
  82.0 5.2 %collective-permute-start.27 = (bf16[32,1536]{1,0:T(8,128)(2,1)S(1)}, bf16[32,1536]{1,0:T(8,128)(2,1)S(1)}, u32[]{:S(2)}, u32[]{:S(2)}) collective-permute-start(bf16[32,1536]{1,0:T(8,128)(2,1)S(1)} %get-tuple-element.45), channel_id=1, source_target_pairs={{0,8},{2,10},{4,12},{6,14},{8,0},{10,2},{12,4},{14,6},{16,24},{18,... | collective-permute-start | bytes 294920 | tf_op jit(solution)/shard_map/ppermute | solution.py:32
  82.9 6.6 %collective-permute-start.28 = (bf16[32,1536]{1,0:T(8,128)(2,1)S(1)}, bf16[32,1536]{1,0:T(8,128)(2,1)S(1)}, u32[]{:S(2)}, u32[]{:S(2)}) collective-permute-start(bf16[32,1536]{1,0:T(8,128)(2,1)S(1)} %get-tuple-element.46), channel_id=1, source_target_pairs={{0,16},{2,18},{4,20},{6,22},{8,24},{10,26},{12,28},{14,30},{16,0},... | collective-permute-start | bytes 294920 | tf_op jit(solution)/shard_map/ppermute | solution.py:32
  84.7 6.5 %collective-permute-start.29 = (bf16[32,1536]{1,0:T(8,128)(2,1)S(1)}, bf16[32,1536]{1,0:T(8,128)(2,1)S(1)}, u32[]{:S(2)}, u32[]{:S(2)}) collective-permute-start(bf16[32,1536]{1,0:T(8,128)(2,1)S(1)} %get-tuple-element.47), channel_id=1, source_target_pairs={{0,24},{2,26},{4,28},{6,30},{8,16},{10,18},{12,20},{14,22},{16,8},... | collective-permute-start | bytes 294920 | tf_op jit(solution)/shard_map/ppermute | solution.py:32
  (8 other events, 47.5 us)
where the time goes:
time: 92.7 us; the launch traced here: 92.5 us
  starting transfers between devices  52 us (56%)
  waiting for transfers between devices  24.2 us (26%)
  Pallas kernels  10.2 us (11%)
  other arithmetic  2.69 us (3%)
  local copies, waits for them, and re-layouts  2.49 us (3%)
    ppermute x29, starting transfers between devices, flip(): return lax.ppermute(array, 'dp', [(i, i ^ mask) for i in range(devices)])  51.9 us
    ppermute x29, waiting for transfers between devices, flip(): return lax.ppermute(array, 'dp', [(i, i ^ mask) for i in range(devices)])  23.1 us
    pallas_call x8, Pallas kernels, call(): pl.pallas_call(kernel, out_shape=out_shape, in_specs=[SMEM_SPEC] * smem +...  10.2 us
  transfers between devices with their start and end apart: 30, of which 15 were waited for; matrix products, arithmetic and copies ran while one was open for 2% of the time, Pallas kernels for 7%

commit v1 on v0

--- a/solution.py
+++ b/solution.py
@@ -71,6 +71,15 @@
 
     def packed(self):
         return sum(self.size - first for _, _, first, _ in self.spots())
+
+
+def choose_kernel(plan, where, slots, factors, inverses, probes, *outs):
+    size = plan.size
+    for k, out in enumerate(outs):
+        slot = slots[where[0] ^ k]
+        out[:, : 2 * size] = factors[slot]
+        out[:, 2 * size : 4 * size] = inverses[slot]
+        out[:, 4 * size :] = probes[slot]
 
 
 def pack_kernel(plan, where, *refs):
@@ -218,20 +227,37 @@
 
     grads = partial_grads[0].reshape(blocks, blocks, group, rows, columns)
     step = blocks // CHUNKS
+    later = lax.optimization_barrier(grads)
     chunks = []
     for i in range(CHUNKS):
-        chunk = grads[:, i * step : (i + 1) * step]
-        chunks.append(
-            [pick(chunk, my_place, 2)]
-            + [flip(pick(chunk, my_place ^ k, 2), devices, k) for k in range(1, group)]
-        )
+        cut = [
+            lax.dynamic_slice(
+                grads if i == 0 and k > 0 else later,
+                (0, i * step, my_place ^ k, 0, 0),
+                (blocks, step, 1, rows, columns),
+            ).reshape(blocks, step, rows, columns)
+            for k in range(group)
+        ]
+        chunks.append([cut[0]] + [flip(cut[k], devices, k) for k in range(1, group)])
 
     old_state = factors[0]
-    wide = jnp.concatenate([old_state, inverse_factors[0], probes[0]], axis=2)
-    chosen = jnp.take(wide, slot_row, axis=0)
-    pieces = [pick(chosen, my_block, 0)] + [
-        flip(pick(chosen, my_block ^ k, 0), devices, k * group) for k in range(1, blocks)
-    ]
+    if in_tiles:
+        pieces = call(
+            functools.partial(choose_kernel, plan),
+            tuple(shaped((rows, 5 * size)) for _ in range(blocks)),
+            [],
+            0,
+            2,
+            where,
+            slot_row,
+            old_state,
+            inverse_factors[0],
+            probes[0],
+        )
+    else:
+        wide = jnp.concatenate([old_state, inverse_factors[0], probes[0]], axis=2)
+        pieces = [pick(wide, slot_row[my_block ^ k], 0) for k in range(blocks)]
+    pieces = [pieces[0]] + [flip(pieces[k], devices, k * group) for k in range(1, blocks)]
     if in_tiles:
         quarter = call(
             functools.partial(pack_kernel, plan),
@@ -269,14 +295,14 @@
     states = [quarter] + [flip(quarter, devices, k) for k in range(1, group)]
     quarters = [grad_quarter] + [flip(grad_quarter, devices, k) for k in range(1, group)]
 
+    squares = functools.reduce(
+        jnp.add,
+        [squares] + [flip(squares, devices, k * group) for k in range(1, blocks)],
+    )
     bit = 1
     while bit < halves:
         other = lax.ppermute(squares, "mp", [(i, i ^ bit) for i in range(halves)])
         squares = squares + other
-        bit *= 2
-    bit = 1
-    while bit < blocks:
-        squares = squares + flip(squares, devices, bit * group)
         bit *= 2
     sums = [squares] + [flip(squares, devices, k) for k in range(1, group)]
 

time: 92.7 us -> 91.6 us (0.988)
  starting transfers between devices: 52 us -> 44.6 us
  waiting for transfers between devices: 24.2 us -> 29 us
  local copies, waits for them, and re-layouts: 2.49 us -> 5.98 us
  other arithmetic: 2.69 us -> 0.08 us
    ppermute x29 -> x30, starting transfers between devices: 51.9 us -> 44.6 us  [flip(): return lax.ppermute(array, 'dp', [(i, i ^ mask) for i in range(devices)])]
    ppermute x29 -> x30, waiting for transfers between devices: 23.1 us -> 29 us  [flip(): return lax.ppermute(array, 'dp', [(i, i ^ mask) for i in range(devices)])]
    unnamed x4 -> x12, local copies, waits for them, and re-layouts: 0.01 us -> 3.47 us
    reshape x0 -> x2, local copies, waits for them, and re-layouts: none -> 2.51 us  [body(): cut = [lax.dynamic_slice(grads if i == 0 and k > 0 else later, (0, i * st...]
    slice x1 -> x0, local copies, waits for them, and re-layouts: 1.68 us -> none  [body(): chunk = grads[:, i * step:(i + 1) * step]]
    ppermute x1, waiting for transfers between devices: 1.15 us -> 0.01 us  [body(): other = lax.ppermute(squares, 'mp', [(i, i ^ bit) for i in range(halves)])]
    concatenate x1 -> x0, other arithmetic: 1.15 us -> none  [body(): wide = jnp.concatenate([old_state, inverse_factors[0], probes[0]], axis=2)]
    pallas_call x8 -> x9, Pallas kernels: 10.2 us -> 10.8 us  [call(): pl.pallas_call(kernel, out_shape=out_shape, in_specs=[SMEM_SPEC] * smem +...]
  transfers between devices with their start and end apart: 30 -> 31, of which waited for: 15 -> 11; matrix products, arithmetic and copies ran while one was open for 2% -> 3% of each run, Pallas kernels for 7% -> 7%
where the time goes in v1:
time: 91.6 us; the launch traced here: 91.3 us
  starting transfers between devices  44.6 us (49%)
  waiting for transfers between devices  29 us (32%)
  Pallas kernels  10.8 us (12%)
  local copies, waits for them, and re-layouts  5.98 us (7%)
    ppermute x30, starting transfers between devices, flip(): return lax.ppermute(array, 'dp', [(i, i ^ mask) for i in range(devices)])  44.6 us
    ppermute x30, waiting for transfers between devices, flip(): return lax.ppermute(array, 'dp', [(i, i ^ mask) for i in range(devices)])  29 us
    pallas_call x9, Pallas kernels, call(): pl.pallas_call(kernel, out_shape=out_shape, in_specs=[SMEM_SPEC] * smem +...  10.8 us
    unnamed x12, local copies, waits for them, and re-layouts  3.47 us
    reshape x2, local copies, waits for them, and re-layouts, body(): cut = [lax.dynamic_slice(grads if i == 0 and k > 0 else later, (0, i * st...  2.51 us
  transfers between devices with their start and end apart: 31, of which 11 were waited for; matrix products, arithmetic and copies ran while one was open for 3% of the time, Pallas kernels for 7%

profile of v1, /device:TPU:0, one launch (start us, length us, event | category | flops | bytes accessed | tf_op | source)
XLA Modules:
  0.0 91.3 jit_solution(781032407648246794)
XLA Ops:
  4.8 3.1 %collective-permute-start.19 = (bf16[32,2560]{1,0:T(8,128)(2,1)S(1)}, bf16[32,2560]{1,0:T(8,128)(2,1)S(1)}, u32[]{:S(2)}, u32[]{:S(2)}) collective-permute-start(bf16[32,2560]{1,0:T(8,128)(2,1)S(1)} %get-tuple-element.40), channel_id=1, source_target_pairs={{0,8},{2,10},{4,12},{6,14},{8,0},{10,2},{12,4},{14,6},{16,24},{18,... | collective-permute-start | bytes 491528 | tf_op jit(solution)/shard_map/ppermute | solution.py:32
  9.3 1.6 %collective-permute-start.6 = (bf16[4,2,32,512]{3,2,1,0:T(8,128)(2,1)S(1)}, bf16[4,2,32,512]{3,2,1,0:T(8,128)(2,1)S(1)}, u32[]{:S(2)}, u32[]{:S(2)}) collective-permute-start(bf16[4,2,32,512]{3,2,1,0:T(8,128)(2,1)S(1)} %get-tuple-element.60), channel_id=1, source_target_pairs={{0,2},{2,0},{4,6},{6,4},{8,10},{10,8},{12,14},{14,12},{16,18},{18,... | collective-permute-start | bytes 786440 | tf_op jit(solution)/shard_map/ppermute | solution.py:32
  10.8 2.6 %collective-permute-start.20 = (bf16[32,2560]{1,0:T(8,128)(2,1)S(1)}, bf16[32,2560]{1,0:T(8,128)(2,1)S(1)}, u32[]{:S(2)}, u32[]{:S(2)}) collective-permute-start(bf16[32,2560]{1,0:T(8,128)(2,1)S(1)} %get-tuple-element.41), channel_id=1, source_target_pairs={{0,16},{2,18},{4,20},{6,22},{8,24},{10,26},{12,28},{14,30},{16,0},... | collective-permute-start | bytes 491528 | tf_op jit(solution)/shard_map/ppermute | solution.py:32
  13.6 1.5 %collective-permute-start.7 = (bf16[4,2,32,512]{3,2,1,0:T(8,128)(2,1)S(1)}, bf16[4,2,32,512]{3,2,1,0:T(8,128)(2,1)S(1)}, u32[]{:S(2)}, u32[]{:S(2)}) collective-permute-start(bf16[4,2,32,512]{3,2,1,0:T(8,128)(2,1)S(1)} %get-tuple-element.59), channel_id=1, source_target_pairs={{0,4},{2,6},{4,0},{6,2},{8,12},{10,14},{12,8},{14,10},{16,20},{18,... | collective-permute-start | bytes 786440 | tf_op jit(solution)/shard_map/ppermute | solution.py:32
  16.6 8.3 %collective-permute-done.20.refs_2_ = bf16[32,2560]{1,0:T(8,128)(2,1)S(1)} collective-permute-done((bf16[32,2560]{1,0:T(8,128)(2,1)S(1)}, bf16[32,2560]{1,0:T(8,128)(2,1)S(1)}, u32[]{:S(2)}, u32[]{:S(2)}) %collective-permute-start.20) | collective-permute-done | bytes 163872 | tf_op jit(solution)/shard_map/ppermute | solution.py:32
  25.8 1.5 %collective-permute-start.1 = (bf16[4,2,32,512]{3,2,1,0:T(8,128)(2,1)S(1)}, bf16[4,2,32,512]{3,2,1,0:T(8,128)(2,1)S(1)}, u32[]{:S(2)}, u32[]{:S(2)}) collective-permute-start(bf16[4,2,32,512]{3,2,1,0:T(8,128)(2,1)S(1)} %get-tuple-element.64), channel_id=1, source_target_pairs={{0,4},{2,6},{4,0},{6,2},{8,12},{10,14},{12,8},{14,10},{16,20},{18,... | collective-permute-start | bytes 786440 | tf_op jit(solution)/shard_map/ppermute | solution.py:32
  30.7 3.5 %collective-permute-start.10 = (bf16[2,32,512]{2,1,0:T(8,128)(2,1)S(1)}, bf16[2,32,512]{2,1,0:T(8,128)(2,1)S(1)}, u32[]{:S(2)}, u32[]{:S(2)}) collective-permute-start(bf16[2,32,512]{2,1,0:T(8,128)(2,1)S(1)} %get-tuple-element.36), channel_id=1, source_target_pairs={{0,16},{2,18},{4,20},{6,22},{8,24},{10,26},{12,28},{14,30},{16,0},... | collective-permute-start | bytes 196616 | tf_op jit(solution)/shard_map/ppermute | solution.py:32
  34.2 2.7 %collective-permute-start.11 = (bf16[2,32,512]{2,1,0:T(8,128)(2,1)S(1)}, bf16[2,32,512]{2,1,0:T(8,128)(2,1)S(1)}, u32[]{:S(2)}, u32[]{:S(2)}) collective-permute-start(bf16[2,32,512]{2,1,0:T(8,128)(2,1)S(1)} %get-tuple-element.37), channel_id=1, source_target_pairs={{0,24},{2,26},{4,28},{6,30},{8,16},{10,18},{12,20},{14,22},{16,8},... | collective-permute-start | bytes 196616 | tf_op jit(solution)/shard_map/ppermute | solution.py:32
  36.9 1.5 %collective-permute-start.23 = (bf16[32,7168]{1,0:T(8,128)(2,1)S(1)}, bf16[32,7168]{1,0:T(8,128)(2,1)S(1)}, u32[]{:S(2)}, u32[]{:S(2)}) collective-permute-start(bf16[32,7168]{1,0:T(8,128)(2,1)S(1)} %shard_map.72.refs_0_), channel_id=1, source_target_pairs={{0,4},{2,6},{4,0},{6,2},{8,12},{10,14},{12,8},{14,10},{16,20},{18,... | collective-permute-start | bytes 1376264 | tf_op jit(solution)/shard_map/ppermute | solution.py:32
  38.4 2.3 %collective-permute-done.2.refs_3_ = bf16[4,2,32,512]{3,2,1,0:T(8,128)(2,1)S(1)} collective-permute-done((bf16[4,2,32,512]{3,2,1,0:T(8,128)(2,1)S(1)}, bf16[4,2,32,512]{3,2,1,0:T(8,128)(2,1)S(1)}, u32[]{:S(2)}, u32[]{:S(2)}) %collective-permute-start.2) | collective-permute-done | bytes 262176 | tf_op jit(solution)/shard_map/ppermute | solution.py:32
  42.2 1.6 %collective-permute-start.9 = (bf16[2,32,512]{2,1,0:T(8,128)(2,1)S(1)}, bf16[2,32,512]{2,1,0:T(8,128)(2,1)S(1)}, u32[]{:S(2)}, u32[]{:S(2)}) collective-permute-start(bf16[2,32,512]{2,1,0:T(8,128)(2,1)S(1)} %get-tuple-element.35), channel_id=1, source_target_pairs={{0,8},{2,10},{4,12},{6,14},{8,0},{10,2},{12,4},{14,6},{16,24},{18,... | collective-permute-start | bytes 196616 | tf_op jit(solution)/shard_map/ppermute | solution.py:32
  44.2 2.2 %collective-permute-done.9.refs_5_ = bf16[2,32,512]{2,1,0:T(8,128)(2,1)S(1)} collective-permute-done((bf16[2,32,512]{2,1,0:T(8,128)(2,1)S(1)}, bf16[2,32,512]{2,1,0:T(8,128)(2,1)S(1)}, u32[]{:S(2)}, u32[]{:S(2)}) %collective-permute-start.9) | collective-permute-done | bytes 65568 | tf_op jit(solution)/shard_map/ppermute | solution.py:32
  46.5 2.9 %collective-permute-start.4 = (bf16[2,32,512]{2,1,0:T(8,128)(2,1)S(1)}, bf16[2,32,512]{2,1,0:T(8,128)(2,1)S(1)}, u32[]{:S(2)}, u32[]{:S(2)}) collective-permute-start(bf16[2,32,512]{2,1,0:T(8,128)(2,1)S(1)} %get-tuple-element.32), channel_id=1, source_target_pairs={{0,16},{2,18},{4,20},{6,22},{8,24},{10,26},{12,28},{14,30},{16,0},... | collective-permute-start | bytes 196616 | tf_op jit(solution)/shard_map/ppermute | solution.py:32
  49.4 1.6 %collective-permute-start.5 = (bf16[2,32,512]{2,1,0:T(8,128)(2,1)S(1)}, bf16[2,32,512]{2,1,0:T(8,128)(2,1)S(1)}, u32[]{:S(2)}, u32[]{:S(2)}) collective-permute-start(bf16[2,32,512]{2,1,0:T(8,128)(2,1)S(1)} %get-tuple-element.33), channel_id=1, source_target_pairs={{0,24},{2,26},{4,28},{6,30},{8,16},{10,18},{12,20},{14,22},{16,8},... | collective-permute-start | bytes 196616 | tf_op jit(solution)/shard_map/ppermute | solution.py:32
  51.9 3.6 %collective-permute-done.5.refs_3_ = bf16[2,32,512]{2,1,0:T(8,128)(2,1)S(1)} collective-permute-done((bf16[2,32,512]{2,1,0:T(8,128)(2,1)S(1)}, bf16[2,32,512]{2,1,0:T(8,128)(2,1)S(1)}, u32[]{:S(2)}, u32[]{:S(2)}) %collective-permute-start.5) | collective-permute-done | bytes 65568 | tf_op jit(solution)/shard_map/ppermute | solution.py:32
  55.8 2.2 %collective-permute-start.13 = (f32[8,128]{1,0:T(8,128)S(1)}, f32[8,128]{1,0:T(8,128)S(1)}, u32[]{:S(2)}, u32[]{:S(2)}) collective-permute-start(f32[8,128]{1,0:T(8,128)S(1)} %get-tuple-element.38), channel_id=1, source_target_pairs={{0,16},{2,18},{4,20},{6,22},{8,24},{10,26},{12,28},{14,30},{16,0},... | collective-permute-start | bytes 12296 | tf_op jit(solution)/shard_map/ppermute | solution.py:32
  59.4 1.6 %collective-permute-start.14 = (f32[8,128]{1,0:T(8,128)S(1)}, f32[8,128]{1,0:T(8,128)S(1)}, u32[]{:S(2)}, u32[]{:S(2)}) collective-permute-start(f32[8,128]{1,0:T(8,128)S(1)} %get-tuple-element.38), channel_id=1, source_target_pairs={{0,24},{2,26},{4,28},{6,30},{8,16},{10,18},{12,20},{14,22},{16,8},... | collective-permute-start | bytes 12296 | tf_op jit(solution)/shard_map/ppermute | solution.py:32
  61.0 3.8 %collective-permute-done.14 = f32[8,128]{1,0:T(8,128)S(1)} collective-permute-done((f32[8,128]{1,0:T(8,128)S(1)}, f32[8,128]{1,0:T(8,128)S(1)}, u32[]{:S(2)}, u32[]{:S(2)}) %collective-permute-start.14) | collective-permute-done | bytes 4128 | tf_op jit(solution)/shard_map/ppermute | solution.py:32
  71.2 2.1 %shard_map.73 = (bf16[512,512]{1,0:T(8,128)(2,1)S(1)}, bf16[512,512]{1,0:T(8,128)(2,1)S(1)}, f32[512,512]{1,0:T(8,128)S(1)}, f32[512,512]{1,0:T(8,128)S(1)}) custom-call(s32[2]{0:T(128)S(1)} %pad_add_fusion.where, bf16[32,7168]{1,0:T(8,128)(2,1)S(1)} %shard_map.72.refs_0_, bf16[32,7168]{1,0:T(8,128)(2,1)S(1)} %collective-permute-done.22.refs_1_, ...), custom_call_target="tpu_custom_call" | custom-call | flops 1073741824 | bytes 4980744 | tf_op jit(solution)/shard_map/pallas_call | solution.py:46
  74.7 2.2 %shard_map.74 = (bf16[512,512]{1,0:T(8,128)(2,1)S(1)}, f32[512,512]{1,0:T(8,128)S(1)}, f32[512,512]{1,0:T(8,128)S(1)}, f32[8,128]{1,0:T(8,128)S(1)}) custom-call(s32[2]{0:T(128)S(1)} %pad_add_fusion.where, bf16[512,512]{1,0:T(8,128)(2,1)S(1)} %get-tuple-element.43.refs_0_.refs_5_, bf16[512,512]{1,0:T(8,128)(2,1)S(1)} %get-tuple-element.44.refs_1_.refs_6_, ...), custom_call_target="tpu_custom_call" | custom-call | flops 1073741824 | bytes 4198408 | tf_op jit(solution)/shard_map/pallas_call | solution.py:46
  77.9 2.4 %shard_map.75 = (bf16[32,1536]{1,0:T(8,128)(2,1)S(1)}, bf16[32,1536]{1,0:T(8,128)(2,1)S(1)}, bf16[32,1536]{1,0:T(8,128)(2,1)S(1)}, bf16[32,1536]{1,0:T(8,128)(2,1)S(1)}) custom-call(s32[2]{0:T(128)S(1)} %pad_add_fusion.where, f32[8,128]{1,0:T(8,128)S(1)} %add.41.refs_0_, f32[8,128]{1,0:T(8,128)S(1)} %collective-permute-done.16.refs_1_, ...), custom_call_target="tpu_custom_call" | custom-call | flops 1342177280 | bytes 6180872 | tf_op jit(solution)/shard_map/pallas_call | solution.py:46
  80.4 2.5 %collective-permute-start.29 = (bf16[32,1536]{1,0:T(8,128)(2,1)S(1)}, bf16[32,1536]{1,0:T(8,128)(2,1)S(1)}, u32[]{:S(2)}, u32[]{:S(2)}) collective-permute-start(bf16[32,1536]{1,0:T(8,128)(2,1)S(1)} %get-tuple-element.54), channel_id=1, source_target_pairs={{0,16},{2,18},{4,20},{6,22},{8,24},{10,26},{12,28},{14,30},{16,0},... | collective-permute-start | bytes 294920 | tf_op jit(solution)/shard_map/ppermute | solution.py:32
  82.9 1.9 %collective-permute-start.30 = (bf16[32,1536]{1,0:T(8,128)(2,1)S(1)}, bf16[32,1536]{1,0:T(8,128)(2,1)S(1)}, u32[]{:S(2)}, u32[]{:S(2)}) collective-permute-start(bf16[32,1536]{1,0:T(8,128)(2,1)S(1)} %get-tuple-element.55), channel_id=1, source_target_pairs={{0,24},{2,26},{4,28},{6,30},{8,16},{10,18},{12,20},{14,22},{16,8},... | collective-permute-start | bytes 294920 | tf_op jit(solution)/shard_map/ppermute | solution.py:32
  85.0 5.0 %collective-permute-done.29.refs_2_ = bf16[32,1536]{1,0:T(8,128)(2,1)S(1)} collective-permute-done((bf16[32,1536]{1,0:T(8,128)(2,1)S(1)}, bf16[32,1536]{1,0:T(8,128)(2,1)S(1)}, u32[]{:S(2)}, u32[]{:S(2)}) %collective-permute-start.29) | collective-permute-done | bytes 98336 | tf_op jit(solution)/shard_map/ppermute | solution.py:32
  (64 shorter events, 26.3 us)
Async XLA Ops:
  4.8 10.4 %collective-permute-start.19 = (bf16[32,2560]{1,0:T(8,128)(2,1)S(1)}, bf16[32,2560]{1,0:T(8,128)(2,1)S(1)}, u32[]{:S(2)}, u32[]{:S(2)}) collective-permute-start(bf16[32,2560]{1,0:T(8,128)(2,1)S(1)} %get-tuple-element.40), channel_id=1, source_target_pairs={{0,8},{2,10},{4,12},{6,14},{8,0},{10,2},{12,4},{14,6},{16,24},{18,... | collective-permute-start | bytes 491528 | tf_op jit(solution)/shard_map/ppermute | solution.py:32
  9.3 18.0 %collective-permute-start.6 = (bf16[4,2,32,512]{3,2,1,0:T(8,128)(2,1)S(1)}, bf16[4,2,32,512]{3,2,1,0:T(8,128)(2,1)S(1)}, u32[]{:S(2)}, u32[]{:S(2)}) collective-permute-start(bf16[4,2,32,512]{3,2,1,0:T(8,128)(2,1)S(1)} %get-tuple-element.60), channel_id=1, source_target_pairs={{0,2},{2,0},{4,6},{6,4},{8,10},{10,8},{12,14},{14,12},{16,18},{18,... | collective-permute-start | bytes 786440 | tf_op jit(solution)/shard_map/ppermute | solution.py:32
  10.8 14.1 %collective-permute-start.20 = (bf16[32,2560]{1,0:T(8,128)(2,1)S(1)}, bf16[32,2560]{1,0:T(8,128)(2,1)S(1)}, u32[]{:S(2)}, u32[]{:S(2)}) collective-permute-start(bf16[32,2560]{1,0:T(8,128)(2,1)S(1)} %get-tuple-element.41), channel_id=1, source_target_pairs={{0,16},{2,18},{4,20},{6,22},{8,24},{10,26},{12,28},{14,30},{16,0},... | collective-permute-start | bytes 491528 | tf_op jit(solution)/shard_map/ppermute | solution.py:32
  13.4 12.4 %collective-permute-start.21 = (bf16[32,2560]{1,0:T(8,128)(2,1)S(1)}, bf16[32,2560]{1,0:T(8,128)(2,1)S(1)}, u32[]{:S(2)}, u32[]{:S(2)}) collective-permute-start(bf16[32,2560]{1,0:T(8,128)(2,1)S(1)} %get-tuple-element.42), channel_id=1, source_target_pairs={{0,24},{2,26},{4,28},{6,30},{8,16},{10,18},{12,20},{14,22},{16,8},... | collective-permute-start | bytes 491528 | tf_op jit(solution)/shard_map/ppermute | solution.py:32
  13.6 15.4 %collective-permute-start.7 = (bf16[4,2,32,512]{3,2,1,0:T(8,128)(2,1)S(1)}, bf16[4,2,32,512]{3,2,1,0:T(8,128)(2,1)S(1)}, u32[]{:S(2)}, u32[]{:S(2)}) collective-permute-start(bf16[4,2,32,512]{3,2,1,0:T(8,128)(2,1)S(1)} %get-tuple-element.59), channel_id=1, source_target_pairs={{0,4},{2,6},{4,0},{6,2},{8,12},{10,14},{12,8},{14,10},{16,20},{18,... | collective-permute-start | bytes 786440 | tf_op jit(solution)/shard_map/ppermute | solution.py:32
  15.2 14.8 %collective-permute-start.8 = (bf16[4,2,32,512]{3,2,1,0:T(8,128)(2,1)S(1)}, bf16[4,2,32,512]{3,2,1,0:T(8,128)(2,1)S(1)}, u32[]{:S(2)}, u32[]{:S(2)}) collective-permute-start(bf16[4,2,32,512]{3,2,1,0:T(8,128)(2,1)S(1)} %get-tuple-element.58), channel_id=1, source_target_pairs={{0,6},{2,4},{4,2},{6,0},{8,14},{10,12},{12,10},{14,8},{16,22},{18,... | collective-permute-start | bytes 786440 | tf_op jit(solution)/shard_map/ppermute | solution.py:32
  24.9 9.2 %collective-permute-start = (bf16[4,2,32,512]{3,2,1,0:T(8,128)(2,1)S(1)}, bf16[4,2,32,512]{3,2,1,0:T(8,128)(2,1)S(1)}, u32[]{:S(2)}, u32[]{:S(2)}) collective-permute-start(bf16[4,2,32,512]{3,2,1,0:T(8,128)(2,1)S(1)} %get-tuple-element.65), channel_id=1, source_target_pairs={{0,2},{2,0},{4,6},{6,4},{8,10},{10,8},{12,14},{14,12},{16,18},{18,... | collective-permute-start | bytes 786440 | tf_op jit(solution)/shard_map/ppermute | solution.py:32
  25.8 11.1 %collective-permute-start.1 = (bf16[4,2,32,512]{3,2,1,0:T(8,128)(2,1)S(1)}, bf16[4,2,32,512]{3,2,1,0:T(8,128)(2,1)S(1)}, u32[]{:S(2)}, u32[]{:S(2)}) collective-permute-start(bf16[4,2,32,512]{3,2,1,0:T(8,128)(2,1)S(1)} %get-tuple-element.64), channel_id=1, source_target_pairs={{0,4},{2,6},{4,0},{6,2},{8,12},{10,14},{12,8},{14,10},{16,20},{18,... | collective-permute-start | bytes 786440 | tf_op jit(solution)/shard_map/ppermute | solution.py:32
  27.3 13.4 %collective-permute-start.2 = (bf16[4,2,32,512]{3,2,1,0:T(8,128)(2,1)S(1)}, bf16[4,2,32,512]{3,2,1,0:T(8,128)(2,1)S(1)}, u32[]{:S(2)}, u32[]{:S(2)}) collective-permute-start(bf16[4,2,32,512]{3,2,1,0:T(8,128)(2,1)S(1)} %get-tuple-element.63), channel_id=1, source_target_pairs={{0,6},{2,4},{4,2},{6,0},{8,14},{10,12},{12,10},{14,8},{16,22},{18,... | collective-permute-start | bytes 786440 | tf_op jit(solution)/shard_map/ppermute | solution.py:32
  29.1 38.6 %collective-permute-start.22 = (bf16[32,7168]{1,0:T(8,128)(2,1)S(1)}, bf16[32,7168]{1,0:T(8,128)(2,1)S(1)}, u32[]{:S(2)}, u32[]{:S(2)}) collective-permute-start(bf16[32,7168]{1,0:T(8,128)(2,1)S(1)} %shard_map.72.refs_0_), channel_id=1, source_target_pairs={{0,2},{2,0},{4,6},{6,4},{8,10},{10,8},{12,14},{14,12},{16,18},{18,... | collective-permute-start | bytes 1376264 | tf_op jit(solution)/shard_map/ppermute | solution.py:32
  30.7 11.5 %collective-permute-start.10 = (bf16[2,32,512]{2,1,0:T(8,128)(2,1)S(1)}, bf16[2,32,512]{2,1,0:T(8,128)(2,1)S(1)}, u32[]{:S(2)}, u32[]{:S(2)}) collective-permute-start(bf16[2,32,512]{2,1,0:T(8,128)(2,1)S(1)} %get-tuple-element.36), channel_id=1, source_target_pairs={{0,16},{2,18},{4,20},{6,22},{8,24},{10,26},{12,28},{14,30},{16,0},... | collective-permute-start | bytes 196616 | tf_op jit(solution)/shard_map/ppermute | solution.py:32
  34.2 9.6 %collective-permute-start.11 = (bf16[2,32,512]{2,1,0:T(8,128)(2,1)S(1)}, bf16[2,32,512]{2,1,0:T(8,128)(2,1)S(1)}, u32[]{:S(2)}, u32[]{:S(2)}) collective-permute-start(bf16[2,32,512]{2,1,0:T(8,128)(2,1)S(1)} %get-tuple-element.37), channel_id=1, source_target_pairs={{0,24},{2,26},{4,28},{6,30},{8,16},{10,18},{12,20},{14,22},{16,8},... | collective-permute-start | bytes 196616 | tf_op jit(solution)/shard_map/ppermute | solution.py:32
  36.9 31.9 %collective-permute-start.23 = (bf16[32,7168]{1,0:T(8,128)(2,1)S(1)}, bf16[32,7168]{1,0:T(8,128)(2,1)S(1)}, u32[]{:S(2)}, u32[]{:S(2)}) collective-permute-start(bf16[32,7168]{1,0:T(8,128)(2,1)S(1)} %shard_map.72.refs_0_), channel_id=1, source_target_pairs={{0,4},{2,6},{4,0},{6,2},{8,12},{10,14},{12,8},{14,10},{16,20},{18,... | collective-permute-start | bytes 1376264 | tf_op jit(solution)/shard_map/ppermute | solution.py:32
  40.7 29.0 %collective-permute-start.24 = (bf16[32,7168]{1,0:T(8,128)(2,1)S(1)}, bf16[32,7168]{1,0:T(8,128)(2,1)S(1)}, u32[]{:S(2)}, u32[]{:S(2)}) collective-permute-start(bf16[32,7168]{1,0:T(8,128)(2,1)S(1)} %shard_map.72.refs_0_), channel_id=1, source_target_pairs={{0,6},{2,4},{4,2},{6,0},{8,14},{10,12},{12,10},{14,8},{16,22},{18,... | collective-permute-start | bytes 1376264 | tf_op jit(solution)/shard_map/ppermute | solution.py:32
  43.8 5.6 %collective-permute-start.3 = (bf16[2,32,512]{2,1,0:T(8,128)(2,1)S(1)}, bf16[2,32,512]{2,1,0:T(8,128)(2,1)S(1)}, u32[]{:S(2)}, u32[]{:S(2)}) collective-permute-start(bf16[2,32,512]{2,1,0:T(8,128)(2,1)S(1)} %get-tuple-element.31), channel_id=1, source_target_pairs={{0,8},{2,10},{4,12},{6,14},{8,0},{10,2},{12,4},{14,6},{16,24},{18,... | collective-permute-start | bytes 196616 | tf_op jit(solution)/shard_map/ppermute | solution.py:32
  46.5 5.4 %collective-permute-start.4 = (bf16[2,32,512]{2,1,0:T(8,128)(2,1)S(1)}, bf16[2,32,512]{2,1,0:T(8,128)(2,1)S(1)}, u32[]{:S(2)}, u32[]{:S(2)}) collective-permute-start(bf16[2,32,512]{2,1,0:T(8,128)(2,1)S(1)} %get-tuple-element.32), channel_id=1, source_target_pairs={{0,16},{2,18},{4,20},{6,22},{8,24},{10,26},{12,28},{14,30},{16,0},... | collective-permute-start | bytes 196616 | tf_op jit(solution)/shard_map/ppermute | solution.py:32
  49.4 6.1 %collective-permute-start.5 = (bf16[2,32,512]{2,1,0:T(8,128)(2,1)S(1)}, bf16[2,32,512]{2,1,0:T(8,128)(2,1)S(1)}, u32[]{:S(2)}, u32[]{:S(2)}) collective-permute-start(bf16[2,32,512]{2,1,0:T(8,128)(2,1)S(1)} %get-tuple-element.33), channel_id=1, source_target_pairs={{0,24},{2,26},{4,28},{6,30},{8,16},{10,18},{12,20},{14,22},{16,8},... | collective-permute-start | bytes 196616 | tf_op jit(solution)/shard_map/ppermute | solution.py:32
  64.8 8.5 %collective-permute-start.25 = (bf16[4,32,512]{2,1,0:T(8,128)(2,1)S(1)}, bf16[4,32,512]{2,1,0:T(8,128)(2,1)S(1)}, u32[]{:S(2)}, u32[]{:S(2)}) collective-permute-start(bf16[4,32,512]{2,1,0:T(8,128)(2,1)S(1)} %get-tuple-element.45.refs_2_), channel_id=1, source_target_pairs={{0,2},{2,0},{4,6},{6,4},{8,10},{10,8},{12,14},{14,12},{16,18},{18,... | collective-permute-start | bytes 393224 | tf_op jit(solution)/shard_map/ppermute | solution.py:32
  66.2 8.3 %collective-permute-start.26 = (bf16[4,32,512]{2,1,0:T(8,128)(2,1)S(1)}, bf16[4,32,512]{2,1,0:T(8,128)(2,1)S(1)}, u32[]{:S(2)}, u32[]{:S(2)}) collective-permute-start(bf16[4,32,512]{2,1,0:T(8,128)(2,1)S(1)} %get-tuple-element.45.refs_2_), channel_id=1, source_target_pairs={{0,4},{2,6},{4,0},{6,2},{8,12},{10,14},{12,8},{14,10},{16,20},{18,... | collective-permute-start | bytes 393224 | tf_op jit(solution)/shard_map/ppermute | solution.py:32
  67.7 7.0 %collective-permute-start.27 = (bf16[4,32,512]{2,1,0:T(8,128)(2,1)S(1)}, bf16[4,32,512]{2,1,0:T(8,128)(2,1)S(1)}, u32[]{:S(2)}, u32[]{:S(2)}) collective-permute-start(bf16[4,32,512]{2,1,0:T(8,128)(2,1)S(1)} %get-tuple-element.45.refs_2_), channel_id=1, source_target_pairs={{0,6},{2,4},{4,2},{6,0},{8,14},{10,12},{12,10},{14,8},{16,22},{18,... | collective-permute-start | bytes 393224 | tf_op jit(solution)/shard_map/ppermute | solution.py:32
  68.8 8.1 %collective-permute-start.16 = (f32[8,128]{1,0:T(8,128)S(1)}, f32[8,128]{1,0:T(8,128)S(1)}, u32[]{:S(2)}, u32[]{:S(2)}) collective-permute-start(f32[8,128]{1,0:T(8,128)S(1)} %add.41.refs_0_), channel_id=1, source_target_pairs={{0,2},{2,0},{4,6},{6,4},{8,10},{10,8},{12,14},{14,12},{16,18},{18,... | collective-permute-start | bytes 12296 | tf_op jit(solution)/shard_map/ppermute | solution.py:32
  69.7 7.2 %collective-permute-start.17 = (f32[8,128]{1,0:T(8,128)S(1)}, f32[8,128]{1,0:T(8,128)S(1)}, u32[]{:S(2)}, u32[]{:S(2)}) collective-permute-start(f32[8,128]{1,0:T(8,128)S(1)} %add.41.refs_0_), channel_id=1, source_target_pairs={{0,4},{2,6},{4,0},{6,2},{8,12},{10,14},{12,8},{14,10},{16,20},{18,... | collective-permute-start | bytes 12296 | tf_op jit(solution)/shard_map/ppermute | solution.py:32
  80.4 9.6 %collective-permute-start.29 = (bf16[32,1536]{1,0:T(8,128)(2,1)S(1)}, bf16[32,1536]{1,0:T(8,128)(2,1)S(1)}, u32[]{:S(2)}, u32[]{:S(2)}) collective-permute-start(bf16[32,1536]{1,0:T(8,128)(2,1)S(1)} %get-tuple-element.54), channel_id=1, source_target_pairs={{0,16},{2,18},{4,20},{6,22},{8,24},{10,26},{12,28},{14,30},{16,0},... | collective-permute-start | bytes 294920 | tf_op jit(solution)/shard_map/ppermute | solution.py:32
  82.9 7.1 %collective-permute-start.30 = (bf16[32,1536]{1,0:T(8,128)(2,1)S(1)}, bf16[32,1536]{1,0:T(8,128)(2,1)S(1)}, u32[]{:S(2)}, u32[]{:S(2)}) collective-permute-start(bf16[32,1536]{1,0:T(8,128)(2,1)S(1)} %get-tuple-element.55), channel_id=1, source_target_pairs={{0,24},{2,26},{4,28},{6,30},{8,16},{10,18},{12,20},{14,22},{16,8},... | collective-permute-start | bytes 294920 | tf_op jit(solution)/shard_map/ppermute | solution.py:32
  (13 other events, 57.0 us)

commit v2 on v1

--- a/solution.py
+++ b/solution.py
@@ -12,7 +12,7 @@
 LEARN_RATE = 0.1
 EPS_NORM = 1e-06
 LANES = 128
-CHUNKS = 2
+CHUNKS = 1
 VMEM_GRANT = 16 * 2**20
 FLOAT = jnp.float32
 HALF = jnp.bfloat16
@@ -41,12 +41,12 @@
     return jnp.stack([pick(stacked, own ^ k, 0) for k in range(len(pieces))])
 
 
-def call(kernel, out_shape, scratch, flops, smem, *operands):
+def call(kernel, out_shape, scratch, flops, smem, *operands, space=pltpu.VMEM):
     moved = sum(x.size * x.dtype.itemsize for x in (*operands, *jax.tree.leaves(out_shape)))
     return pl.pallas_call(
         kernel,
         out_shape=out_shape,
-        in_specs=[SMEM_SPEC] * smem + [VMEM_SPEC] * (len(operands) - smem),
+        in_specs=[SMEM_SPEC] * smem + [pl.BlockSpec(memory_space=space)] * (len(operands) - smem),
         out_specs=jax.tree.map(lambda _: VMEM_SPEC, out_shape),
         scratch_shapes=scratch,
         cost_estimate=pl.CostEstimate(flops=flops, bytes_accessed=moved, transcendentals=0),
@@ -73,13 +73,22 @@
         return sum(self.size - first for _, _, first, _ in self.spots())
 
 
-def choose_kernel(plan, where, slots, factors, inverses, probes, *outs):
-    size = plan.size
+def choose_kernel(plan, where, slots, factors, inverses, probes, *refs):
+    outs, done = refs[:-1], refs[-1]
+    size, copies = plan.size, []
     for k, out in enumerate(outs):
         slot = slots[where[0] ^ k]
-        out[:, : 2 * size] = factors[slot]
-        out[:, 2 * size : 4 * size] = inverses[slot]
-        out[:, 4 * size :] = probes[slot]
+        parts = (
+            (factors, out.at[:, : 2 * size]),
+            (inverses, out.at[:, 2 * size : 4 * size]),
+            (probes, out.at[:, 4 * size :]),
+        )
+        for i, (source, target) in enumerate(parts):
+            copies.append(pltpu.make_async_copy(source.at[slot], target, done.at[3 * k + i]))
+    for copy in copies:
+        copy.start()
+    for copy in copies:
+        copy.wait()
 
 
 def pack_kernel(plan, where, *refs):
@@ -245,7 +254,7 @@
         pieces = call(
             functools.partial(choose_kernel, plan),
             tuple(shaped((rows, 5 * size)) for _ in range(blocks)),
-            [],
+            [pltpu.SemaphoreType.DMA((3 * blocks,))],
             0,
             2,
             where,
@@ -253,6 +262,7 @@
             old_state,
             inverse_factors[0],
             probes[0],
+            space=pl.ANY,
         )
     else:
         wide = jnp.concatenate([old_state, inverse_factors[0], probes[0]], axis=2)

time: 91.6 us -> 80.5 us (0.88)
  starting transfers between devices: 44.6 us -> 38.9 us
  waiting for transfers between devices: 29 us -> 26.3 us
  local copies, waits for them, and re-layouts: 5.98 us -> 3.72 us
    ppermute x30 -> x24, starting transfers between devices: 44.6 us -> 38.9 us  [flip(): return lax.ppermute(array, 'dp', [(i, i ^ mask) for i in range(devices)])]
    unnamed x12 -> x8, local copies, waits for them, and re-layouts: 3.47 us -> 0.02 us
    ppermute x30 -> x24, waiting for transfers between devices: 29 us -> 26.3 us  [flip(): return lax.ppermute(array, 'dp', [(i, i ^ mask) for i in range(devices)])]
    reshape x2, local copies, waits for them, and re-layouts: 2.51 us -> 3.7 us  [body(): cut = [lax.dynamic_slice(grads if i == 0 and k > 0 else later, (0, i * st...]
    pallas_call x9 -> x8, Pallas kernels: 10.8 us -> 10.5 us  [call(): pl.pallas_call(kernel, out_shape=out_shape, in_specs=[SMEM_SPEC] * smem +...]
  transfers between devices with their start and end apart: 31 -> 25, of which waited for: 11 -> 10; matrix products, arithmetic and copies ran while one was open for 3% -> 1% of each run, Pallas kernels for 7% -> 9%
where the time goes in v2:
time: 80.5 us; the launch traced here: 80.3 us
  starting transfers between devices  38.9 us (48%)
  waiting for transfers between devices  26.3 us (33%)
  Pallas kernels  10.5 us (13%)
  local copies, waits for them, and re-layouts  3.72 us (5%)
  between operations  0.83 us (1%)
    ppermute x24, starting transfers between devices, flip(): return lax.ppermute(array, 'dp', [(i, i ^ mask) for i in range(devices)])  38.9 us
    ppermute x24, waiting for transfers between devices, flip(): return lax.ppermute(array, 'dp', [(i, i ^ mask) for i in range(devices)])  26.3 us
    pallas_call x8, Pallas kernels, call(): pl.pallas_call(kernel, out_shape=out_shape, in_specs=[SMEM_SPEC] * smem +...  10.5 us
    reshape x2, local copies, waits for them, and re-layouts, body(): cut = [lax.dynamic_slice(grads if i == 0 and k > 0 else later, (0, i * st...  3.7 us
  transfers between devices with their start and end apart: 25, of which 10 were waited for; matrix products, arithmetic and copies ran while one was open for 1% of the time, Pallas kernels for 9%

profile of v2, /device:TPU:0, one launch (start us, length us, event | category | flops | bytes accessed | tf_op | source)
XLA Modules:
  0.0 80.3 jit_solution(1403856610893429893)
XLA Ops:
  0.7 2.6 %dynamic-slice_bitcast_fusion = (bf16[4,4,32,512]{3,2,1,0:T(8,128)(2,1)}, bf16[4,4,32,512]{3,2,1,0:T(8,128)(2,1)}, bf16[4,4,32,512]{3,2,1,0:T(8,128)(2,1)}) fusion(bf16[4,4,4,32,512]{4,3,2,1,0:T(8,128)(2,1)} %bitcast.31, s32[]{:T(128)S(6)} %select_n.28, s32[]{:T(128)S(6)} %select_n.27, s32[]{:T(128)S(6)} %select_n.26), kind=kLoop, calls=%fused_computation | loop fusion | bytes 3145740 | tf_op jit(solution)/shard_map/reshape | solution.py:247
  3.3 3.0 %collective-permute-start = (bf16[4,4,32,512]{3,2,1,0:T(8,128)(2,1)}, bf16[4,4,32,512]{3,2,1,0:T(8,128)(2,1)S(1)}, u32[]{:S(2)}, u32[]{:S(2)}) collective-permute-start(bf16[4,4,32,512]{3,2,1,0:T(8,128)(2,1)} %get-tuple-element.52), channel_id=1, source_target_pairs={{0,2},{2,0},{4,6},{6,4},{8,10},{10,8},{12,14},{14,12},{16,18},{18,... | collective-permute-start | bytes 1572872 | tf_op jit(solution)/shard_map/ppermute | solution.py:32
  8.8 2.1 %collective-permute-start.13 = (bf16[32,2560]{1,0:T(8,128)(2,1)S(1)}, bf16[32,2560]{1,0:T(8,128)(2,1)S(1)}, u32[]{:S(2)}, u32[]{:S(2)}) collective-permute-start(bf16[32,2560]{1,0:T(8,128)(2,1)S(1)} %get-tuple-element.32), channel_id=1, source_target_pairs={{0,8},{2,10},{4,12},{6,14},{8,0},{10,2},{12,4},{14,6},{16,24},{18,... | collective-permute-start | bytes 491528 | tf_op jit(solution)/shard_map/ppermute | solution.py:32
  10.9 2.6 %collective-permute-start.14 = (bf16[32,2560]{1,0:T(8,128)(2,1)S(1)}, bf16[32,2560]{1,0:T(8,128)(2,1)S(1)}, u32[]{:S(2)}, u32[]{:S(2)}) collective-permute-start(bf16[32,2560]{1,0:T(8,128)(2,1)S(1)} %get-tuple-element.33), channel_id=1, source_target_pairs={{0,16},{2,18},{4,20},{6,22},{8,24},{10,26},{12,28},{14,30},{16,0},... | collective-permute-start | bytes 491528 | tf_op jit(solution)/shard_map/ppermute | solution.py:32
  13.5 3.2 %collective-permute-done.13.refs_1_ = bf16[32,2560]{1,0:T(8,128)(2,1)S(1)} collective-permute-done((bf16[32,2560]{1,0:T(8,128)(2,1)S(1)}, bf16[32,2560]{1,0:T(8,128)(2,1)S(1)}, u32[]{:S(2)}, u32[]{:S(2)}) %collective-permute-start.13) | collective-permute-done | bytes 163872 | tf_op jit(solution)/shard_map/ppermute | solution.py:32
  16.7 3.9 %collective-permute-start.15 = (bf16[32,2560]{1,0:T(8,128)(2,1)S(1)}, bf16[32,2560]{1,0:T(8,128)(2,1)S(1)}, u32[]{:S(2)}, u32[]{:S(2)}) collective-permute-start(bf16[32,2560]{1,0:T(8,128)(2,1)S(1)} %get-tuple-element.34), channel_id=1, source_target_pairs={{0,24},{2,26},{4,28},{6,30},{8,16},{10,18},{12,20},{14,22},{16,8},... | collective-permute-start | bytes 491528 | tf_op jit(solution)/shard_map/ppermute | solution.py:32
  20.5 3.8 %collective-permute-done.14.refs_2_ = bf16[32,2560]{1,0:T(8,128)(2,1)S(1)} collective-permute-done((bf16[32,2560]{1,0:T(8,128)(2,1)S(1)}, bf16[32,2560]{1,0:T(8,128)(2,1)S(1)}, u32[]{:S(2)}, u32[]{:S(2)}) %collective-permute-start.14) | collective-permute-done | bytes 163872 | tf_op jit(solution)/shard_map/ppermute | solution.py:32
  25.0 1.9 %collective-permute-start.16 = (bf16[32,7168]{1,0:T(8,128)(2,1)S(1)}, bf16[32,7168]{1,0:T(8,128)(2,1)S(1)}, u32[]{:S(2)}, u32[]{:S(2)}) collective-permute-start(bf16[32,7168]{1,0:T(8,128)(2,1)S(1)} %shard_map.71.refs_0_), channel_id=1, source_target_pairs={{0,2},{2,0},{4,6},{6,4},{8,10},{10,8},{12,14},{14,12},{16,18},{18,... | collective-permute-start | bytes 1376264 | tf_op jit(solution)/shard_map/ppermute | solution.py:32
  28.0 2.3 %collective-permute-done.1.refs_2_ = bf16[4,4,32,512]{3,2,1,0:T(8,128)(2,1)S(1)} collective-permute-done((bf16[4,4,32,512]{3,2,1,0:T(8,128)(2,1)}, bf16[4,4,32,512]{3,2,1,0:T(8,128)(2,1)S(1)}, u32[]{:S(2)}, u32[]{:S(2)}) %collective-permute-start.1) | collective-permute-done | bytes 524320 | tf_op jit(solution)/shard_map/ppermute | solution.py:32
  30.3 1.8 %collective-permute-done.2.refs_3_ = bf16[4,4,32,512]{3,2,1,0:T(8,128)(2,1)S(1)} collective-permute-done((bf16[4,4,32,512]{3,2,1,0:T(8,128)(2,1)}, bf16[4,4,32,512]{3,2,1,0:T(8,128)(2,1)S(1)}, u32[]{:S(2)}, u32[]{:S(2)}) %collective-permute-start.2) | collective-permute-done | bytes 524320 | tf_op jit(solution)/shard_map/ppermute | solution.py:32
  35.1 2.1 %collective-permute-start.18 = (bf16[32,7168]{1,0:T(8,128)(2,1)S(1)}, bf16[32,7168]{1,0:T(8,128)(2,1)S(1)}, u32[]{:S(2)}, u32[]{:S(2)}) collective-permute-start(bf16[32,7168]{1,0:T(8,128)(2,1)S(1)} %shard_map.71.refs_0_), channel_id=1, source_target_pairs={{0,6},{2,4},{4,2},{6,0},{8,14},{10,12},{12,10},{14,8},{16,22},{18,... | collective-permute-start | bytes 1376264 | tf_op jit(solution)/shard_map/ppermute | solution.py:32
  37.2 2.8 %collective-permute-start.4 = (bf16[4,32,512]{2,1,0:T(8,128)(2,1)S(1)}, bf16[4,32,512]{2,1,0:T(8,128)(2,1)S(1)}, u32[]{:S(2)}, u32[]{:S(2)}) collective-permute-start(bf16[4,32,512]{2,1,0:T(8,128)(2,1)S(1)} %get-tuple-element.28), channel_id=1, source_target_pairs={{0,16},{2,18},{4,20},{6,22},{8,24},{10,26},{12,28},{14,30},{16,0},... | collective-permute-start | bytes 393224 | tf_op jit(solution)/shard_map/ppermute | solution.py:32
  40.0 2.6 %collective-permute-start.5 = (bf16[4,32,512]{2,1,0:T(8,128)(2,1)S(1)}, bf16[4,32,512]{2,1,0:T(8,128)(2,1)S(1)}, u32[]{:S(2)}, u32[]{:S(2)}) collective-permute-start(bf16[4,32,512]{2,1,0:T(8,128)(2,1)S(1)} %get-tuple-element.29), channel_id=1, source_target_pairs={{0,24},{2,26},{4,28},{6,30},{8,16},{10,18},{12,20},{14,22},{16,8},... | collective-permute-start | bytes 393224 | tf_op jit(solution)/shard_map/ppermute | solution.py:32
  42.5 5.1 %collective-permute-done.4.refs_2_ = bf16[4,32,512]{2,1,0:T(8,128)(2,1)S(1)} collective-permute-done((bf16[4,32,512]{2,1,0:T(8,128)(2,1)S(1)}, bf16[4,32,512]{2,1,0:T(8,128)(2,1)S(1)}, u32[]{:S(2)}, u32[]{:S(2)}) %collective-permute-start.4) | collective-permute-done | bytes 131104 | tf_op jit(solution)/shard_map/ppermute | solution.py:32
  47.9 2.0 %collective-permute-start.6 = (f32[8,128]{1,0:T(8,128)S(1)}, f32[8,128]{1,0:T(8,128)S(1)}, u32[]{:S(2)}, u32[]{:S(2)}) collective-permute-start(f32[8,128]{1,0:T(8,128)S(1)} %get-tuple-element.30), channel_id=1, source_target_pairs={{0,8},{2,10},{4,12},{6,14},{8,0},{10,2},{12,4},{14,6},{16,24},{18,... | collective-permute-start | bytes 12296 | tf_op jit(solution)/shard_map/ppermute | solution.py:32
  54.9 1.6 %collective-permute-done.8 = f32[8,128]{1,0:T(8,128)S(1)} collective-permute-done((f32[8,128]{1,0:T(8,128)S(1)}, f32[8,128]{1,0:T(8,128)S(1)}, u32[]{:S(2)}, u32[]{:S(2)}) %collective-permute-start.8) | collective-permute-done | bytes 4128 | tf_op jit(solution)/shard_map/ppermute | solution.py:32
  57.1 2.1 %shard_map.72 = (bf16[512,512]{1,0:T(8,128)(2,1)S(1)}, bf16[512,512]{1,0:T(8,128)(2,1)S(1)}, f32[512,512]{1,0:T(8,128)S(1)}, f32[512,512]{1,0:T(8,128)S(1)}) custom-call(s32[2]{0:T(128)S(1)} %pad_add_fusion.where, bf16[32,7168]{1,0:T(8,128)(2,1)S(1)} %shard_map.71.refs_0_, bf16[32,7168]{1,0:T(8,128)(2,1)S(1)} %collective-permute-done.16.refs_1_, ...), custom_call_target="tpu_custom_call" | custom-call | flops 1073741824 | bytes 4980744 | tf_op jit(solution)/shard_map/pallas_call | solution.py:46
  59.2 1.6 %collective-permute-start.10 = (f32[8,128]{1,0:T(8,128)S(1)}, f32[8,128]{1,0:T(8,128)S(1)}, u32[]{:S(2)}, u32[]{:S(2)}) collective-permute-start(f32[8,128]{1,0:T(8,128)S(1)} %add.37.refs_0_), channel_id=1, source_target_pairs={{0,2},{2,0},{4,6},{6,4},{8,10},{10,8},{12,14},{14,12},{16,18},{18,... | collective-permute-start | bytes 12296 | tf_op jit(solution)/shard_map/ppermute | solution.py:32
  62.8 2.2 %shard_map.73 = (bf16[512,512]{1,0:T(8,128)(2,1)S(1)}, f32[512,512]{1,0:T(8,128)S(1)}, f32[512,512]{1,0:T(8,128)S(1)}, f32[8,128]{1,0:T(8,128)S(1)}) custom-call(s32[2]{0:T(128)S(1)} %pad_add_fusion.where, bf16[512,512]{1,0:T(8,128)(2,1)S(1)} %get-tuple-element.35.refs_0_.refs_5_, bf16[512,512]{1,0:T(8,128)(2,1)S(1)} %get-tuple-element.36.refs_1_.refs_6_, ...), custom_call_target="tpu_custom_call" | custom-call | flops 1073741824 | bytes 4198408 | tf_op jit(solution)/shard_map/pallas_call | solution.py:46
  65.0 1.8 %collective-permute-done.12.refs_3_ = f32[8,128]{1,0:T(8,128)S(1)} collective-permute-done((f32[8,128]{1,0:T(8,128)S(1)}, f32[8,128]{1,0:T(8,128)S(1)}, u32[]{:S(2)}, u32[]{:S(2)}) %collective-permute-start.12) | collective-permute-done | bytes 4128 | tf_op jit(solution)/shard_map/ppermute | solution.py:32
  66.8 2.3 %shard_map.74 = (bf16[32,1536]{1,0:T(8,128)(2,1)S(1)}, bf16[32,1536]{1,0:T(8,128)(2,1)S(1)}, bf16[32,1536]{1,0:T(8,128)(2,1)S(1)}, bf16[32,1536]{1,0:T(8,128)(2,1)S(1)}) custom-call(s32[2]{0:T(128)S(1)} %pad_add_fusion.where, f32[8,128]{1,0:T(8,128)S(1)} %add.37.refs_0_, f32[8,128]{1,0:T(8,128)S(1)} %collective-permute-done.10.refs_1_, ...), custom_call_target="tpu_custom_call" | custom-call | flops 1342177280 | bytes 6180872 | tf_op jit(solution)/shard_map/pallas_call | solution.py:46
  69.4 1.8 %collective-permute-start.23 = (bf16[32,1536]{1,0:T(8,128)(2,1)S(1)}, bf16[32,1536]{1,0:T(8,128)(2,1)S(1)}, u32[]{:S(2)}, u32[]{:S(2)}) collective-permute-start(bf16[32,1536]{1,0:T(8,128)(2,1)S(1)} %get-tuple-element.46), channel_id=1, source_target_pairs={{0,16},{2,18},{4,20},{6,22},{8,24},{10,26},{12,28},{14,30},{16,0},... | collective-permute-start | bytes 294920 | tf_op jit(solution)/shard_map/ppermute | solution.py:32
  71.2 2.4 %collective-permute-start.24 = (bf16[32,1536]{1,0:T(8,128)(2,1)S(1)}, bf16[32,1536]{1,0:T(8,128)(2,1)S(1)}, u32[]{:S(2)}, u32[]{:S(2)}) collective-permute-start(bf16[32,1536]{1,0:T(8,128)(2,1)S(1)} %get-tuple-element.47), channel_id=1, source_target_pairs={{0,24},{2,26},{4,28},{6,30},{8,16},{10,18},{12,20},{14,22},{16,8},... | collective-permute-start | bytes 294920 | tf_op jit(solution)/shard_map/ppermute | solution.py:32
  73.8 5.2 %collective-permute-done.23.refs_2_ = bf16[32,1536]{1,0:T(8,128)(2,1)S(1)} collective-permute-done((bf16[32,1536]{1,0:T(8,128)(2,1)S(1)}, bf16[32,1536]{1,0:T(8,128)(2,1)S(1)}, u32[]{:S(2)}, u32[]{:S(2)}) %collective-permute-start.23) | collective-permute-done | bytes 98336 | tf_op jit(solution)/shard_map/ppermute | solution.py:32
  (47 shorter events, 16.9 us)
Async XLA Ops:
  3.3 24.6 %collective-permute-start = (bf16[4,4,32,512]{3,2,1,0:T(8,128)(2,1)}, bf16[4,4,32,512]{3,2,1,0:T(8,128)(2,1)S(1)}, u32[]{:S(2)}, u32[]{:S(2)}) collective-permute-start(bf16[4,4,32,512]{3,2,1,0:T(8,128)(2,1)} %get-tuple-element.52), channel_id=1, source_target_pairs={{0,2},{2,0},{4,6},{6,4},{8,10},{10,8},{12,14},{14,12},{16,18},{18,... | collective-permute-start | bytes 1572872 | tf_op jit(solution)/shard_map/ppermute | solution.py:32
  6.3 24.0 %collective-permute-start.1 = (bf16[4,4,32,512]{3,2,1,0:T(8,128)(2,1)}, bf16[4,4,32,512]{3,2,1,0:T(8,128)(2,1)S(1)}, u32[]{:S(2)}, u32[]{:S(2)}) collective-permute-start(bf16[4,4,32,512]{3,2,1,0:T(8,128)(2,1)} %get-tuple-element.51), channel_id=1, source_target_pairs={{0,4},{2,6},{4,0},{6,2},{8,12},{10,14},{12,8},{14,10},{16,20},{18,... | collective-permute-start | bytes 1572872 | tf_op jit(solution)/shard_map/ppermute | solution.py:32
  7.8 24.2 %collective-permute-start.2 = (bf16[4,4,32,512]{3,2,1,0:T(8,128)(2,1)}, bf16[4,4,32,512]{3,2,1,0:T(8,128)(2,1)S(1)}, u32[]{:S(2)}, u32[]{:S(2)}) collective-permute-start(bf16[4,4,32,512]{3,2,1,0:T(8,128)(2,1)} %get-tuple-element.50), channel_id=1, source_target_pairs={{0,6},{2,4},{4,2},{6,0},{8,14},{10,12},{12,10},{14,8},{16,22},{18,... | collective-permute-start | bytes 1572872 | tf_op jit(solution)/shard_map/ppermute | solution.py:32
  8.8 7.9 %collective-permute-start.13 = (bf16[32,2560]{1,0:T(8,128)(2,1)S(1)}, bf16[32,2560]{1,0:T(8,128)(2,1)S(1)}, u32[]{:S(2)}, u32[]{:S(2)}) collective-permute-start(bf16[32,2560]{1,0:T(8,128)(2,1)S(1)} %get-tuple-element.32), channel_id=1, source_target_pairs={{0,8},{2,10},{4,12},{6,14},{8,0},{10,2},{12,4},{14,6},{16,24},{18,... | collective-permute-start | bytes 491528 | tf_op jit(solution)/shard_map/ppermute | solution.py:32
  10.9 13.4 %collective-permute-start.14 = (bf16[32,2560]{1,0:T(8,128)(2,1)S(1)}, bf16[32,2560]{1,0:T(8,128)(2,1)S(1)}, u32[]{:S(2)}, u32[]{:S(2)}) collective-permute-start(bf16[32,2560]{1,0:T(8,128)(2,1)S(1)} %get-tuple-element.33), channel_id=1, source_target_pairs={{0,16},{2,18},{4,20},{6,22},{8,24},{10,26},{12,28},{14,30},{16,0},... | collective-permute-start | bytes 491528 | tf_op jit(solution)/shard_map/ppermute | solution.py:32
  16.7 7.7 %collective-permute-start.15 = (bf16[32,2560]{1,0:T(8,128)(2,1)S(1)}, bf16[32,2560]{1,0:T(8,128)(2,1)S(1)}, u32[]{:S(2)}, u32[]{:S(2)}) collective-permute-start(bf16[32,2560]{1,0:T(8,128)(2,1)S(1)} %get-tuple-element.34), channel_id=1, source_target_pairs={{0,24},{2,26},{4,28},{6,30},{8,16},{10,18},{12,20},{14,22},{16,8},... | collective-permute-start | bytes 491528 | tf_op jit(solution)/shard_map/ppermute | solution.py:32
  25.0 26.2 %collective-permute-start.16 = (bf16[32,7168]{1,0:T(8,128)(2,1)S(1)}, bf16[32,7168]{1,0:T(8,128)(2,1)S(1)}, u32[]{:S(2)}, u32[]{:S(2)}) collective-permute-start(bf16[32,7168]{1,0:T(8,128)(2,1)S(1)} %shard_map.71.refs_0_), channel_id=1, source_target_pairs={{0,2},{2,0},{4,6},{6,4},{8,10},{10,8},{12,14},{14,12},{16,18},{18,... | collective-permute-start | bytes 1376264 | tf_op jit(solution)/shard_map/ppermute | solution.py:32
  32.8 7.1 %collective-permute-start.3 = (bf16[4,32,512]{2,1,0:T(8,128)(2,1)S(1)}, bf16[4,32,512]{2,1,0:T(8,128)(2,1)S(1)}, u32[]{:S(2)}, u32[]{:S(2)}) collective-permute-start(bf16[4,32,512]{2,1,0:T(8,128)(2,1)S(1)} %get-tuple-element.27), channel_id=1, source_target_pairs={{0,8},{2,10},{4,12},{6,14},{8,0},{10,2},{12,4},{14,6},{16,24},{18,... | collective-permute-start | bytes 393224 | tf_op jit(solution)/shard_map/ppermute | solution.py:32
  34.3 22.7 %collective-permute-start.17 = (bf16[32,7168]{1,0:T(8,128)(2,1)S(1)}, bf16[32,7168]{1,0:T(8,128)(2,1)S(1)}, u32[]{:S(2)}, u32[]{:S(2)}) collective-permute-start(bf16[32,7168]{1,0:T(8,128)(2,1)S(1)} %shard_map.71.refs_0_), channel_id=1, source_target_pairs={{0,4},{2,6},{4,0},{6,2},{8,12},{10,14},{12,8},{14,10},{16,20},{18,... | collective-permute-start | bytes 1376264 | tf_op jit(solution)/shard_map/ppermute | solution.py:32
  35.1 22.0 %collective-permute-start.18 = (bf16[32,7168]{1,0:T(8,128)(2,1)S(1)}, bf16[32,7168]{1,0:T(8,128)(2,1)S(1)}, u32[]{:S(2)}, u32[]{:S(2)}) collective-permute-start(bf16[32,7168]{1,0:T(8,128)(2,1)S(1)} %shard_map.71.refs_0_), channel_id=1, source_target_pairs={{0,6},{2,4},{4,2},{6,0},{8,14},{10,12},{12,10},{14,8},{16,22},{18,... | collective-permute-start | bytes 1376264 | tf_op jit(solution)/shard_map/ppermute | solution.py:32
  37.2 10.4 %collective-permute-start.4 = (bf16[4,32,512]{2,1,0:T(8,128)(2,1)S(1)}, bf16[4,32,512]{2,1,0:T(8,128)(2,1)S(1)}, u32[]{:S(2)}, u32[]{:S(2)}) collective-permute-start(bf16[4,32,512]{2,1,0:T(8,128)(2,1)S(1)} %get-tuple-element.28), channel_id=1, source_target_pairs={{0,16},{2,18},{4,20},{6,22},{8,24},{10,26},{12,28},{14,30},{16,0},... | collective-permute-start | bytes 393224 | tf_op jit(solution)/shard_map/ppermute | solution.py:32
  40.0 7.6 %collective-permute-start.5 = (bf16[4,32,512]{2,1,0:T(8,128)(2,1)S(1)}, bf16[4,32,512]{2,1,0:T(8,128)(2,1)S(1)}, u32[]{:S(2)}, u32[]{:S(2)}) collective-permute-start(bf16[4,32,512]{2,1,0:T(8,128)(2,1)S(1)} %get-tuple-element.29), channel_id=1, source_target_pairs={{0,24},{2,26},{4,28},{6,30},{8,16},{10,18},{12,20},{14,22},{16,8},... | collective-permute-start | bytes 393224 | tf_op jit(solution)/shard_map/ppermute | solution.py:32
  47.9 4.7 %collective-permute-start.6 = (f32[8,128]{1,0:T(8,128)S(1)}, f32[8,128]{1,0:T(8,128)S(1)}, u32[]{:S(2)}, u32[]{:S(2)}) collective-permute-start(f32[8,128]{1,0:T(8,128)S(1)} %get-tuple-element.30), channel_id=1, source_target_pairs={{0,8},{2,10},{4,12},{6,14},{8,0},{10,2},{12,4},{14,6},{16,24},{18,... | collective-permute-start | bytes 12296 | tf_op jit(solution)/shard_map/ppermute | solution.py:32
  49.9 4.5 %collective-permute-start.7 = (f32[8,128]{1,0:T(8,128)S(1)}, f32[8,128]{1,0:T(8,128)S(1)}, u32[]{:S(2)}, u32[]{:S(2)}) collective-permute-start(f32[8,128]{1,0:T(8,128)S(1)} %get-tuple-element.30), channel_id=1, source_target_pairs={{0,16},{2,18},{4,20},{6,22},{8,24},{10,26},{12,28},{14,30},{16,0},... | collective-permute-start | bytes 12296 | tf_op jit(solution)/shard_map/ppermute | solution.py:32
  51.1 5.4 %collective-permute-start.8 = (f32[8,128]{1,0:T(8,128)S(1)}, f32[8,128]{1,0:T(8,128)S(1)}, u32[]{:S(2)}, u32[]{:S(2)}) collective-permute-start(f32[8,128]{1,0:T(8,128)S(1)} %get-tuple-element.30), channel_id=1, source_target_pairs={{0,24},{2,26},{4,28},{6,30},{8,16},{10,18},{12,20},{14,22},{16,8},... | collective-permute-start | bytes 12296 | tf_op jit(solution)/shard_map/ppermute | solution.py:32
  52.5 9.8 %collective-permute-start.19 = (bf16[4,32,512]{2,1,0:T(8,128)(2,1)S(1)}, bf16[4,32,512]{2,1,0:T(8,128)(2,1)S(1)}, u32[]{:S(2)}, u32[]{:S(2)}) collective-permute-start(bf16[4,32,512]{2,1,0:T(8,128)(2,1)S(1)} %get-tuple-element.37.refs_2_), channel_id=1, source_target_pairs={{0,2},{2,0},{4,6},{6,4},{8,10},{10,8},{12,14},{14,12},{16,18},{18,... | collective-permute-start | bytes 393224 | tf_op jit(solution)/shard_map/ppermute | solution.py:32
  54.4 8.4 %collective-permute-start.20 = (bf16[4,32,512]{2,1,0:T(8,128)(2,1)S(1)}, bf16[4,32,512]{2,1,0:T(8,128)(2,1)S(1)}, u32[]{:S(2)}, u32[]{:S(2)}) collective-permute-start(bf16[4,32,512]{2,1,0:T(8,128)(2,1)S(1)} %get-tuple-element.37.refs_2_), channel_id=1, source_target_pairs={{0,4},{2,6},{4,0},{6,2},{8,12},{10,14},{12,8},{14,10},{16,20},{18,... | collective-permute-start | bytes 393224 | tf_op jit(solution)/shard_map/ppermute | solution.py:32
  56.5 6.3 %collective-permute-start.21 = (bf16[4,32,512]{2,1,0:T(8,128)(2,1)S(1)}, bf16[4,32,512]{2,1,0:T(8,128)(2,1)S(1)}, u32[]{:S(2)}, u32[]{:S(2)}) collective-permute-start(bf16[4,32,512]{2,1,0:T(8,128)(2,1)S(1)} %get-tuple-element.37.refs_2_), channel_id=1, source_target_pairs={{0,6},{2,4},{4,2},{6,0},{8,14},{10,12},{12,10},{14,8},{16,22},{18,... | collective-permute-start | bytes 393224 | tf_op jit(solution)/shard_map/ppermute | solution.py:32
  59.2 5.8 %collective-permute-start.10 = (f32[8,128]{1,0:T(8,128)S(1)}, f32[8,128]{1,0:T(8,128)S(1)}, u32[]{:S(2)}, u32[]{:S(2)}) collective-permute-start(f32[8,128]{1,0:T(8,128)S(1)} %add.37.refs_0_), channel_id=1, source_target_pairs={{0,2},{2,0},{4,6},{6,4},{8,10},{10,8},{12,14},{14,12},{16,18},{18,... | collective-permute-start | bytes 12296 | tf_op jit(solution)/shard_map/ppermute | solution.py:32
  60.9 4.2 %collective-permute-start.11 = (f32[8,128]{1,0:T(8,128)S(1)}, f32[8,128]{1,0:T(8,128)S(1)}, u32[]{:S(2)}, u32[]{:S(2)}) collective-permute-start(f32[8,128]{1,0:T(8,128)S(1)} %add.37.refs_0_), channel_id=1, source_target_pairs={{0,4},{2,6},{4,0},{6,2},{8,12},{10,14},{12,8},{14,10},{16,20},{18,... | collective-permute-start | bytes 12296 | tf_op jit(solution)/shard_map/ppermute | solution.py:32
  62.3 4.5 %collective-permute-start.12 = (f32[8,128]{1,0:T(8,128)S(1)}, f32[8,128]{1,0:T(8,128)S(1)}, u32[]{:S(2)}, u32[]{:S(2)}) collective-permute-start(f32[8,128]{1,0:T(8,128)S(1)} %add.37.refs_0_), channel_id=1, source_target_pairs={{0,6},{2,4},{4,2},{6,0},{8,14},{10,12},{12,10},{14,8},{16,22},{18,... | collective-permute-start | bytes 12296 | tf_op jit(solution)/shard_map/ppermute | solution.py:32
  69.2 4.7 %collective-permute-start.22 = (bf16[32,1536]{1,0:T(8,128)(2,1)S(1)}, bf16[32,1536]{1,0:T(8,128)(2,1)S(1)}, u32[]{:S(2)}, u32[]{:S(2)}) collective-permute-start(bf16[32,1536]{1,0:T(8,128)(2,1)S(1)} %get-tuple-element.45), channel_id=1, source_target_pairs={{0,8},{2,10},{4,12},{6,14},{8,0},{10,2},{12,4},{14,6},{16,24},{18,... | collective-permute-start | bytes 294920 | tf_op jit(solution)/shard_map/ppermute | solution.py:32
  69.4 9.6 %collective-permute-start.23 = (bf16[32,1536]{1,0:T(8,128)(2,1)S(1)}, bf16[32,1536]{1,0:T(8,128)(2,1)S(1)}, u32[]{:S(2)}, u32[]{:S(2)}) collective-permute-start(bf16[32,1536]{1,0:T(8,128)(2,1)S(1)} %get-tuple-element.46), channel_id=1, source_target_pairs={{0,16},{2,18},{4,20},{6,22},{8,24},{10,26},{12,28},{14,30},{16,0},... | collective-permute-start | bytes 294920 | tf_op jit(solution)/shard_map/ppermute | solution.py:32
  71.2 7.8 %collective-permute-start.24 = (bf16[32,1536]{1,0:T(8,128)(2,1)S(1)}, bf16[32,1536]{1,0:T(8,128)(2,1)S(1)}, u32[]{:S(2)}, u32[]{:S(2)}) collective-permute-start(bf16[32,1536]{1,0:T(8,128)(2,1)S(1)} %get-tuple-element.47), channel_id=1, source_target_pairs={{0,24},{2,26},{4,28},{6,30},{8,16},{10,18},{12,20},{14,22},{16,8},... | collective-permute-start | bytes 294920 | tf_op jit(solution)/shard_map/ppermute | solution.py:32
  (5 other events, 31.2 us)

commit v3 on v2

--- a/solution.py
+++ b/solution.py
@@ -12,7 +12,6 @@
 LEARN_RATE = 0.1
 EPS_NORM = 1e-06
 LANES = 128
-CHUNKS = 1
 VMEM_GRANT = 16 * 2**20
 FLOAT = jnp.float32
 HALF = jnp.bfloat16
@@ -124,14 +123,21 @@
     right_gram[...] = product(conjugate, conjugate, 0, 0)
 
 
-def gather_kernel(plan, where, *refs):
-    terms, outs = refs[: plan.group], refs[plan.group :]
+def relay_kernel(where, low_own, low_seen, high_own, high_seen, low_out, high_out):
+    seen = low_seen[:, :, 1 - where[3]].astype(FLOAT)
+    low_out[...] = (low_own[...].astype(FLOAT) + seen).astype(HALF)
+    seen = high_seen[:, :, 1 - where[2]].astype(FLOAT)
+    high_out[...] = (high_own[...].astype(FLOAT) + seen).astype(HALF)
+
+
+def gather_kernel(where, own, low_seen, low_last, high_seen, high_last, *outs):
+    middle = own.shape[1] // 2
     for k, out in enumerate(outs):
         block = where[0] ^ k
-        total = terms[0][block].astype(FLOAT)
-        for term in terms[1:]:
-            total = total + term[block].astype(FLOAT)
-        out[...] = total.astype(HALF)
+        low = own[block, :middle].astype(FLOAT) + low_seen[block, :, where[3]].astype(FLOAT)
+        out[:middle] = (low + low_last[block].astype(FLOAT)).astype(HALF)
+        high = own[block, middle:].astype(FLOAT) + high_seen[block, :, where[2]].astype(FLOAT)
+        out[middle:] = (high + high_last[block].astype(FLOAT)).astype(HALF)
 
 
 def sum_kernel(blocks, *refs):
@@ -229,25 +235,72 @@
     group, rows = plan.group, plan.rows
     my_block = me // group
     my_place = me % group
-    where = jnp.stack([my_block, my_place]).astype(jnp.int32)
+    my_low, my_high = my_place % 2, my_place // 2
+    where = jnp.stack([my_block, my_place, my_low, my_high]).astype(jnp.int32)
     slot_row = slot_table[0]
     in_tiles = rows % 16 == 0
     limit = CLIP_RMS * math.sqrt(blocks * size * columns * halves)
 
     grads = partial_grads[0].reshape(blocks, blocks, group, rows, columns)
-    step = blocks // CHUNKS
-    later = lax.optimization_barrier(grads)
-    chunks = []
-    for i in range(CHUNKS):
-        cut = [
-            lax.dynamic_slice(
-                grads if i == 0 and k > 0 else later,
-                (0, i * step, my_place ^ k, 0, 0),
-                (blocks, step, 1, rows, columns),
-            ).reshape(blocks, step, rows, columns)
-            for k in range(group)
-        ]
-        chunks.append([cut[0]] + [flip(cut[k], devices, k) for k in range(1, group)])
+    middle = blocks // 2
+    if in_tiles and group == 4:
+
+        def part(array, half, high, low):
+            start = (0, (half or 0) * middle, high, low, 0, 0)
+            extent = (
+                blocks,
+                blocks if half is None else middle,
+                2 if high is None else 1,
+                2 if low is None else 1,
+                rows,
+                columns,
+            )
+            array = array.reshape(blocks, blocks, 2, 2, rows, columns)
+            cut = lax.dynamic_slice(array, [0 if i is None else i for i in start], extent)
+            return cut.reshape([n for i, n in enumerate(extent) if n > 1 or i not in (2, 3)])
+
+        low_seen = flip(part(grads, 0, None, 1 - my_low), devices, 1)
+        high_seen = flip(part(grads, 1, 1 - my_high, None), devices, 2)
+        low_sent, high_sent = call(
+            relay_kernel,
+            (shaped((blocks, middle, rows, columns)),) * 2,
+            [],
+            0,
+            1,
+            where,
+            part(grads, 0, 1 - my_high, my_low),
+            low_seen,
+            part(grads, 1, my_high, 1 - my_low),
+            high_seen,
+        )
+        parts = call(
+            gather_kernel,
+            tuple(shaped((blocks, rows, columns)) for _ in range(blocks)),
+            [],
+            0,
+            1,
+            where,
+            part(grads, None, my_high, my_low),
+            low_seen,
+            flip(low_sent, devices, 2),
+            high_seen,
+            flip(high_sent, devices, 1),
+        )
+    else:
+        halves_of = []
+        masks = [1 << i for i in range(group.bit_length() - 1)]
+        for half, order in enumerate((masks, masks[::-1])):
+            kept = grads[:, half * middle : (half + 1) * middle].astype(FLOAT)
+            kept = kept.reshape(blocks, middle, *[2] * len(masks), rows, columns)
+            left = sorted(masks, reverse=True)
+            for mask in order:
+                axis, bit = 2 + left.index(mask), my_place // mask % 2
+                sent = pick(kept, 1 - bit, axis).astype(HALF)
+                left.remove(mask)
+                kept = pick(kept, bit, axis) + flip(sent, devices, mask)
+            halves_of.append(kept)
+        total = jnp.concatenate(halves_of, axis=1).astype(HALF)
+        parts = [pick(total, my_block ^ k, 0) for k in range(blocks)]
 
     old_state = factors[0]
     if in_tiles:
@@ -262,7 +315,7 @@
             old_state,
             inverse_factors[0],
             probes[0],
-            space=pl.ANY,
+            space=pltpu.HBM,
         )
     else:
         wide = jnp.concatenate([old_state, inverse_factors[0], probes[0]], axis=2)
@@ -281,18 +334,7 @@
     else:
         quarter = unflip(pieces, my_block)
 
-    terms = []
-    for chunk in chunks:
-        mine = call(
-            functools.partial(gather_kernel, plan),
-            tuple(shaped((step, rows, columns)) for _ in range(blocks)),
-            [],
-            0,
-            1,
-            where,
-            *chunk,
-        )
-        terms += [mine[0]] + [flip(mine[k], devices, k * group) for k in range(1, blocks)]
+    terms = [parts[0]] + [flip(parts[k], devices, k * group) for k in range(1, blocks)]
     grad_quarter, squares = call(
         functools.partial(sum_kernel, blocks),
         (shaped((blocks, rows, columns)), shaped((8, LANES), FLOAT)),

time: 80.5 us -> 80.6 us (level)
  starting transfers between devices: 38.9 us -> 34.4 us
  waiting for transfers between devices: 26.3 us -> 28.7 us
  local copies, waits for them, and re-layouts: 3.72 us -> 5.19 us
    ppermute x24 -> x25, starting transfers between devices: 38.9 us -> 34.3 us  [flip(): return lax.ppermute(array, 'dp', [(i, i ^ mask) for i in range(devices)])]
    ppermute x24 -> x25, waiting for transfers between devices: 26.3 us -> 28.7 us  [flip(): return lax.ppermute(array, 'dp', [(i, i ^ mask) for i in range(devices)])]
    reshape x2 -> x4, local copies, waits for them, and re-layouts: 3.7 us -> 5.17 us  [part(): cut.reshape([n for i, n in enumerate(extent) if n > 1 or i not in (2, 3)])]
    pallas_call x8 -> x9, Pallas kernels: 10.5 us -> 11.1 us  [call(): pl.pallas_call(kernel, out_shape=out_shape, in_specs=[SMEM_SPEC] * smem +...]
  transfers between devices with their start and end apart: 25 -> 26, of which waited for: 10 -> 12; matrix products, arithmetic and copies ran while one was open for 1% -> 5% of each run, Pallas kernels for 9% -> 9%
where the time goes in v3:
time: 80.6 us; the launch traced here: 80.3 us
  starting transfers between devices  34.4 us (43%)
  waiting for transfers between devices  28.7 us (36%)
  Pallas kernels  11.1 us (14%)
  local copies, waits for them, and re-layouts  5.19 us (6%)
  between operations  0.89 us (1%)
    ppermute x25, starting transfers between devices, flip(): return lax.ppermute(array, 'dp', [(i, i ^ mask) for i in range(devices)])  34.3 us
    ppermute x25, waiting for transfers between devices, flip(): return lax.ppermute(array, 'dp', [(i, i ^ mask) for i in range(devices)])  28.7 us
    pallas_call x9, Pallas kernels, call(): pl.pallas_call(kernel, out_shape=out_shape, in_specs=[SMEM_SPEC] * smem +...  11.1 us
    reshape x4, local copies, waits for them, and re-layouts, part(): cut.reshape([n for i, n in enumerate(extent) if n > 1 or i not in (2, 3)])  5.17 us
  transfers between devices with their start and end apart: 26, of which 12 were waited for; matrix products, arithmetic and copies ran while one was open for 5% of the time, Pallas kernels for 9%

profile of v3, /device:TPU:0, one launch (start us, length us, event | category | flops | bytes accessed | tf_op | source)
XLA Modules:
  0.0 80.3 jit_solution(9781882567191662189)
XLA Ops:
  1.9 3.0 %collective-permute-start = (bf16[4,2,2,32,512]{4,3,2,1,0:T(8,128)(2,1)S(1)}, bf16[4,2,2,32,512]{4,3,2,1,0:T(8,128)(2,1)S(1)}, u32[]{:S(2)}, u32[]{:S(2)}) collective-permute-start(bf16[4,2,2,32,512]{4,3,2,1,0:T(8,128)(2,1)S(1)} %dynamic-slice_bitcast_fusion.1), channel_id=1, source_target_pairs={{0,2},{2,0},{4,6},{6,4},{8,10},{10,8},{12,14},{14,12},{16,18},{18,... | collective-permute-start | bytes 1572872 | tf_op jit(solution)/shard_map/ppermute | solution.py:31
  4.9 1.9 %dynamic-slice_bitcast_fusion = bf16[4,2,2,32,512]{4,3,2,1,0:T(8,128)(2,1)} fusion(bf16[4,4,2,2,32,512]{5,4,3,2,1,0:T(8,128)(2,1)} %bitcast.38, s32[]{:T(128)S(6)} %select_n.41), kind=kLoop, calls=%fused_computation | loop fusion | bytes 1048580 | tf_op jit(solution)/shard_map/reshape | solution.py:260
  6.8 1.5 %collective-permute-start.1 = (bf16[4,2,2,32,512]{4,3,2,1,0:T(8,128)(2,1)}, bf16[4,2,2,32,512]{4,3,2,1,0:T(8,128)(2,1)S(1)}, u32[]{:S(2)}, u32[]{:S(2)}) collective-permute-start(bf16[4,2,2,32,512]{4,3,2,1,0:T(8,128)(2,1)} %dynamic-slice_bitcast_fusion), channel_id=1, source_target_pairs={{0,4},{2,6},{4,0},{6,2},{8,12},{10,14},{12,8},{14,10},{16,20},{18,... | collective-permute-start | bytes 1572872 | tf_op jit(solution)/shard_map/ppermute | solution.py:31
  9.3 1.6 %collective-permute-start.14 = (bf16[32,2560]{1,0:T(8,128)(2,1)S(1)}, bf16[32,2560]{1,0:T(8,128)(2,1)S(1)}, u32[]{:S(2)}, u32[]{:S(2)}) collective-permute-start(bf16[32,2560]{1,0:T(8,128)(2,1)S(1)} %get-tuple-element.36), channel_id=1, source_target_pairs={{0,8},{2,10},{4,12},{6,14},{8,0},{10,2},{12,4},{14,6},{16,24},{18,... | collective-permute-start | bytes 491528 | tf_op jit(solution)/shard_map/ppermute | solution.py:31
  10.9 2.6 %collective-permute-start.15 = (bf16[32,2560]{1,0:T(8,128)(2,1)S(1)}, bf16[32,2560]{1,0:T(8,128)(2,1)S(1)}, u32[]{:S(2)}, u32[]{:S(2)}) collective-permute-start(bf16[32,2560]{1,0:T(8,128)(2,1)S(1)} %get-tuple-element.37), channel_id=1, source_target_pairs={{0,16},{2,18},{4,20},{6,22},{8,24},{10,26},{12,28},{14,30},{16,0},... | collective-permute-start | bytes 491528 | tf_op jit(solution)/shard_map/ppermute | solution.py:31
  14.8 2.0 %collective-permute-done.low_seen = bf16[4,2,2,32,512]{4,3,2,1,0:T(8,128)(2,1)S(1)} collective-permute-done((bf16[4,2,2,32,512]{4,3,2,1,0:T(8,128)(2,1)S(1)}, bf16[4,2,2,32,512]{4,3,2,1,0:T(8,128)(2,1)S(1)}, u32[]{:S(2)}, u32[]{:S(2)}) %collective-permute-start) | collective-permute-done | bytes 524320 | tf_op jit(solution)/shard_map/ppermute | solution.py:31
  16.8 3.6 %collective-permute-done.1.high_seen = bf16[4,2,2,32,512]{4,3,2,1,0:T(8,128)(2,1)S(1)} collective-permute-done((bf16[4,2,2,32,512]{4,3,2,1,0:T(8,128)(2,1)}, bf16[4,2,2,32,512]{4,3,2,1,0:T(8,128)(2,1)S(1)}, u32[]{:S(2)}, u32[]{:S(2)}) %collective-permute-start.1) | collective-permute-done | bytes 524320 | tf_op jit(solution)/shard_map/ppermute | solution.py:31
  21.0 1.6 %collective-permute-start.2 = (bf16[4,2,32,512]{3,2,1,0:T(8,128)(2,1)S(1)}, bf16[4,2,32,512]{3,2,1,0:T(8,128)(2,1)S(1)}, u32[]{:S(2)}, u32[]{:S(2)}) collective-permute-start(bf16[4,2,32,512]{3,2,1,0:T(8,128)(2,1)S(1)} %get-tuple-element.28), channel_id=1, source_target_pairs={{0,4},{2,6},{4,0},{6,2},{8,12},{10,14},{12,8},{14,10},{16,20},{18,... | collective-permute-start | bytes 786440 | tf_op jit(solution)/shard_map/ppermute | solution.py:31
  23.2 2.6 %collective-permute-done.15.refs_2_ = bf16[32,2560]{1,0:T(8,128)(2,1)S(1)} collective-permute-done((bf16[32,2560]{1,0:T(8,128)(2,1)S(1)}, bf16[32,2560]{1,0:T(8,128)(2,1)S(1)}, u32[]{:S(2)}, u32[]{:S(2)}) %collective-permute-start.15) | collective-permute-done | bytes 163872 | tf_op jit(solution)/shard_map/ppermute | solution.py:31
  28.1 3.7 %collective-permute-done.3.high_last = bf16[4,2,32,512]{3,2,1,0:T(8,128)(2,1)S(1)} collective-permute-done((bf16[4,2,32,512]{3,2,1,0:T(8,128)(2,1)S(1)}, bf16[4,2,32,512]{3,2,1,0:T(8,128)(2,1)S(1)}, u32[]{:S(2)}, u32[]{:S(2)}) %collective-permute-start.3) | collective-permute-done | bytes 262176 | tf_op jit(solution)/shard_map/ppermute | solution.py:31
  34.7 4.0 %collective-permute-start.5 = (bf16[4,32,512]{2,1,0:T(8,128)(2,1)S(1)}, bf16[4,32,512]{2,1,0:T(8,128)(2,1)S(1)}, u32[]{:S(2)}, u32[]{:S(2)}) collective-permute-start(bf16[4,32,512]{2,1,0:T(8,128)(2,1)S(1)} %get-tuple-element.32), channel_id=1, source_target_pairs={{0,16},{2,18},{4,20},{6,22},{8,24},{10,26},{12,28},{14,30},{16,0},... | collective-permute-start | bytes 393224 | tf_op jit(solution)/shard_map/ppermute | solution.py:31
  38.8 1.4 %collective-permute-done.4.refs_1_ = bf16[4,32,512]{2,1,0:T(8,128)(2,1)S(1)} collective-permute-done((bf16[4,32,512]{2,1,0:T(8,128)(2,1)S(1)}, bf16[4,32,512]{2,1,0:T(8,128)(2,1)S(1)}, u32[]{:S(2)}, u32[]{:S(2)}) %collective-permute-start.4) | collective-permute-done | bytes 131104 | tf_op jit(solution)/shard_map/ppermute | solution.py:31
  40.1 3.3 %collective-permute-start.6 = (bf16[4,32,512]{2,1,0:T(8,128)(2,1)S(1)}, bf16[4,32,512]{2,1,0:T(8,128)(2,1)S(1)}, u32[]{:S(2)}, u32[]{:S(2)}) collective-permute-start(bf16[4,32,512]{2,1,0:T(8,128)(2,1)S(1)} %get-tuple-element.33), channel_id=1, source_target_pairs={{0,24},{2,26},{4,28},{6,30},{8,16},{10,18},{12,20},{14,22},{16,8},... | collective-permute-start | bytes 393224 | tf_op jit(solution)/shard_map/ppermute | solution.py:31
  43.4 3.6 %collective-permute-done.6.refs_3_ = bf16[4,32,512]{2,1,0:T(8,128)(2,1)S(1)} collective-permute-done((bf16[4,32,512]{2,1,0:T(8,128)(2,1)S(1)}, bf16[4,32,512]{2,1,0:T(8,128)(2,1)S(1)}, u32[]{:S(2)}, u32[]{:S(2)}) %collective-permute-start.6) | collective-permute-done | bytes 131104 | tf_op jit(solution)/shard_map/ppermute | solution.py:31
  47.3 3.8 %collective-permute-start.8 = (f32[8,128]{1,0:T(8,128)S(1)}, f32[8,128]{1,0:T(8,128)S(1)}, u32[]{:S(2)}, u32[]{:S(2)}) collective-permute-start(f32[8,128]{1,0:T(8,128)S(1)} %get-tuple-element.34), channel_id=1, source_target_pairs={{0,16},{2,18},{4,20},{6,22},{8,24},{10,26},{12,28},{14,30},{16,0},... | collective-permute-start | bytes 12296 | tf_op jit(solution)/shard_map/ppermute | solution.py:31
  53.2 3.4 %collective-permute-done.9 = f32[8,128]{1,0:T(8,128)S(1)} collective-permute-done((f32[8,128]{1,0:T(8,128)S(1)}, f32[8,128]{1,0:T(8,128)S(1)}, u32[]{:S(2)}, u32[]{:S(2)}) %collective-permute-start.9) | collective-permute-done | bytes 4128 | tf_op jit(solution)/shard_map/ppermute | solution.py:31
  56.7 2.1 %shard_map.73 = (bf16[512,512]{1,0:T(8,128)(2,1)S(1)}, bf16[512,512]{1,0:T(8,128)(2,1)S(1)}, f32[512,512]{1,0:T(8,128)S(1)}, f32[512,512]{1,0:T(8,128)S(1)}) custom-call(s32[4]{0:T(128)S(1)} %pad_add_fusion.where, bf16[32,7168]{1,0:T(8,128)(2,1)S(1)} %shard_map.72.refs_0_, bf16[32,7168]{1,0:T(8,128)(2,1)S(1)} %collective-permute-done.17.refs_1_, ...), custom_call_target="tpu_custom_call" | custom-call | flops 1073741824 | bytes 4980752 | tf_op jit(solution)/shard_map/pallas_call | solution.py:45
  58.8 1.9 %collective-permute-start.11 = (f32[8,128]{1,0:T(8,128)S(1)}, f32[8,128]{1,0:T(8,128)S(1)}, u32[]{:S(2)}, u32[]{:S(2)}) collective-permute-start(f32[8,128]{1,0:T(8,128)S(1)} %add.48.refs_0_), channel_id=1, source_target_pairs={{0,2},{2,0},{4,6},{6,4},{8,10},{10,8},{12,14},{14,12},{16,18},{18,... | collective-permute-start | bytes 12296 | tf_op jit(solution)/shard_map/ppermute | solution.py:31
  60.7 1.6 %collective-permute-start.12 = (f32[8,128]{1,0:T(8,128)S(1)}, f32[8,128]{1,0:T(8,128)S(1)}, u32[]{:S(2)}, u32[]{:S(2)}) collective-permute-start(f32[8,128]{1,0:T(8,128)S(1)} %add.48.refs_0_), channel_id=1, source_target_pairs={{0,4},{2,6},{4,0},{6,2},{8,12},{10,14},{12,8},{14,10},{16,20},{18,... | collective-permute-start | bytes 12296 | tf_op jit(solution)/shard_map/ppermute | solution.py:31
  62.4 2.2 %shard_map.74 = (bf16[512,512]{1,0:T(8,128)(2,1)S(1)}, f32[512,512]{1,0:T(8,128)S(1)}, f32[512,512]{1,0:T(8,128)S(1)}, f32[8,128]{1,0:T(8,128)S(1)}) custom-call(s32[4]{0:T(128)S(1)} %pad_add_fusion.where, bf16[512,512]{1,0:T(8,128)(2,1)S(1)} %get-tuple-element.39.refs_0_.refs_5_, bf16[512,512]{1,0:T(8,128)(2,1)S(1)} %get-tuple-element.40.refs_1_.refs_6_, ...), custom_call_target="tpu_custom_call" | custom-call | flops 1073741824 | bytes 4198416 | tf_op jit(solution)/shard_map/pallas_call | solution.py:45
  64.7 2.2 %collective-permute-done.13.refs_3_ = f32[8,128]{1,0:T(8,128)S(1)} collective-permute-done((f32[8,128]{1,0:T(8,128)S(1)}, f32[8,128]{1,0:T(8,128)S(1)}, u32[]{:S(2)}, u32[]{:S(2)}) %collective-permute-start.13) | collective-permute-done | bytes 4128 | tf_op jit(solution)/shard_map/ppermute | solution.py:31
  66.9 2.3 %shard_map.75 = (bf16[32,1536]{1,0:T(8,128)(2,1)S(1)}, bf16[32,1536]{1,0:T(8,128)(2,1)S(1)}, bf16[32,1536]{1,0:T(8,128)(2,1)S(1)}, bf16[32,1536]{1,0:T(8,128)(2,1)S(1)}) custom-call(s32[4]{0:T(128)S(1)} %pad_add_fusion.where, f32[8,128]{1,0:T(8,128)S(1)} %add.48.refs_0_, f32[8,128]{1,0:T(8,128)S(1)} %collective-permute-done.11.refs_1_, ...), custom_call_target="tpu_custom_call" | custom-call | flops 1342177280 | bytes 6180880 | tf_op jit(solution)/shard_map/pallas_call | solution.py:45
  70.4 3.3 %collective-permute-start.25 = (bf16[32,1536]{1,0:T(8,128)(2,1)S(1)}, bf16[32,1536]{1,0:T(8,128)(2,1)S(1)}, u32[]{:S(2)}, u32[]{:S(2)}) collective-permute-start(bf16[32,1536]{1,0:T(8,128)(2,1)S(1)} %get-tuple-element.51), channel_id=1, source_target_pairs={{0,24},{2,26},{4,28},{6,30},{8,16},{10,18},{12,20},{14,22},{16,8},... | collective-permute-start | bytes 294920 | tf_op jit(solution)/shard_map/ppermute | solution.py:31
  73.9 5.1 %collective-permute-done.24.refs_2_ = bf16[32,1536]{1,0:T(8,128)(2,1)S(1)} collective-permute-done((bf16[32,1536]{1,0:T(8,128)(2,1)S(1)}, bf16[32,1536]{1,0:T(8,128)(2,1)S(1)}, u32[]{:S(2)}, u32[]{:S(2)}) %collective-permute-start.24) | collective-permute-done | bytes 98336 | tf_op jit(solution)/shard_map/ppermute | solution.py:31
  (52 shorter events, 15.1 us)
Async XLA Ops:
  1.9 15.0 %collective-permute-start = (bf16[4,2,2,32,512]{4,3,2,1,0:T(8,128)(2,1)S(1)}, bf16[4,2,2,32,512]{4,3,2,1,0:T(8,128)(2,1)S(1)}, u32[]{:S(2)}, u32[]{:S(2)}) collective-permute-start(bf16[4,2,2,32,512]{4,3,2,1,0:T(8,128)(2,1)S(1)} %dynamic-slice_bitcast_fusion.1), channel_id=1, source_target_pairs={{0,2},{2,0},{4,6},{6,4},{8,10},{10,8},{12,14},{14,12},{16,18},{18,... | collective-permute-start | bytes 1572872 | tf_op jit(solution)/shard_map/ppermute | solution.py:31
  6.8 13.6 %collective-permute-start.1 = (bf16[4,2,2,32,512]{4,3,2,1,0:T(8,128)(2,1)}, bf16[4,2,2,32,512]{4,3,2,1,0:T(8,128)(2,1)S(1)}, u32[]{:S(2)}, u32[]{:S(2)}) collective-permute-start(bf16[4,2,2,32,512]{4,3,2,1,0:T(8,128)(2,1)} %dynamic-slice_bitcast_fusion), channel_id=1, source_target_pairs={{0,4},{2,6},{4,0},{6,2},{8,12},{10,14},{12,8},{14,10},{16,20},{18,... | collective-permute-start | bytes 1572872 | tf_op jit(solution)/shard_map/ppermute | solution.py:31
  9.3 13.9 %collective-permute-start.14 = (bf16[32,2560]{1,0:T(8,128)(2,1)S(1)}, bf16[32,2560]{1,0:T(8,128)(2,1)S(1)}, u32[]{:S(2)}, u32[]{:S(2)}) collective-permute-start(bf16[32,2560]{1,0:T(8,128)(2,1)S(1)} %get-tuple-element.36), channel_id=1, source_target_pairs={{0,8},{2,10},{4,12},{6,14},{8,0},{10,2},{12,4},{14,6},{16,24},{18,... | collective-permute-start | bytes 491528 | tf_op jit(solution)/shard_map/ppermute | solution.py:31
  10.9 14.8 %collective-permute-start.15 = (bf16[32,2560]{1,0:T(8,128)(2,1)S(1)}, bf16[32,2560]{1,0:T(8,128)(2,1)S(1)}, u32[]{:S(2)}, u32[]{:S(2)}) collective-permute-start(bf16[32,2560]{1,0:T(8,128)(2,1)S(1)} %get-tuple-element.37), channel_id=1, source_target_pairs={{0,16},{2,18},{4,20},{6,22},{8,24},{10,26},{12,28},{14,30},{16,0},... | collective-permute-start | bytes 491528 | tf_op jit(solution)/shard_map/ppermute | solution.py:31
  13.5 12.2 %collective-permute-start.16 = (bf16[32,2560]{1,0:T(8,128)(2,1)S(1)}, bf16[32,2560]{1,0:T(8,128)(2,1)S(1)}, u32[]{:S(2)}, u32[]{:S(2)}) collective-permute-start(bf16[32,2560]{1,0:T(8,128)(2,1)S(1)} %get-tuple-element.38), channel_id=1, source_target_pairs={{0,24},{2,26},{4,28},{6,30},{8,16},{10,18},{12,20},{14,22},{16,8},... | collective-permute-start | bytes 491528 | tf_op jit(solution)/shard_map/ppermute | solution.py:31
  21.0 7.0 %collective-permute-start.2 = (bf16[4,2,32,512]{3,2,1,0:T(8,128)(2,1)S(1)}, bf16[4,2,32,512]{3,2,1,0:T(8,128)(2,1)S(1)}, u32[]{:S(2)}, u32[]{:S(2)}) collective-permute-start(bf16[4,2,32,512]{3,2,1,0:T(8,128)(2,1)S(1)} %get-tuple-element.28), channel_id=1, source_target_pairs={{0,4},{2,6},{4,0},{6,2},{8,12},{10,14},{12,8},{14,10},{16,20},{18,... | collective-permute-start | bytes 786440 | tf_op jit(solution)/shard_map/ppermute | solution.py:31
  22.6 9.2 %collective-permute-start.3 = (bf16[4,2,32,512]{3,2,1,0:T(8,128)(2,1)S(1)}, bf16[4,2,32,512]{3,2,1,0:T(8,128)(2,1)S(1)}, u32[]{:S(2)}, u32[]{:S(2)}) collective-permute-start(bf16[4,2,32,512]{3,2,1,0:T(8,128)(2,1)S(1)} %get-tuple-element.29), channel_id=1, source_target_pairs={{0,2},{2,0},{4,6},{6,4},{8,10},{10,8},{12,14},{14,12},{16,18},{18,... | collective-permute-start | bytes 786440 | tf_op jit(solution)/shard_map/ppermute | solution.py:31
  26.4 24.8 %collective-permute-start.17 = (bf16[32,7168]{1,0:T(8,128)(2,1)S(1)}, bf16[32,7168]{1,0:T(8,128)(2,1)S(1)}, u32[]{:S(2)}, u32[]{:S(2)}) collective-permute-start(bf16[32,7168]{1,0:T(8,128)(2,1)S(1)} %shard_map.72.refs_0_), channel_id=1, source_target_pairs={{0,2},{2,0},{4,6},{6,4},{8,10},{10,8},{12,14},{14,12},{16,18},{18,... | collective-permute-start | bytes 1376264 | tf_op jit(solution)/shard_map/ppermute | solution.py:31
  32.5 7.6 %collective-permute-start.4 = (bf16[4,32,512]{2,1,0:T(8,128)(2,1)S(1)}, bf16[4,32,512]{2,1,0:T(8,128)(2,1)S(1)}, u32[]{:S(2)}, u32[]{:S(2)}) collective-permute-start(bf16[4,32,512]{2,1,0:T(8,128)(2,1)S(1)} %get-tuple-element.31), channel_id=1, source_target_pairs={{0,8},{2,10},{4,12},{6,14},{8,0},{10,2},{12,4},{14,6},{16,24},{18,... | collective-permute-start | bytes 393224 | tf_op jit(solution)/shard_map/ppermute | solution.py:31
  32.7 23.8 %collective-permute-start.18 = (bf16[32,7168]{1,0:T(8,128)(2,1)S(1)}, bf16[32,7168]{1,0:T(8,128)(2,1)S(1)}, u32[]{:S(2)}, u32[]{:S(2)}) collective-permute-start(bf16[32,7168]{1,0:T(8,128)(2,1)S(1)} %shard_map.72.refs_0_), channel_id=1, source_target_pairs={{0,4},{2,6},{4,0},{6,2},{8,12},{10,14},{12,8},{14,10},{16,20},{18,... | collective-permute-start | bytes 1376264 | tf_op jit(solution)/shard_map/ppermute | solution.py:31
  33.5 23.1 %collective-permute-start.19 = (bf16[32,7168]{1,0:T(8,128)(2,1)S(1)}, bf16[32,7168]{1,0:T(8,128)(2,1)S(1)}, u32[]{:S(2)}, u32[]{:S(2)}) collective-permute-start(bf16[32,7168]{1,0:T(8,128)(2,1)S(1)} %shard_map.72.refs_0_), channel_id=1, source_target_pairs={{0,6},{2,4},{4,2},{6,0},{8,14},{10,12},{12,10},{14,8},{16,22},{18,... | collective-permute-start | bytes 1376264 | tf_op jit(solution)/shard_map/ppermute | solution.py:31
  34.7 8.7 %collective-permute-start.5 = (bf16[4,32,512]{2,1,0:T(8,128)(2,1)S(1)}, bf16[4,32,512]{2,1,0:T(8,128)(2,1)S(1)}, u32[]{:S(2)}, u32[]{:S(2)}) collective-permute-start(bf16[4,32,512]{2,1,0:T(8,128)(2,1)S(1)} %get-tuple-element.32), channel_id=1, source_target_pairs={{0,16},{2,18},{4,20},{6,22},{8,24},{10,26},{12,28},{14,30},{16,0},... | collective-permute-start | bytes 393224 | tf_op jit(solution)/shard_map/ppermute | solution.py:31
  40.1 6.9 %collective-permute-start.6 = (bf16[4,32,512]{2,1,0:T(8,128)(2,1)S(1)}, bf16[4,32,512]{2,1,0:T(8,128)(2,1)S(1)}, u32[]{:S(2)}, u32[]{:S(2)}) collective-permute-start(bf16[4,32,512]{2,1,0:T(8,128)(2,1)S(1)} %get-tuple-element.33), channel_id=1, source_target_pairs={{0,24},{2,26},{4,28},{6,30},{8,16},{10,18},{12,20},{14,22},{16,8},... | collective-permute-start | bytes 393224 | tf_op jit(solution)/shard_map/ppermute | solution.py:31
  47.2 4.5 %collective-permute-start.7 = (f32[8,128]{1,0:T(8,128)S(1)}, f32[8,128]{1,0:T(8,128)S(1)}, u32[]{:S(2)}, u32[]{:S(2)}) collective-permute-start(f32[8,128]{1,0:T(8,128)S(1)} %get-tuple-element.34), channel_id=1, source_target_pairs={{0,8},{2,10},{4,12},{6,14},{8,0},{10,2},{12,4},{14,6},{16,24},{18,... | collective-permute-start | bytes 12296 | tf_op jit(solution)/shard_map/ppermute | solution.py:31
  47.3 5.4 %collective-permute-start.8 = (f32[8,128]{1,0:T(8,128)S(1)}, f32[8,128]{1,0:T(8,128)S(1)}, u32[]{:S(2)}, u32[]{:S(2)}) collective-permute-start(f32[8,128]{1,0:T(8,128)S(1)} %get-tuple-element.34), channel_id=1, source_target_pairs={{0,16},{2,18},{4,20},{6,22},{8,24},{10,26},{12,28},{14,30},{16,0},... | collective-permute-start | bytes 12296 | tf_op jit(solution)/shard_map/ppermute | solution.py:31
  51.2 5.4 %collective-permute-start.9 = (f32[8,128]{1,0:T(8,128)S(1)}, f32[8,128]{1,0:T(8,128)S(1)}, u32[]{:S(2)}, u32[]{:S(2)}) collective-permute-start(f32[8,128]{1,0:T(8,128)S(1)} %get-tuple-element.34), channel_id=1, source_target_pairs={{0,24},{2,26},{4,28},{6,30},{8,16},{10,18},{12,20},{14,22},{16,8},... | collective-permute-start | bytes 12296 | tf_op jit(solution)/shard_map/ppermute | solution.py:31
  51.7 10.6 %collective-permute-start.20 = (bf16[4,32,512]{2,1,0:T(8,128)(2,1)S(1)}, bf16[4,32,512]{2,1,0:T(8,128)(2,1)S(1)}, u32[]{:S(2)}, u32[]{:S(2)}) collective-permute-start(bf16[4,32,512]{2,1,0:T(8,128)(2,1)S(1)} %get-tuple-element.41.refs_2_), channel_id=1, source_target_pairs={{0,2},{2,0},{4,6},{6,4},{8,10},{10,8},{12,14},{14,12},{16,18},{18,... | collective-permute-start | bytes 393224 | tf_op jit(solution)/shard_map/ppermute | solution.py:31
  52.7 9.6 %collective-permute-start.21 = (bf16[4,32,512]{2,1,0:T(8,128)(2,1)S(1)}, bf16[4,32,512]{2,1,0:T(8,128)(2,1)S(1)}, u32[]{:S(2)}, u32[]{:S(2)}) collective-permute-start(bf16[4,32,512]{2,1,0:T(8,128)(2,1)S(1)} %get-tuple-element.41.refs_2_), channel_id=1, source_target_pairs={{0,4},{2,6},{4,0},{6,2},{8,12},{10,14},{12,8},{14,10},{16,20},{18,... | collective-permute-start | bytes 393224 | tf_op jit(solution)/shard_map/ppermute | solution.py:31
  56.6 5.9 %collective-permute-start.22 = (bf16[4,32,512]{2,1,0:T(8,128)(2,1)S(1)}, bf16[4,32,512]{2,1,0:T(8,128)(2,1)S(1)}, u32[]{:S(2)}, u32[]{:S(2)}) collective-permute-start(bf16[4,32,512]{2,1,0:T(8,128)(2,1)S(1)} %get-tuple-element.41.refs_2_), channel_id=1, source_target_pairs={{0,6},{2,4},{4,2},{6,0},{8,14},{10,12},{12,10},{14,8},{16,22},{18,... | collective-permute-start | bytes 393224 | tf_op jit(solution)/shard_map/ppermute | solution.py:31
  58.8 5.8 %collective-permute-start.11 = (f32[8,128]{1,0:T(8,128)S(1)}, f32[8,128]{1,0:T(8,128)S(1)}, u32[]{:S(2)}, u32[]{:S(2)}) collective-permute-start(f32[8,128]{1,0:T(8,128)S(1)} %add.48.refs_0_), channel_id=1, source_target_pairs={{0,2},{2,0},{4,6},{6,4},{8,10},{10,8},{12,14},{14,12},{16,18},{18,... | collective-permute-start | bytes 12296 | tf_op jit(solution)/shard_map/ppermute | solution.py:31
  62.3 4.5 %collective-permute-start.13 = (f32[8,128]{1,0:T(8,128)S(1)}, f32[8,128]{1,0:T(8,128)S(1)}, u32[]{:S(2)}, u32[]{:S(2)}) collective-permute-start(f32[8,128]{1,0:T(8,128)S(1)} %add.48.refs_0_), channel_id=1, source_target_pairs={{0,6},{2,4},{4,2},{6,0},{8,14},{10,12},{12,10},{14,8},{16,22},{18,... | collective-permute-start | bytes 12296 | tf_op jit(solution)/shard_map/ppermute | solution.py:31
  69.2 4.7 %collective-permute-start.23 = (bf16[32,1536]{1,0:T(8,128)(2,1)S(1)}, bf16[32,1536]{1,0:T(8,128)(2,1)S(1)}, u32[]{:S(2)}, u32[]{:S(2)}) collective-permute-start(bf16[32,1536]{1,0:T(8,128)(2,1)S(1)} %get-tuple-element.49), channel_id=1, source_target_pairs={{0,8},{2,10},{4,12},{6,14},{8,0},{10,2},{12,4},{14,6},{16,24},{18,... | collective-permute-start | bytes 294920 | tf_op jit(solution)/shard_map/ppermute | solution.py:31
  69.3 9.7 %collective-permute-start.24 = (bf16[32,1536]{1,0:T(8,128)(2,1)S(1)}, bf16[32,1536]{1,0:T(8,128)(2,1)S(1)}, u32[]{:S(2)}, u32[]{:S(2)}) collective-permute-start(bf16[32,1536]{1,0:T(8,128)(2,1)S(1)} %get-tuple-element.50), channel_id=1, source_target_pairs={{0,16},{2,18},{4,20},{6,22},{8,24},{10,26},{12,28},{14,30},{16,0},... | collective-permute-start | bytes 294920 | tf_op jit(solution)/shard_map/ppermute | solution.py:31
  70.4 8.6 %collective-permute-start.25 = (bf16[32,1536]{1,0:T(8,128)(2,1)S(1)}, bf16[32,1536]{1,0:T(8,128)(2,1)S(1)}, u32[]{:S(2)}, u32[]{:S(2)}) collective-permute-start(bf16[32,1536]{1,0:T(8,128)(2,1)S(1)} %get-tuple-element.51), channel_id=1, source_target_pairs={{0,24},{2,26},{4,28},{6,30},{8,16},{10,18},{12,20},{14,22},{16,8},... | collective-permute-start | bytes 294920 | tf_op jit(solution)/shard_map/ppermute | solution.py:31
  (6 other events, 37.1 us)

commit v4 on v3

--- a/solution.py
+++ b/solution.py
@@ -68,6 +68,10 @@
                 yield z, what, first, offset
                 offset += self.size - first
 
+    def split(self):
+        half = self.packed() // 2
+        return min((offset for _, _, _, offset in self.spots()), key=lambda x: abs(x - half))
+
     def packed(self):
         return sum(self.size - first for _, _, first, _ in self.spots())
 
@@ -103,19 +107,21 @@
     size, rows = plan.size, plan.rows
     for z in range(1, plan.blocks):
         for target in targets[:4]:
-            if target is not None and plan.first[z]:
+            if plan.first[z]:
                 span = size // plan.blocks
                 target[z * span : (z + 1) * span, : plan.first[z]] = jnp.zeros((span, plan.first[z]), HALF)
-    for k, piece in enumerate(pieces):
+    for k in range(plan.group):
         for z, what, first, offset in plan.spots():
-            if targets[what] is not None:
-                row = pl.multiple_of((z * plan.group + (where[1] ^ k)) * rows, rows)
-                targets[what][pl.ds(row, rows), first:] = piece[:, offset : offset + size - first]
+            piece, start = pieces[k], offset
+            if len(pieces) > plan.group and k == plan.group - 1 and offset >= plan.split():
+                piece, start = pieces[k + 1], offset - plan.split()
+            row = pl.multiple_of((z * plan.group + (where[1] ^ k)) * rows, rows)
+            targets[what][pl.ds(row, rows), first:] = piece[:, start : start + size - first]
 
 
 def probe_kernel(plan, where, *refs):
-    pieces = refs[: plan.group]
-    left, right, left_gram, right_gram, left_inv, right_inv, probe = refs[plan.group :]
+    pieces = refs[:-7]
+    left, right, left_gram, right_gram, left_inv, right_inv, probe = refs[-7:]
     spread(plan, where, pieces, (left, right, left_inv, right_inv, probe))
     half_conjugate = product(left_inv[...], probe[...], 0, 0).astype(HALF)
     conjugate = product(half_conjugate, right_inv[...]).astype(HALF)
@@ -123,21 +129,24 @@
     right_gram[...] = product(conjugate, conjugate, 0, 0)
 
 
-def relay_kernel(where, low_own, low_seen, high_own, high_seen, low_out, high_out):
-    seen = low_seen[:, :, 1 - where[3]].astype(FLOAT)
-    low_out[...] = (low_own[...].astype(FLOAT) + seen).astype(HALF)
-    seen = high_seen[:, :, 1 - where[2]].astype(FLOAT)
-    high_out[...] = (high_own[...].astype(FLOAT) + seen).astype(HALF)
-
-
-def gather_kernel(where, own, low_seen, low_last, high_seen, high_last, *outs):
+def relay_kernel(where, own, low_own, low_seen, high_own, high_seen, kept, low_out, high_out):
     middle = own.shape[1] // 2
+
+    def add(mine, seen):
+        return mine.astype(FLOAT) + seen.astype(FLOAT)
+
+    kept[:, :middle] = add(own[:, :middle], low_seen[:, :, where[3]])
+    kept[:, middle:] = add(own[:, middle:], high_seen[:, :, where[2]])
+    low_out[...] = add(low_own[...], low_seen[:, :, 1 - where[3]]).astype(HALF)
+    high_out[...] = add(high_own[...], high_seen[:, :, 1 - where[2]]).astype(HALF)
+
+
+def gather_kernel(where, kept, low_last, high_last, *outs):
+    middle = kept.shape[1] // 2
     for k, out in enumerate(outs):
         block = where[0] ^ k
-        low = own[block, :middle].astype(FLOAT) + low_seen[block, :, where[3]].astype(FLOAT)
-        out[:middle] = (low + low_last[block].astype(FLOAT)).astype(HALF)
-        high = own[block, middle:].astype(FLOAT) + high_seen[block, :, where[2]].astype(FLOAT)
-        out[middle:] = (high + high_last[block].astype(FLOAT)).astype(HALF)
+        out[:middle] = (kept[block, :middle] + low_last[block].astype(FLOAT)).astype(HALF)
+        out[middle:] = (kept[block, middle:] + high_last[block].astype(FLOAT)).astype(HALF)
 
 
 def sum_kernel(blocks, *refs):
@@ -183,42 +192,43 @@
     return (factor.astype(FLOAT) - LEARN_RATE / bound_value * moved_rows).astype(HALF)
 
 
-def finish_kernel(plan, limit, where, *refs):
-    sums, refs = refs[: plan.group], refs[plan.group :]
-    own_clip, left, right, grad, left_p, right_p, left_q, right_q = refs[:8]
-    outs, (new_left, new_right, square, result) = refs[8:-4], refs[-4:]
-    squares = sums[0][0:1, 0:1]
-    for ref in sums[1:]:
-        squares = squares + ref[0:1, 0:1]
-    clip = bound_of(limit, squares)
-    ratio = clip / own_clip[0:1, 0:1]
+def clip_of(limit, squares):
+    return bound_of(limit, squares[0:1, 0:1])
+
+
+def factor_kernel(plan, limit, where, *refs):
+    squares, own_clip, left, right, left_p, right_p, left_q, right_q = refs[:8]
+    new_left, new_right, outs = refs[8], refs[9], refs[10:]
+    ratio = clip_of(limit, squares) / own_clip[0:1, 0:1]
     ratio = ratio * ratio
     size, rows = plan.size, plan.rows
     new_left[...] = step_factor(left[...], ratio, left_p, left_q)
     new_right[...] = step_factor(right[...], ratio, right_p, right_q)
+    for k, out in enumerate(outs):
+        row = pl.multiple_of(((where[0] ^ k) * plan.group + where[1]) * rows, rows)
+        out[:, :size] = new_left[pl.ds(row, rows), :]
+        out[:, size:] = new_right[pl.ds(row, rows), :]
+
+
+def result_kernel(plan, limit, where, squares, new_left, new_right, grad, *refs):
+    outs, (square, result) = refs[:-2], refs[-2:]
+    size, rows = plan.size, plan.rows
     square[...] = product(new_left[...], new_left[...], 0, 0).astype(HALF)
     precond_right = product(new_right[...], new_right[...], 0, 0).astype(HALF)
-
-    def at(z):
-        return pl.ds(pl.multiple_of((z * plan.group + where[1]) * rows, rows), rows)
-
-    precond_left = jnp.concatenate([square[at(z), :] for z in range(plan.blocks)], axis=0)
-    middle = (clip * product(precond_left, grad[...])).astype(HALF)
+    starts = [pl.multiple_of((z * plan.group + where[1]) * rows, rows) for z in range(plan.blocks)]
+    precond_left = jnp.concatenate([square[pl.ds(row, rows), :] for row in starts], axis=0)
+    middle = (clip_of(limit, squares) * product(precond_left, grad[...])).astype(HALF)
     result[...] = product(middle, precond_right).astype(HALF).reshape(plan.blocks, rows, size)
     for k, out in enumerate(outs):
-        z = where[0] ^ k
-        out[:, :size] = new_left[at(z), :]
-        out[:, size : 2 * size] = new_right[at(z), :]
-        out[:, 2 * size :] = result[z]
+        out[...] = result[where[0] ^ k]
 
 
 def place_kernel(plan, where, slots, old_state, *refs):
-    pieces, (precond, new_state) = refs[: plan.blocks], refs[plan.blocks :]
-    size = plan.size
+    pieces, (precond, new_state) = refs[:-2], refs[-2:]
     new_state[...] = old_state[...]
-    for k, piece in enumerate(pieces):
-        precond[where[0] ^ k] = piece[:, 2 * size :]
-        new_state[slots[where[0] ^ k]] = piece[:, : 2 * size]
+    for k in range(plan.blocks):
+        new_state[slots[where[0] ^ k]] = pieces[k][...]
+        precond[where[0] ^ k] = pieces[plan.blocks + k][...]
 
 
 def shaped(shape, dtype=HALF):
@@ -261,13 +271,15 @@
 
         low_seen = flip(part(grads, 0, None, 1 - my_low), devices, 1)
         high_seen = flip(part(grads, 1, 1 - my_high, None), devices, 2)
-        low_sent, high_sent = call(
+        kept, low_sent, high_sent = call(
             relay_kernel,
-            (shaped((blocks, middle, rows, columns)),) * 2,
+            (shaped((blocks, blocks, rows, columns), FLOAT),)
+            + (shaped((blocks, middle, rows, columns)),) * 2,
             [],
             0,
             1,
             where,
+            part(grads, None, my_high, my_low),
             part(grads, 0, 1 - my_high, my_low),
             low_seen,
             part(grads, 1, my_high, 1 - my_low),
@@ -280,10 +292,8 @@
             0,
             1,
             where,
-            part(grads, None, my_high, my_low),
-            low_seen,
+            kept,
             flip(low_sent, devices, 2),
-            high_seen,
             flip(high_sent, devices, 1),
         )
     else:
@@ -344,7 +354,12 @@
         *terms,
     )
 
-    states = [quarter] + [flip(quarter, devices, k) for k in range(1, group)]
+    if in_tiles and group == 4:
+        states = [quarter] + [flip(quarter, devices, k) for k in (1, 2)]
+        cut = states[1][:, : plan.split()], states[2][:, plan.split() :]
+        states += [flip(cut[i], devices, 2 - i) for i in range(2)]
+    else:
+        states = [quarter] + [flip(quarter, devices, k) for k in range(1, group)]
     quarters = [grad_quarter] + [flip(grad_quarter, devices, k) for k in range(1, group)]
 
     squares = functools.reduce(
@@ -356,7 +371,10 @@
         other = lax.ppermute(squares, "mp", [(i, i ^ bit) for i in range(halves)])
         squares = squares + other
         bit *= 2
-    sums = [squares] + [flip(squares, devices, k) for k in range(1, group)]
+    bit = 1
+    while bit < group:
+        squares = squares + flip(squares, devices, bit)
+        bit *= 2
 
     gram = shaped((size, size), FLOAT)
     square = shaped((size, size))
@@ -382,26 +400,38 @@
             right_q,
             *quarters,
         )
-        back = call(
-            functools.partial(finish_kernel, plan, limit),
-            tuple(shaped((rows, 2 * size + columns)) for _ in range(blocks)),
-            [pltpu.VMEM((size, size), HALF)] * 3 + [pltpu.VMEM((blocks, rows, columns), HALF)],
-            5 * matmul,
-            1,
-            where,
-            *sums,
+        new_left, new_right, *back = call(
+            functools.partial(factor_kernel, plan, limit),
+            (square, square) + tuple(shaped((rows, 2 * size)) for _ in range(blocks)),
+            [],
+            2 * matmul,
+            1,
+            where,
+            squares,
             own_clip,
             left_q,
             right_q,
-            gradient,
             left_w,
             right_w,
             left_c,
             right_c,
         )
+        last = call(
+            functools.partial(result_kernel, plan, limit),
+            tuple(shaped((rows, columns)) for _ in range(blocks)),
+            [pltpu.VMEM((size, size), HALF), pltpu.VMEM((blocks, rows, columns), HALF)],
+            3 * matmul,
+            1,
+            where,
+            squares,
+            new_left,
+            new_right,
+            gradient,
+        )
     else:
-        back = plain_block(plan, limit, my_block, my_place, sums, states, quarters)
+        back, last = plain_block(plan, limit, my_block, my_place, squares, states, quarters)
     back = [back[0]] + [flip(back[k], devices, k * group) for k in range(1, blocks)]
+    last = [last[0]] + [flip(last[k], devices, k * group) for k in range(1, blocks)]
     precond, new_state = call(
         functools.partial(place_kernel, plan),
         (shaped((blocks, rows, columns)), shaped(old_state.shape)),
@@ -412,15 +442,16 @@
         slot_row,
         old_state,
         *back,
+        *last,
     )
     return (precond.reshape(experts, block_rows, rows, columns), new_state[None])
 
 
-def plain_block(plan, limit, my_block, my_place, sums, states, quarters):
+def plain_block(plan, limit, my_block, my_place, squares, states, quarters):
     size, blocks, group, rows = plan.size, plan.blocks, plan.group, plan.rows
     state = unflip(states, my_place).transpose(1, 0, 2, 3).reshape(size, 5 * size)
     gradient = unflip(quarters, my_place).transpose(1, 0, 2, 3).reshape(size, -1)
-    clip = bound_of(limit, functools.reduce(jnp.add, sums)[0:1, 0:1])
+    clip = clip_of(limit, squares)
     left_q, right_q, left_inv, right_inv, probe_mat = jnp.split(state, 5, axis=1)
     half_conjugate = product(left_inv, probe_mat, 0, 0).astype(HALF)
     conjugate = product(half_conjugate, right_inv).astype(HALF)
@@ -440,8 +471,9 @@
 
     middle = (clip * product(my_rows(precond_left).reshape(blocks * rows, size), gradient)).astype(HALF)
     result = product(middle, precond_right).astype(HALF).reshape(blocks, rows, -1)
-    back = jnp.concatenate([my_rows(new_left), my_rows(new_right), result], axis=2)
-    return [pick(back, my_block ^ k, 0) for k in range(blocks)]
+    back = jnp.concatenate([my_rows(new_left), my_rows(new_right)], axis=2)
+    order = [my_block ^ k for k in range(blocks)]
+    return [pick(back, b, 0) for b in order], [pick(result, b, 0) for b in order]
 
 
 def solution(mesh):

time: 80.6 us -> 95.6 us (1.19)
  waiting for transfers between devices: 28.7 us -> 37.1 us
  starting transfers between devices: 34.4 us -> 40.3 us
    ppermute x25 -> x28, waiting for transfers between devices: 28.7 us -> 35.9 us  [flip(): return lax.ppermute(array, 'dp', [(i, i ^ mask) for i in range(devices)])]
    ppermute x25 -> x28, starting transfers between devices: 34.3 us -> 40.3 us  [flip(): return lax.ppermute(array, 'dp', [(i, i ^ mask) for i in range(devices)])]
    ppermute x1, waiting for transfers between devices: 0.01 us -> 1.16 us  [body(): other = lax.ppermute(squares, 'mp', [(i, i ^ bit) for i in range(halves)])]
    pallas_call x9 -> x10, Pallas kernels: 11.1 us -> 11.8 us  [call(): pl.pallas_call(kernel, out_shape=out_shape, in_specs=[SMEM_SPEC] * smem +...]
  transfers between devices with their start and end apart: 26 -> 29, of which waited for: 12 -> 12; matrix products, arithmetic and copies ran while one was open for 5% -> 4% of each run, Pallas kernels for 9% -> 6%
where the time goes in v4:
time: 95.6 us; the launch traced here: 95.3 us
  starting transfers between devices  40.3 us (42%)
  waiting for transfers between devices  37.1 us (39%)
  Pallas kernels  11.8 us (12%)
  local copies, waits for them, and re-layouts  5.23 us (5%)
    ppermute x28, starting transfers between devices, flip(): return lax.ppermute(array, 'dp', [(i, i ^ mask) for i in range(devices)])  40.3 us
    ppermute x28, waiting for transfers between devices, flip(): return lax.ppermute(array, 'dp', [(i, i ^ mask) for i in range(devices)])  35.9 us
    pallas_call x10, Pallas kernels, call(): pl.pallas_call(kernel, out_shape=out_shape, in_specs=[SMEM_SPEC] * smem +...  11.8 us
    reshape x4, local copies, waits for them, and re-layouts, part(): cut.reshape([n for i, n in enumerate(extent) if n > 1 or i not in (2, 3)])  5.18 us
  transfers between devices with their start and end apart: 29, of which 12 were waited for; matrix products, arithmetic and copies ran while one was open for 4% of the time, Pallas kernels for 6%

profile of v4, /device:TPU:0, one launch (start us, length us, event | category | flops | bytes accessed | tf_op | source)
XLA Modules:
  0.0 95.3 jit_solution(13381328817877801898)
XLA Ops:
  1.9 3.0 %collective-permute-start = (bf16[4,2,2,32,512]{4,3,2,1,0:T(8,128)(2,1)S(1)}, bf16[4,2,2,32,512]{4,3,2,1,0:T(8,128)(2,1)S(1)}, u32[]{:S(2)}, u32[]{:S(2)}) collective-permute-start(bf16[4,2,2,32,512]{4,3,2,1,0:T(8,128)(2,1)S(1)} %dynamic-slice_bitcast_fusion.1), channel_id=1, source_target_pairs={{0,2},{2,0},{4,6},{6,4},{8,10},{10,8},{12,14},{14,12},{16,18},{18,... | collective-permute-start | bytes 1572872 | tf_op jit(solution)/shard_map/ppermute | solution.py:31
  4.9 1.9 %dynamic-slice_bitcast_fusion = bf16[4,2,2,32,512]{4,3,2,1,0:T(8,128)(2,1)} fusion(bf16[4,4,2,2,32,512]{5,4,3,2,1,0:T(8,128)(2,1)} %bitcast.38, s32[]{:T(128)S(6)} %select_n.40), kind=kLoop, calls=%fused_computation | loop fusion | bytes 1048580 | tf_op jit(solution)/shard_map/reshape | solution.py:270
  6.8 1.5 %collective-permute-start.1 = (bf16[4,2,2,32,512]{4,3,2,1,0:T(8,128)(2,1)}, bf16[4,2,2,32,512]{4,3,2,1,0:T(8,128)(2,1)S(1)}, u32[]{:S(2)}, u32[]{:S(2)}) collective-permute-start(bf16[4,2,2,32,512]{4,3,2,1,0:T(8,128)(2,1)} %dynamic-slice_bitcast_fusion), channel_id=1, source_target_pairs={{0,4},{2,6},{4,0},{6,2},{8,12},{10,14},{12,8},{14,10},{16,20},{18,... | collective-permute-start | bytes 1572872 | tf_op jit(solution)/shard_map/ppermute | solution.py:31
  9.3 1.6 %collective-permute-start.13 = (bf16[32,2560]{1,0:T(8,128)(2,1)S(1)}, bf16[32,2560]{1,0:T(8,128)(2,1)S(1)}, u32[]{:S(2)}, u32[]{:S(2)}) collective-permute-start(bf16[32,2560]{1,0:T(8,128)(2,1)S(1)} %get-tuple-element.44), channel_id=1, source_target_pairs={{0,8},{2,10},{4,12},{6,14},{8,0},{10,2},{12,4},{14,6},{16,24},{18,... | collective-permute-start | bytes 491528 | tf_op jit(solution)/shard_map/ppermute | solution.py:31
  10.9 2.6 %collective-permute-start.14 = (bf16[32,2560]{1,0:T(8,128)(2,1)S(1)}, bf16[32,2560]{1,0:T(8,128)(2,1)S(1)}, u32[]{:S(2)}, u32[]{:S(2)}) collective-permute-start(bf16[32,2560]{1,0:T(8,128)(2,1)S(1)} %get-tuple-element.45), channel_id=1, source_target_pairs={{0,16},{2,18},{4,20},{6,22},{8,24},{10,26},{12,28},{14,30},{16,0},... | collective-permute-start | bytes 491528 | tf_op jit(solution)/shard_map/ppermute | solution.py:31
  14.8 2.0 %collective-permute-done.13.refs_1_ = bf16[32,2560]{1,0:T(8,128)(2,1)S(1)} collective-permute-done((bf16[32,2560]{1,0:T(8,128)(2,1)S(1)}, bf16[32,2560]{1,0:T(8,128)(2,1)S(1)}, u32[]{:S(2)}, u32[]{:S(2)}) %collective-permute-start.13) | collective-permute-done | bytes 163872 | tf_op jit(solution)/shard_map/ppermute | solution.py:31
  16.9 8.9 %collective-permute-done.14.refs_2_ = bf16[32,2560]{1,0:T(8,128)(2,1)S(1)} collective-permute-done((bf16[32,2560]{1,0:T(8,128)(2,1)S(1)}, bf16[32,2560]{1,0:T(8,128)(2,1)S(1)}, u32[]{:S(2)}, u32[]{:S(2)}) %collective-permute-start.14) | collective-permute-done | bytes 163872 | tf_op jit(solution)/shard_map/ppermute | solution.py:31
  29.4 1.6 %collective-permute-start.2 = (bf16[4,2,32,512]{3,2,1,0:T(8,128)(2,1)S(1)}, bf16[4,2,32,512]{3,2,1,0:T(8,128)(2,1)S(1)}, u32[]{:S(2)}, u32[]{:S(2)}) collective-permute-start(bf16[4,2,32,512]{3,2,1,0:T(8,128)(2,1)S(1)} %get-tuple-element.36), channel_id=1, source_target_pairs={{0,4},{2,6},{4,0},{6,2},{8,12},{10,14},{12,8},{14,10},{16,20},{18,... | collective-permute-start | bytes 786440 | tf_op jit(solution)/shard_map/ppermute | solution.py:31
  31.0 1.5 %collective-permute-start.3 = (bf16[4,2,32,512]{3,2,1,0:T(8,128)(2,1)S(1)}, bf16[4,2,32,512]{3,2,1,0:T(8,128)(2,1)S(1)}, u32[]{:S(2)}, u32[]{:S(2)}) collective-permute-start(bf16[4,2,32,512]{3,2,1,0:T(8,128)(2,1)S(1)} %get-tuple-element.37), channel_id=1, source_target_pairs={{0,2},{2,0},{4,6},{6,4},{8,10},{10,8},{12,14},{14,12},{16,18},{18,... | collective-permute-start | bytes 786440 | tf_op jit(solution)/shard_map/ppermute | solution.py:31
  32.5 8.5 %collective-permute-done.2.low_last = bf16[4,2,32,512]{3,2,1,0:T(8,128)(2,1)S(1)} collective-permute-done((bf16[4,2,32,512]{3,2,1,0:T(8,128)(2,1)S(1)}, bf16[4,2,32,512]{3,2,1,0:T(8,128)(2,1)S(1)}, u32[]{:S(2)}, u32[]{:S(2)}) %collective-permute-start.2) | collective-permute-done | bytes 262176 | tf_op jit(solution)/shard_map/ppermute | solution.py:31
  41.9 4.0 %collective-permute-start.4 = (bf16[4,32,512]{2,1,0:T(8,128)(2,1)S(1)}, bf16[4,32,512]{2,1,0:T(8,128)(2,1)S(1)}, u32[]{:S(2)}, u32[]{:S(2)}) collective-permute-start(bf16[4,32,512]{2,1,0:T(8,128)(2,1)S(1)} %get-tuple-element.39), channel_id=1, source_target_pairs={{0,8},{2,10},{4,12},{6,14},{8,0},{10,2},{12,4},{14,6},{16,24},{18,... | collective-permute-start | bytes 393224 | tf_op jit(solution)/shard_map/ppermute | solution.py:31
  45.8 1.7 %collective-permute-start.5 = (bf16[4,32,512]{2,1,0:T(8,128)(2,1)S(1)}, bf16[4,32,512]{2,1,0:T(8,128)(2,1)S(1)}, u32[]{:S(2)}, u32[]{:S(2)}) collective-permute-start(bf16[4,32,512]{2,1,0:T(8,128)(2,1)S(1)} %get-tuple-element.40), channel_id=1, source_target_pairs={{0,16},{2,18},{4,20},{6,22},{8,24},{10,26},{12,28},{14,30},{16,0},... | collective-permute-start | bytes 393224 | tf_op jit(solution)/shard_map/ppermute | solution.py:31
  49.4 7.5 %collective-permute-done.5.refs_2_ = bf16[4,32,512]{2,1,0:T(8,128)(2,1)S(1)} collective-permute-done((bf16[4,32,512]{2,1,0:T(8,128)(2,1)S(1)}, bf16[4,32,512]{2,1,0:T(8,128)(2,1)S(1)}, u32[]{:S(2)}, u32[]{:S(2)}) %collective-permute-start.5) | collective-permute-done | bytes 131104 | tf_op jit(solution)/shard_map/ppermute | solution.py:31
  57.1 2.2 %collective-permute-start.9 = (f32[8,128]{1,0:T(8,128)S(1)}, f32[8,128]{1,0:T(8,128)S(1)}, u32[]{:S(2)}, u32[]{:S(2)}) collective-permute-start(f32[8,128]{1,0:T(8,128)S(1)} %get-tuple-element.42), channel_id=1, source_target_pairs={{0,24},{2,26},{4,28},{6,30},{8,16},{10,18},{12,20},{14,22},{16,8},... | collective-permute-start | bytes 12296 | tf_op jit(solution)/shard_map/ppermute | solution.py:31
  62.2 1.5 %collective-permute-start.18 = (bf16[32,3712]{1,0:T(8,128)(2,1)S(1)}, bf16[32,3712]{1,0:T(8,128)(2,1)S(1)}, u32[]{:S(2)}, u32[]{:S(2)}) collective-permute-start(bf16[32,3712]{1,0:T(8,128)(2,1)S(1)} %slice.8), channel_id=1, source_target_pairs={{0,4},{2,6},{4,0},{6,2},{8,12},{10,14},{12,8},{14,10},{16,20},{18,... | collective-permute-start | bytes 712712 | tf_op jit(solution)/shard_map/ppermute | solution.py:31
  66.5 1.9 %collective-permute-start.22 = (bf16[4,32,512]{2,1,0:T(8,128)(2,1)S(1)}, bf16[4,32,512]{2,1,0:T(8,128)(2,1)S(1)}, u32[]{:S(2)}, u32[]{:S(2)}) collective-permute-start(bf16[4,32,512]{2,1,0:T(8,128)(2,1)S(1)} %get-tuple-element.49.refs_2_), channel_id=1, source_target_pairs={{0,6},{2,4},{4,2},{6,0},{8,14},{10,12},{12,10},{14,8},{16,22},{18,... | collective-permute-start | bytes 393224 | tf_op jit(solution)/shard_map/ppermute | solution.py:31
  71.0 2.1 %shard_map.73 = (bf16[512,512]{1,0:T(8,128)(2,1)S(1)}, bf16[512,512]{1,0:T(8,128)(2,1)S(1)}, f32[512,512]{1,0:T(8,128)S(1)}, f32[512,512]{1,0:T(8,128)S(1)}) custom-call(s32[4]{0:T(128)S(1)} %pad_add_fusion.where, bf16[32,7168]{1,0:T(8,128)(2,1)S(1)} %shard_map.72.refs_0_, bf16[32,7168]{1,0:T(8,128)(2,1)S(1)} %collective-permute-done.16.refs_1_, ...), custom_call_target="tpu_custom_call" | custom-call | flops 1073741824 | bytes 4980752 | tf_op jit(solution)/shard_map/pallas_call | solution.py:45
  73.1 2.5 %collective-permute-done.12 = f32[8,128]{1,0:T(8,128)S(1)} collective-permute-done((f32[8,128]{1,0:T(8,128)S(1)}, f32[8,128]{1,0:T(8,128)S(1)}, u32[]{:S(2)}, u32[]{:S(2)}) %collective-permute-start.12) | collective-permute-done | bytes 4128 | tf_op jit(solution)/shard_map/ppermute | solution.py:31
  75.6 2.2 %shard_map.74 = (bf16[512,512]{1,0:T(8,128)(2,1)S(1)}, f32[512,512]{1,0:T(8,128)S(1)}, f32[512,512]{1,0:T(8,128)S(1)}, f32[8,128]{1,0:T(8,128)S(1)}) custom-call(s32[4]{0:T(128)S(1)} %pad_add_fusion.where, bf16[512,512]{1,0:T(8,128)(2,1)S(1)} %get-tuple-element.47.refs_0_.refs_2_, bf16[512,512]{1,0:T(8,128)(2,1)S(1)} %get-tuple-element.48.refs_1_.refs_3_, ...), custom_call_target="tpu_custom_call" | custom-call | flops 1073741824 | bytes 4198416 | tf_op jit(solution)/shard_map/pallas_call | solution.py:45
  77.9 1.5 %shard_map.75 = (bf16[512,512]{1,0:T(8,128)(2,1)S(1)}, bf16[512,512]{1,0:T(8,128)(2,1)S(1)}, bf16[32,1024]{1,0:T(8,128)(2,1)S(1)}, bf16[32,1024]{1,0:T(8,128)(2,...) custom-call(s32[4]{0:T(128)S(1)} %pad_add_fusion.where, f32[8,128]{1,0:T(8,128)S(1)} %add.56.refs_0_.squares, ...), custom_call_target="tpu_custom_call" | custom-call | flops 536870912 | bytes 6561808 | tf_op jit(solution)/shard_map/pallas_call | solution.py:45
  79.3 1.5 %shard_map.76 = (bf16[32,512]{1,0:T(8,128)(2,1)S(1)}, bf16[32,512]{1,0:T(8,128)(2,1)S(1)}, bf16[32,512]{1,0:T(8,128)(2,1)S(1)}, bf16[32,512]{1,0:T(8,128)(2,1)S(1)}) custom-call(s32[4]{0:T(128)S(1)} %pad_add_fusion.where, f32[8,128]{1,0:T(8,128)S(1)} %add.56.refs_0_.squares, bf16[512,512]{1,0:T(8,128)(2,1)S(1)} %get-tuple-element.59.new_left, ...), custom_call_target="tpu_custom_call" | custom-call | flops 805306368 | bytes 1708048 | tf_op jit(solution)/shard_map/pallas_call | solution.py:45
  83.0 2.0 %collective-permute-start.24 = (bf16[32,1024]{1,0:T(8,128)(2,1)S(1)}, bf16[32,1024]{1,0:T(8,128)(2,1)S(1)}, u32[]{:S(2)}, u32[]{:S(2)}) collective-permute-start(bf16[32,1024]{1,0:T(8,128)(2,1)S(1)} %get-tuple-element.57), channel_id=1, source_target_pairs={{0,16},{2,18},{4,20},{6,22},{8,24},{10,26},{12,28},{14,30},{16,0},... | collective-permute-start | bytes 196616 | tf_op jit(solution)/shard_map/ppermute | solution.py:31
  87.1 1.7 %collective-permute-start.28 = (bf16[32,512]{1,0:T(8,128)(2,1)S(1)}, bf16[32,512]{1,0:T(8,128)(2,1)S(1)}, u32[]{:S(2)}, u32[]{:S(2)}) collective-permute-start(bf16[32,512]{1,0:T(8,128)(2,1)S(1)} %get-tuple-element.65), channel_id=1, source_target_pairs={{0,24},{2,26},{4,28},{6,30},{8,16},{10,18},{12,20},{14,22},{16,8},... | collective-permute-start | bytes 98312 | tf_op jit(solution)/shard_map/ppermute | solution.py:31
  88.8 5.1 %collective-permute-done.27.refs_6_ = bf16[32,512]{1,0:T(8,128)(2,1)S(1)} collective-permute-done((bf16[32,512]{1,0:T(8,128)(2,1)S(1)}, bf16[32,512]{1,0:T(8,128)(2,1)S(1)}, u32[]{:S(2)}, u32[]{:S(2)}) %collective-permute-start.27) | collective-permute-done | bytes 32800 | tf_op jit(solution)/shard_map/ppermute | solution.py:31
  (63 shorter events, 23.9 us)
Async XLA Ops:
  1.9 26.7 %collective-permute-start = (bf16[4,2,2,32,512]{4,3,2,1,0:T(8,128)(2,1)S(1)}, bf16[4,2,2,32,512]{4,3,2,1,0:T(8,128)(2,1)S(1)}, u32[]{:S(2)}, u32[]{:S(2)}) collective-permute-start(bf16[4,2,2,32,512]{4,3,2,1,0:T(8,128)(2,1)S(1)} %dynamic-slice_bitcast_fusion.1), channel_id=1, source_target_pairs={{0,2},{2,0},{4,6},{6,4},{8,10},{10,8},{12,14},{14,12},{16,18},{18,... | collective-permute-start | bytes 1572872 | tf_op jit(solution)/shard_map/ppermute | solution.py:31
  6.8 21.8 %collective-permute-start.1 = (bf16[4,2,2,32,512]{4,3,2,1,0:T(8,128)(2,1)}, bf16[4,2,2,32,512]{4,3,2,1,0:T(8,128)(2,1)S(1)}, u32[]{:S(2)}, u32[]{:S(2)}) collective-permute-start(bf16[4,2,2,32,512]{4,3,2,1,0:T(8,128)(2,1)} %dynamic-slice_bitcast_fusion), channel_id=1, source_target_pairs={{0,4},{2,6},{4,0},{6,2},{8,12},{10,14},{12,8},{14,10},{16,20},{18,... | collective-permute-start | bytes 1572872 | tf_op jit(solution)/shard_map/ppermute | solution.py:31
  9.3 7.6 %collective-permute-start.13 = (bf16[32,2560]{1,0:T(8,128)(2,1)S(1)}, bf16[32,2560]{1,0:T(8,128)(2,1)S(1)}, u32[]{:S(2)}, u32[]{:S(2)}) collective-permute-start(bf16[32,2560]{1,0:T(8,128)(2,1)S(1)} %get-tuple-element.44), channel_id=1, source_target_pairs={{0,8},{2,10},{4,12},{6,14},{8,0},{10,2},{12,4},{14,6},{16,24},{18,... | collective-permute-start | bytes 491528 | tf_op jit(solution)/shard_map/ppermute | solution.py:31
  10.9 14.8 %collective-permute-start.14 = (bf16[32,2560]{1,0:T(8,128)(2,1)S(1)}, bf16[32,2560]{1,0:T(8,128)(2,1)S(1)}, u32[]{:S(2)}, u32[]{:S(2)}) collective-permute-start(bf16[32,2560]{1,0:T(8,128)(2,1)S(1)} %get-tuple-element.45), channel_id=1, source_target_pairs={{0,16},{2,18},{4,20},{6,22},{8,24},{10,26},{12,28},{14,30},{16,0},... | collective-permute-start | bytes 491528 | tf_op jit(solution)/shard_map/ppermute | solution.py:31
  13.5 12.2 %collective-permute-start.15 = (bf16[32,2560]{1,0:T(8,128)(2,1)S(1)}, bf16[32,2560]{1,0:T(8,128)(2,1)S(1)}, u32[]{:S(2)}, u32[]{:S(2)}) collective-permute-start(bf16[32,2560]{1,0:T(8,128)(2,1)S(1)} %get-tuple-element.46), channel_id=1, source_target_pairs={{0,24},{2,26},{4,28},{6,30},{8,16},{10,18},{12,20},{14,22},{16,8},... | collective-permute-start | bytes 491528 | tf_op jit(solution)/shard_map/ppermute | solution.py:31
  26.4 35.2 %collective-permute-start.17 = (bf16[32,7168]{1,0:T(8,128)(2,1)S(1)}, bf16[32,7168]{1,0:T(8,128)(2,1)S(1)}, u32[]{:S(2)}, u32[]{:S(2)}) collective-permute-start(bf16[32,7168]{1,0:T(8,128)(2,1)S(1)} %shard_map.72.refs_0_), channel_id=1, source_target_pairs={{0,4},{2,6},{4,0},{6,2},{8,12},{10,14},{12,8},{14,10},{16,20},{18,... | collective-permute-start | bytes 1376264 | tf_op jit(solution)/shard_map/ppermute | solution.py:31
  27.0 35.2 %collective-permute-start.16 = (bf16[32,7168]{1,0:T(8,128)(2,1)S(1)}, bf16[32,7168]{1,0:T(8,128)(2,1)S(1)}, u32[]{:S(2)}, u32[]{:S(2)}) collective-permute-start(bf16[32,7168]{1,0:T(8,128)(2,1)S(1)} %shard_map.72.refs_0_), channel_id=1, source_target_pairs={{0,2},{2,0},{4,6},{6,4},{8,10},{10,8},{12,14},{14,12},{16,18},{18,... | collective-permute-start | bytes 1376264 | tf_op jit(solution)/shard_map/ppermute | solution.py:31
  29.4 11.6 %collective-permute-start.2 = (bf16[4,2,32,512]{3,2,1,0:T(8,128)(2,1)S(1)}, bf16[4,2,32,512]{3,2,1,0:T(8,128)(2,1)S(1)}, u32[]{:S(2)}, u32[]{:S(2)}) collective-permute-start(bf16[4,2,32,512]{3,2,1,0:T(8,128)(2,1)S(1)} %get-tuple-element.36), channel_id=1, source_target_pairs={{0,4},{2,6},{4,0},{6,2},{8,12},{10,14},{12,8},{14,10},{16,20},{18,... | collective-permute-start | bytes 786440 | tf_op jit(solution)/shard_map/ppermute | solution.py:31
  31.0 10.3 %collective-permute-start.3 = (bf16[4,2,32,512]{3,2,1,0:T(8,128)(2,1)S(1)}, bf16[4,2,32,512]{3,2,1,0:T(8,128)(2,1)S(1)}, u32[]{:S(2)}, u32[]{:S(2)}) collective-permute-start(bf16[4,2,32,512]{3,2,1,0:T(8,128)(2,1)S(1)} %get-tuple-element.37), channel_id=1, source_target_pairs={{0,2},{2,0},{4,6},{6,4},{8,10},{10,8},{12,14},{14,12},{16,18},{18,... | collective-permute-start | bytes 786440 | tf_op jit(solution)/shard_map/ppermute | solution.py:31
  41.9 7.6 %collective-permute-start.4 = (bf16[4,32,512]{2,1,0:T(8,128)(2,1)S(1)}, bf16[4,32,512]{2,1,0:T(8,128)(2,1)S(1)}, u32[]{:S(2)}, u32[]{:S(2)}) collective-permute-start(bf16[4,32,512]{2,1,0:T(8,128)(2,1)S(1)} %get-tuple-element.39), channel_id=1, source_target_pairs={{0,8},{2,10},{4,12},{6,14},{8,0},{10,2},{12,4},{14,6},{16,24},{18,... | collective-permute-start | bytes 393224 | tf_op jit(solution)/shard_map/ppermute | solution.py:31
  45.8 11.1 %collective-permute-start.5 = (bf16[4,32,512]{2,1,0:T(8,128)(2,1)S(1)}, bf16[4,32,512]{2,1,0:T(8,128)(2,1)S(1)}, u32[]{:S(2)}, u32[]{:S(2)}) collective-permute-start(bf16[4,32,512]{2,1,0:T(8,128)(2,1)S(1)} %get-tuple-element.40), channel_id=1, source_target_pairs={{0,16},{2,18},{4,20},{6,22},{8,24},{10,26},{12,28},{14,30},{16,0},... | collective-permute-start | bytes 393224 | tf_op jit(solution)/shard_map/ppermute | solution.py:31
  47.5 9.4 %collective-permute-start.6 = (bf16[4,32,512]{2,1,0:T(8,128)(2,1)S(1)}, bf16[4,32,512]{2,1,0:T(8,128)(2,1)S(1)}, u32[]{:S(2)}, u32[]{:S(2)}) collective-permute-start(bf16[4,32,512]{2,1,0:T(8,128)(2,1)S(1)} %get-tuple-element.41), channel_id=1, source_target_pairs={{0,24},{2,26},{4,28},{6,30},{8,16},{10,18},{12,20},{14,22},{16,8},... | collective-permute-start | bytes 393224 | tf_op jit(solution)/shard_map/ppermute | solution.py:31
  57.1 6.6 %collective-permute-start.9 = (f32[8,128]{1,0:T(8,128)S(1)}, f32[8,128]{1,0:T(8,128)S(1)}, u32[]{:S(2)}, u32[]{:S(2)}) collective-permute-start(f32[8,128]{1,0:T(8,128)S(1)} %get-tuple-element.42), channel_id=1, source_target_pairs={{0,24},{2,26},{4,28},{6,30},{8,16},{10,18},{12,20},{14,22},{16,8},... | collective-permute-start | bytes 12296 | tf_op jit(solution)/shard_map/ppermute | solution.py:31
  61.6 8.5 %collective-permute-start.19 = (bf16[32,3456]{1,0:T(8,128)(2,1)S(1)}, bf16[32,3456]{1,0:T(8,128)(2,1)S(1)}, u32[]{:S(2)}, u32[]{:S(2)}) collective-permute-start(bf16[32,3456]{1,0:T(8,128)(2,1)S(1)} %slice.9), channel_id=1, source_target_pairs={{0,2},{2,0},{4,6},{6,4},{8,10},{10,8},{12,14},{14,12},{16,18},{18,... | collective-permute-start | bytes 663560 | tf_op jit(solution)/shard_map/ppermute | solution.py:31
  62.2 8.8 %collective-permute-start.18 = (bf16[32,3712]{1,0:T(8,128)(2,1)S(1)}, bf16[32,3712]{1,0:T(8,128)(2,1)S(1)}, u32[]{:S(2)}, u32[]{:S(2)}) collective-permute-start(bf16[32,3712]{1,0:T(8,128)(2,1)S(1)} %slice.8), channel_id=1, source_target_pairs={{0,4},{2,6},{4,0},{6,2},{8,12},{10,14},{12,8},{14,10},{16,20},{18,... | collective-permute-start | bytes 712712 | tf_op jit(solution)/shard_map/ppermute | solution.py:31
  66.5 9.1 %collective-permute-start.22 = (bf16[4,32,512]{2,1,0:T(8,128)(2,1)S(1)}, bf16[4,32,512]{2,1,0:T(8,128)(2,1)S(1)}, u32[]{:S(2)}, u32[]{:S(2)}) collective-permute-start(bf16[4,32,512]{2,1,0:T(8,128)(2,1)S(1)} %get-tuple-element.49.refs_2_), channel_id=1, source_target_pairs={{0,6},{2,4},{4,2},{6,0},{8,14},{10,12},{12,10},{14,8},{16,22},{18,... | collective-permute-start | bytes 393224 | tf_op jit(solution)/shard_map/ppermute | solution.py:31
  68.3 7.3 %collective-permute-start.21 = (bf16[4,32,512]{2,1,0:T(8,128)(2,1)S(1)}, bf16[4,32,512]{2,1,0:T(8,128)(2,1)S(1)}, u32[]{:S(2)}, u32[]{:S(2)}) collective-permute-start(bf16[4,32,512]{2,1,0:T(8,128)(2,1)S(1)} %get-tuple-element.49.refs_2_), channel_id=1, source_target_pairs={{0,4},{2,6},{4,0},{6,2},{8,12},{10,14},{12,8},{14,10},{16,20},{18,... | collective-permute-start | bytes 393224 | tf_op jit(solution)/shard_map/ppermute | solution.py:31
  69.0 6.6 %collective-permute-start.20 = (bf16[4,32,512]{2,1,0:T(8,128)(2,1)S(1)}, bf16[4,32,512]{2,1,0:T(8,128)(2,1)S(1)}, u32[]{:S(2)}, u32[]{:S(2)}) collective-permute-start(bf16[4,32,512]{2,1,0:T(8,128)(2,1)S(1)} %get-tuple-element.49.refs_2_), channel_id=1, source_target_pairs={{0,2},{2,0},{4,6},{6,4},{8,10},{10,8},{12,14},{14,12},{16,18},{18,... | collective-permute-start | bytes 393224 | tf_op jit(solution)/shard_map/ppermute | solution.py:31
  80.9 6.3 %collective-permute-start.26 = (bf16[32,512]{1,0:T(8,128)(2,1)S(1)}, bf16[32,512]{1,0:T(8,128)(2,1)S(1)}, u32[]{:S(2)}, u32[]{:S(2)}) collective-permute-start(bf16[32,512]{1,0:T(8,128)(2,1)S(1)} %get-tuple-element.63), channel_id=1, source_target_pairs={{0,8},{2,10},{4,12},{6,14},{8,0},{10,2},{12,4},{14,6},{16,24},{18,... | collective-permute-start | bytes 98312 | tf_op jit(solution)/shard_map/ppermute | solution.py:31
  82.0 12.0 %collective-permute-start.23 = (bf16[32,1024]{1,0:T(8,128)(2,1)S(1)}, bf16[32,1024]{1,0:T(8,128)(2,1)S(1)}, u32[]{:S(2)}, u32[]{:S(2)}) collective-permute-start(bf16[32,1024]{1,0:T(8,128)(2,1)S(1)} %get-tuple-element.56), channel_id=1, source_target_pairs={{0,8},{2,10},{4,12},{6,14},{8,0},{10,2},{12,4},{14,6},{16,24},{18,... | collective-permute-start | bytes 196616 | tf_op jit(solution)/shard_map/ppermute | solution.py:31
  83.0 11.0 %collective-permute-start.24 = (bf16[32,1024]{1,0:T(8,128)(2,1)S(1)}, bf16[32,1024]{1,0:T(8,128)(2,1)S(1)}, u32[]{:S(2)}, u32[]{:S(2)}) collective-permute-start(bf16[32,1024]{1,0:T(8,128)(2,1)S(1)} %get-tuple-element.57), channel_id=1, source_target_pairs={{0,16},{2,18},{4,20},{6,22},{8,24},{10,26},{12,28},{14,30},{16,0},... | collective-permute-start | bytes 196616 | tf_op jit(solution)/shard_map/ppermute | solution.py:31
  85.0 9.0 %collective-permute-start.25 = (bf16[32,1024]{1,0:T(8,128)(2,1)S(1)}, bf16[32,1024]{1,0:T(8,128)(2,1)S(1)}, u32[]{:S(2)}, u32[]{:S(2)}) collective-permute-start(bf16[32,1024]{1,0:T(8,128)(2,1)S(1)} %get-tuple-element.58), channel_id=1, source_target_pairs={{0,24},{2,26},{4,28},{6,30},{8,16},{10,18},{12,20},{14,22},{16,8},... | collective-permute-start | bytes 196616 | tf_op jit(solution)/shard_map/ppermute | solution.py:31
  86.4 7.6 %collective-permute-start.27 = (bf16[32,512]{1,0:T(8,128)(2,1)S(1)}, bf16[32,512]{1,0:T(8,128)(2,1)S(1)}, u32[]{:S(2)}, u32[]{:S(2)}) collective-permute-start(bf16[32,512]{1,0:T(8,128)(2,1)S(1)} %get-tuple-element.64), channel_id=1, source_target_pairs={{0,16},{2,18},{4,20},{6,22},{8,24},{10,26},{12,28},{14,30},{16,0},... | collective-permute-start | bytes 98312 | tf_op jit(solution)/shard_map/ppermute | solution.py:31
  87.1 6.8 %collective-permute-start.28 = (bf16[32,512]{1,0:T(8,128)(2,1)S(1)}, bf16[32,512]{1,0:T(8,128)(2,1)S(1)}, u32[]{:S(2)}, u32[]{:S(2)}) collective-permute-start(bf16[32,512]{1,0:T(8,128)(2,1)S(1)} %get-tuple-element.65), channel_id=1, source_target_pairs={{0,24},{2,26},{4,28},{6,30},{8,16},{10,18},{12,20},{14,22},{16,8},... | collective-permute-start | bytes 98312 | tf_op jit(solution)/shard_map/ppermute | solution.py:31
  (9 other events, 49.3 us)

commit v5 on v4

--- a/solution.py
+++ b/solution.py
@@ -123,10 +123,17 @@
     pieces = refs[:-7]
     left, right, left_gram, right_gram, left_inv, right_inv, probe = refs[-7:]
     spread(plan, where, pieces, (left, right, left_inv, right_inv, probe))
-    half_conjugate = product(left_inv[...], probe[...], 0, 0).astype(HALF)
-    conjugate = product(half_conjugate, right_inv[...]).astype(HALF)
-    left_gram[...] = product(conjugate, conjugate, 1, 1)
-    right_gram[...] = product(conjugate, conjugate, 0, 0)
+    h = plan.size // 2
+    half_conjugate = jnp.concatenate(
+        [product(left_inv[:h, :h], probe[:h, :], 0, 0), product(left_inv[:, h:], probe[...], 0, 0)],
+        axis=0,
+    ).astype(HALF)
+    conjugate = jnp.concatenate(
+        [product(half_conjugate[:, :h], right_inv[:h, :h]), product(half_conjugate, right_inv[:, h:])],
+        axis=1,
+    ).astype(HALF)
+    gram_rows(left_gram, conjugate)
+    gram_columns(right_gram, conjugate)
 
 
 def relay_kernel(where, own, low_own, low_seen, high_own, high_seen, kept, low_out, high_out):
@@ -176,10 +183,17 @@
     wide = grad[...].astype(FLOAT)
     clip = bound_of(limit, jnp.sum(wide * wide, keepdims=True))
     own_clip[...] = jnp.broadcast_to(clip, own_clip.shape)
-    left_times = (clip * product(left[...], grad[...])).astype(HALF)
-    whitened = product(left_times, right[...], 1, 1).astype(HALF)
-    left_gram[...] = product(whitened, whitened, 1, 1)
-    right_gram[...] = product(whitened, whitened, 0, 0)
+    h = plan.size // 2
+    left_times = jnp.concatenate(
+        [product(left[:h, :], grad[...]), product(left[h:, h:], grad[h:, :])], axis=0
+    )
+    left_times = (clip * left_times).astype(HALF)
+    whitened = jnp.concatenate(
+        [product(left_times, right[:h, :], 1, 1), product(left_times[:, h:], right[h:, h:], 1, 1)],
+        axis=1,
+    ).astype(HALF)
+    gram_rows(left_gram, whitened)
+    gram_columns(right_gram, whitened)
 
 
 def step_factor(factor, ratio, first_ref, second_ref):
@@ -196,39 +210,82 @@
     return bound_of(limit, squares[0:1, 0:1])
 
 
-def factor_kernel(plan, limit, where, *refs):
-    squares, own_clip, left, right, left_p, right_p, left_q, right_q = refs[:8]
-    new_left, new_right, outs = refs[8], refs[9], refs[10:]
-    ratio = clip_of(limit, squares) / own_clip[0:1, 0:1]
+def gram_rows(out, matrix):
+    h = out.shape[0] // 2
+    out[:h, :] = product(matrix[:h, :], matrix, 1, 1)
+    out[h:, h:] = product(matrix[h:, :], matrix[h:, :], 1, 1)
+
+
+def gram_columns(out, matrix):
+    h = out.shape[0] // 2
+    out[:h, :] = product(matrix[:, :h], matrix, 0, 0)
+    out[h:, h:] = product(matrix[:, h:], matrix[:, h:], 0, 0)
+
+
+def move_factor(out, factor, ratio, first, second):
+    h = out.shape[0] // 2
+    firsts = ratio * first[:h, :], ratio * first[h:, h:]
+    seconds = second[:h, :], second[h:, h:]
+    peaks = [jnp.max(jnp.abs(p + q), keepdims=True) for p, q in zip(firsts, seconds)]
+    scale = LEARN_RATE / (jnp.maximum(*peaks) + EPS_NORM)
+    top, end = [
+        jnp.where(
+            lax.broadcasted_iota(jnp.int32, p.shape, 0) <= lax.broadcasted_iota(jnp.int32, p.shape, 1),
+            p - q,
+            0.0,
+        ).astype(HALF)
+        for p, q in zip(firsts, seconds)
+    ]
+
+    def moved(old, moved_rows):
+        return (old.astype(FLOAT) - scale * moved_rows).astype(HALF)
+
+    out[:h, :h] = moved(factor[:h, :h], product(top[:, :h], factor[:h, :h]))
+    out[:h, h:] = moved(factor[:h, h:], product(top, factor[:, h:]))
+    out[h:, :h] = jnp.zeros((h, h), HALF)
+    out[h:, h:] = moved(factor[h:, h:], product(end, factor[h:, h:]))
+
+
+def square_of(out, factor):
+    h = out.shape[0] // 2
+    out[:h, :] = product(factor[:h, :h], factor[:h, :], 0, 0).astype(HALF)
+    out[h:, :h] = product(factor[:h, h:], factor[:h, :h], 0, 0).astype(HALF)
+    out[h:, h:] = product(factor[:, h:], factor[:, h:], 0, 0).astype(HALF)
+
+
+def finish_kernel(plan, limit, where, *refs):
+    squares, own_clip, left, right, grad, left_p, right_p, left_q, right_q = refs[:9]
+    outs, (new_left, new_right, left_square, right_square, result) = refs[9:-5], refs[-5:]
+    clip = clip_of(limit, squares)
+    ratio = clip / own_clip[0:1, 0:1]
     ratio = ratio * ratio
     size, rows = plan.size, plan.rows
-    new_left[...] = step_factor(left[...], ratio, left_p, left_q)
-    new_right[...] = step_factor(right[...], ratio, right_p, right_q)
+    move_factor(new_left, left, ratio, left_p, left_q)
+    move_factor(new_right, right, ratio, right_p, right_q)
+    square_of(left_square, new_left)
+    square_of(right_square, new_right)
+
+    def at(z):
+        return pl.ds(pl.multiple_of((z * plan.group + where[1]) * rows, rows), rows)
+
+    precond_left = jnp.concatenate([left_square[at(z), :] for z in range(plan.blocks)], axis=0)
+    middle = (clip * product(precond_left, grad[...])).astype(HALF)
+    done = product(middle, right_square[...]).astype(HALF)
+    result[...] = done.reshape(plan.blocks, rows, size)
     for k, out in enumerate(outs):
-        row = pl.multiple_of(((where[0] ^ k) * plan.group + where[1]) * rows, rows)
-        out[:, :size] = new_left[pl.ds(row, rows), :]
-        out[:, size:] = new_right[pl.ds(row, rows), :]
-
-
-def result_kernel(plan, limit, where, squares, new_left, new_right, grad, *refs):
-    outs, (square, result) = refs[:-2], refs[-2:]
-    size, rows = plan.size, plan.rows
-    square[...] = product(new_left[...], new_left[...], 0, 0).astype(HALF)
-    precond_right = product(new_right[...], new_right[...], 0, 0).astype(HALF)
-    starts = [pl.multiple_of((z * plan.group + where[1]) * rows, rows) for z in range(plan.blocks)]
-    precond_left = jnp.concatenate([square[pl.ds(row, rows), :] for row in starts], axis=0)
-    middle = (clip_of(limit, squares) * product(precond_left, grad[...])).astype(HALF)
-    result[...] = product(middle, precond_right).astype(HALF).reshape(plan.blocks, rows, size)
-    for k, out in enumerate(outs):
-        out[...] = result[where[0] ^ k]
+        z = where[0] ^ k
+        out[:, :size] = new_left[at(z), :]
+        out[:, size : 2 * size] = new_right[at(z), :]
+        out[:, 2 * size :] = result[z]
 
 
 def place_kernel(plan, where, slots, old_state, *refs):
-    pieces, (precond, new_state) = refs[:-2], refs[-2:]
+    pieces, (precond, new_state) = refs[: plan.blocks], refs[plan.blocks :]
+    size = plan.size
     new_state[...] = old_state[...]
-    for k in range(plan.blocks):
-        new_state[slots[where[0] ^ k]] = pieces[k][...]
-        precond[where[0] ^ k] = pieces[plan.blocks + k][...]
+    for k, piece in enumerate(pieces):
+        precond[where[0] ^ k] = piece[:, 2 * size :]
+        new_state[slots[where[0] ^ k]] = piece[:, : 2 * size]
 
 
 def shaped(shape, dtype=HALF):
@@ -248,7 +305,7 @@
     my_low, my_high = my_place % 2, my_place // 2
     where = jnp.stack([my_block, my_place, my_low, my_high]).astype(jnp.int32)
     slot_row = slot_table[0]
-    in_tiles = rows % 16 == 0
+    in_tiles = rows % 16 == 0 and size % (2 * LANES) == 0
     limit = CLIP_RMS * math.sqrt(blocks * size * columns * halves)
 
     grads = partial_grads[0].reshape(blocks, blocks, group, rows, columns)
@@ -400,38 +457,26 @@
             right_q,
             *quarters,
         )
-        new_left, new_right, *back = call(
-            functools.partial(factor_kernel, plan, limit),
-            (square, square) + tuple(shaped((rows, 2 * size)) for _ in range(blocks)),
-            [],
-            2 * matmul,
+        back = call(
+            functools.partial(finish_kernel, plan, limit),
+            tuple(shaped((rows, 2 * size + columns)) for _ in range(blocks)),
+            [pltpu.VMEM((size, size), HALF)] * 4 + [pltpu.VMEM((blocks, rows, columns), HALF)],
+            5 * matmul,
             1,
             where,
             squares,
             own_clip,
             left_q,
             right_q,
+            gradient,
             left_w,
             right_w,
             left_c,
             right_c,
         )
-        last = call(
-            functools.partial(result_kernel, plan, limit),
-            tuple(shaped((rows, columns)) for _ in range(blocks)),
-            [pltpu.VMEM((size, size), HALF), pltpu.VMEM((blocks, rows, columns), HALF)],
-            3 * matmul,
-            1,
-            where,
-            squares,
-            new_left,
-            new_right,
-            gradient,
-        )
     else:
-        back, last = plain_block(plan, limit, my_block, my_place, squares, states, quarters)
+        back = plain_block(plan, limit, my_block, my_place, squares, states, quarters)
     back = [back[0]] + [flip(back[k], devices, k * group) for k in range(1, blocks)]
-    last = [last[0]] + [flip(last[k], devices, k * group) for k in range(1, blocks)]
     precond, new_state = call(
         functools.partial(place_kernel, plan),
         (shaped((blocks, rows, columns)), shaped(old_state.shape)),
@@ -442,7 +487,6 @@
         slot_row,
         old_state,
         *back,
-        *last,
     )
     return (precond.reshape(experts, block_rows, rows, columns), new_state[None])
 
@@ -471,9 +515,8 @@
 
     middle = (clip * product(my_rows(precond_left).reshape(blocks * rows, size), gradient)).astype(HALF)
     result = product(middle, precond_right).astype(HALF).reshape(blocks, rows, -1)
-    back = jnp.concatenate([my_rows(new_left), my_rows(new_right)], axis=2)
-    order = [my_block ^ k for k in range(blocks)]
-    return [pick(back, b, 0) for b in order], [pick(result, b, 0) for b in order]
+    back = jnp.concatenate([my_rows(new_left), my_rows(new_right), result], axis=2)
+    return [pick(back, my_block ^ k, 0) for k in range(blocks)]
 
 
 def solution(mesh):

time: 95.6 us -> 93 us (0.973)
  starting transfers between devices: 40.3 us -> 36.8 us
  waiting for transfers between devices: 37.1 us -> 39.4 us
  Pallas kernels: 11.8 us -> 10.4 us
    ppermute x28 -> x25, starting transfers between devices: 40.3 us -> 36.8 us  [flip(): return lax.ppermute(array, 'dp', [(i, i ^ mask) for i in range(devices)])]
    ppermute x28 -> x25, waiting for transfers between devices: 35.9 us -> 38.2 us  [flip(): return lax.ppermute(array, 'dp', [(i, i ^ mask) for i in range(devices)])]
    pallas_call x10 -> x9, Pallas kernels: 11.8 us -> 10.4 us  [call(): pl.pallas_call(kernel, out_shape=out_shape, in_specs=[SMEM_SPEC] * smem +...]
  transfers between devices with their start and end apart: 29 -> 26, of which waited for: 12 -> 13; matrix products, arithmetic and copies ran while one was open for 4% -> 4% of each run, Pallas kernels for 6% -> 5%
where the time goes in v5:
time: 93 us; the launch traced here: 92.8 us
  waiting for transfers between devices  39.4 us (42%)
  starting transfers between devices  36.8 us (40%)
  Pallas kernels  10.4 us (11%)
  local copies, waits for them, and re-layouts  5.24 us (6%)
    ppermute x25, waiting for transfers between devices, flip(): return lax.ppermute(array, 'dp', [(i, i ^ mask) for i in range(devices)])  38.2 us
    ppermute x25, starting transfers between devices, flip(): return lax.ppermute(array, 'dp', [(i, i ^ mask) for i in range(devices)])  36.8 us
    pallas_call x9, Pallas kernels, call(): pl.pallas_call(kernel, out_shape=out_shape, in_specs=[SMEM_SPEC] * smem +...  10.4 us
    reshape x4, local copies, waits for them, and re-layouts, part(): cut.reshape([n for i, n in enumerate(extent) if n > 1 or i not in (2, 3)])  5.19 us
  transfers between devices with their start and end apart: 26, of which 13 were waited for; matrix products, arithmetic and copies ran while one was open for 4% of the time, Pallas kernels for 5%

profile of v5, /device:TPU:0, one launch (start us, length us, event | category | flops | bytes accessed | tf_op | source)
XLA Modules:
  0.0 92.8 jit_solution(11053137260621691498)
XLA Ops:
  1.9 3.0 %collective-permute-start = (bf16[4,2,2,32,512]{4,3,2,1,0:T(8,128)(2,1)S(1)}, bf16[4,2,2,32,512]{4,3,2,1,0:T(8,128)(2,1)S(1)}, u32[]{:S(2)}, u32[]{:S(2)}) collective-permute-start(bf16[4,2,2,32,512]{4,3,2,1,0:T(8,128)(2,1)S(1)} %dynamic-slice_bitcast_fusion.1), channel_id=1, source_target_pairs={{0,2},{2,0},{4,6},{6,4},{8,10},{10,8},{12,14},{14,12},{16,18},{18,... | collective-permute-start | bytes 1572872 | tf_op jit(solution)/shard_map/ppermute | solution.py:31
  4.9 1.9 %dynamic-slice_bitcast_fusion = bf16[4,2,2,32,512]{4,3,2,1,0:T(8,128)(2,1)} fusion(bf16[4,4,2,2,32,512]{5,4,3,2,1,0:T(8,128)(2,1)} %bitcast.38, s32[]{:T(128)S(6)} %select_n.40), kind=kLoop, calls=%fused_computation | loop fusion | bytes 1048580 | tf_op jit(solution)/shard_map/reshape | solution.py:327
  6.8 1.5 %collective-permute-start.1 = (bf16[4,2,2,32,512]{4,3,2,1,0:T(8,128)(2,1)}, bf16[4,2,2,32,512]{4,3,2,1,0:T(8,128)(2,1)S(1)}, u32[]{:S(2)}, u32[]{:S(2)}) collective-permute-start(bf16[4,2,2,32,512]{4,3,2,1,0:T(8,128)(2,1)} %dynamic-slice_bitcast_fusion), channel_id=1, source_target_pairs={{0,4},{2,6},{4,0},{6,2},{8,12},{10,14},{12,8},{14,10},{16,20},{18,... | collective-permute-start | bytes 1572872 | tf_op jit(solution)/shard_map/ppermute | solution.py:31
  9.3 1.6 %collective-permute-start.13 = (bf16[32,2560]{1,0:T(8,128)(2,1)S(1)}, bf16[32,2560]{1,0:T(8,128)(2,1)S(1)}, u32[]{:S(2)}, u32[]{:S(2)}) collective-permute-start(bf16[32,2560]{1,0:T(8,128)(2,1)S(1)} %get-tuple-element.38), channel_id=1, source_target_pairs={{0,8},{2,10},{4,12},{6,14},{8,0},{10,2},{12,4},{14,6},{16,24},{18,... | collective-permute-start | bytes 491528 | tf_op jit(solution)/shard_map/ppermute | solution.py:31
  11.0 2.6 %collective-permute-start.14 = (bf16[32,2560]{1,0:T(8,128)(2,1)S(1)}, bf16[32,2560]{1,0:T(8,128)(2,1)S(1)}, u32[]{:S(2)}, u32[]{:S(2)}) collective-permute-start(bf16[32,2560]{1,0:T(8,128)(2,1)S(1)} %get-tuple-element.39), channel_id=1, source_target_pairs={{0,16},{2,18},{4,20},{6,22},{8,24},{10,26},{12,28},{14,30},{16,0},... | collective-permute-start | bytes 491528 | tf_op jit(solution)/shard_map/ppermute | solution.py:31
  14.9 2.0 %collective-permute-done.13.refs_1_ = bf16[32,2560]{1,0:T(8,128)(2,1)S(1)} collective-permute-done((bf16[32,2560]{1,0:T(8,128)(2,1)S(1)}, bf16[32,2560]{1,0:T(8,128)(2,1)S(1)}, u32[]{:S(2)}, u32[]{:S(2)}) %collective-permute-start.13) | collective-permute-done | bytes 163872 | tf_op jit(solution)/shard_map/ppermute | solution.py:31
  16.9 8.9 %collective-permute-done.14.refs_2_ = bf16[32,2560]{1,0:T(8,128)(2,1)S(1)} collective-permute-done((bf16[32,2560]{1,0:T(8,128)(2,1)S(1)}, bf16[32,2560]{1,0:T(8,128)(2,1)S(1)}, u32[]{:S(2)}, u32[]{:S(2)}) %collective-permute-start.14) | collective-permute-done | bytes 163872 | tf_op jit(solution)/shard_map/ppermute | solution.py:31
  29.4 1.6 %collective-permute-start.2 = (bf16[4,2,32,512]{3,2,1,0:T(8,128)(2,1)S(1)}, bf16[4,2,32,512]{3,2,1,0:T(8,128)(2,1)S(1)}, u32[]{:S(2)}, u32[]{:S(2)}) collective-permute-start(bf16[4,2,32,512]{3,2,1,0:T(8,128)(2,1)S(1)} %get-tuple-element.30), channel_id=1, source_target_pairs={{0,4},{2,6},{4,0},{6,2},{8,12},{10,14},{12,8},{14,10},{16,20},{18,... | collective-permute-start | bytes 786440 | tf_op jit(solution)/shard_map/ppermute | solution.py:31
  31.0 1.5 %collective-permute-start.3 = (bf16[4,2,32,512]{3,2,1,0:T(8,128)(2,1)S(1)}, bf16[4,2,32,512]{3,2,1,0:T(8,128)(2,1)S(1)}, u32[]{:S(2)}, u32[]{:S(2)}) collective-permute-start(bf16[4,2,32,512]{3,2,1,0:T(8,128)(2,1)S(1)} %get-tuple-element.31), channel_id=1, source_target_pairs={{0,2},{2,0},{4,6},{6,4},{8,10},{10,8},{12,14},{14,12},{16,18},{18,... | collective-permute-start | bytes 786440 | tf_op jit(solution)/shard_map/ppermute | solution.py:31
  32.5 8.5 %collective-permute-done.2.low_last = bf16[4,2,32,512]{3,2,1,0:T(8,128)(2,1)S(1)} collective-permute-done((bf16[4,2,32,512]{3,2,1,0:T(8,128)(2,1)S(1)}, bf16[4,2,32,512]{3,2,1,0:T(8,128)(2,1)S(1)}, u32[]{:S(2)}, u32[]{:S(2)}) %collective-permute-start.2) | collective-permute-done | bytes 262176 | tf_op jit(solution)/shard_map/ppermute | solution.py:31
  41.9 4.0 %collective-permute-start.4 = (bf16[4,32,512]{2,1,0:T(8,128)(2,1)S(1)}, bf16[4,32,512]{2,1,0:T(8,128)(2,1)S(1)}, u32[]{:S(2)}, u32[]{:S(2)}) collective-permute-start(bf16[4,32,512]{2,1,0:T(8,128)(2,1)S(1)} %get-tuple-element.33), channel_id=1, source_target_pairs={{0,8},{2,10},{4,12},{6,14},{8,0},{10,2},{12,4},{14,6},{16,24},{18,... | collective-permute-start | bytes 393224 | tf_op jit(solution)/shard_map/ppermute | solution.py:31
  45.8 1.7 %collective-permute-start.5 = (bf16[4,32,512]{2,1,0:T(8,128)(2,1)S(1)}, bf16[4,32,512]{2,1,0:T(8,128)(2,1)S(1)}, u32[]{:S(2)}, u32[]{:S(2)}) collective-permute-start(bf16[4,32,512]{2,1,0:T(8,128)(2,1)S(1)} %get-tuple-element.34), channel_id=1, source_target_pairs={{0,16},{2,18},{4,20},{6,22},{8,24},{10,26},{12,28},{14,30},{16,0},... | collective-permute-start | bytes 393224 | tf_op jit(solution)/shard_map/ppermute | solution.py:31
  49.4 7.5 %collective-permute-done.5.refs_2_ = bf16[4,32,512]{2,1,0:T(8,128)(2,1)S(1)} collective-permute-done((bf16[4,32,512]{2,1,0:T(8,128)(2,1)S(1)}, bf16[4,32,512]{2,1,0:T(8,128)(2,1)S(1)}, u32[]{:S(2)}, u32[]{:S(2)}) %collective-permute-start.5) | collective-permute-done | bytes 131104 | tf_op jit(solution)/shard_map/ppermute | solution.py:31
  57.1 2.2 %collective-permute-start.9 = (f32[8,128]{1,0:T(8,128)S(1)}, f32[8,128]{1,0:T(8,128)S(1)}, u32[]{:S(2)}, u32[]{:S(2)}) collective-permute-start(f32[8,128]{1,0:T(8,128)S(1)} %get-tuple-element.36), channel_id=1, source_target_pairs={{0,24},{2,26},{4,28},{6,30},{8,16},{10,18},{12,20},{14,22},{16,8},... | collective-permute-start | bytes 12296 | tf_op jit(solution)/shard_map/ppermute | solution.py:31
  62.2 1.5 %collective-permute-start.18 = (bf16[32,3712]{1,0:T(8,128)(2,1)S(1)}, bf16[32,3712]{1,0:T(8,128)(2,1)S(1)}, u32[]{:S(2)}, u32[]{:S(2)}) collective-permute-start(bf16[32,3712]{1,0:T(8,128)(2,1)S(1)} %slice.8), channel_id=1, source_target_pairs={{0,4},{2,6},{4,0},{6,2},{8,12},{10,14},{12,8},{14,10},{16,20},{18,... | collective-permute-start | bytes 712712 | tf_op jit(solution)/shard_map/ppermute | solution.py:31
  66.5 1.9 %collective-permute-start.22 = (bf16[4,32,512]{2,1,0:T(8,128)(2,1)S(1)}, bf16[4,32,512]{2,1,0:T(8,128)(2,1)S(1)}, u32[]{:S(2)}, u32[]{:S(2)}) collective-permute-start(bf16[4,32,512]{2,1,0:T(8,128)(2,1)S(1)} %get-tuple-element.43.refs_2_), channel_id=1, source_target_pairs={{0,6},{2,4},{4,2},{6,0},{8,14},{10,12},{12,10},{14,8},{16,22},{18,... | collective-permute-start | bytes 393224 | tf_op jit(solution)/shard_map/ppermute | solution.py:31
  71.1 1.9 %shard_map.73 = (bf16[512,512]{1,0:T(8,128)(2,1)S(1)}, bf16[512,512]{1,0:T(8,128)(2,1)S(1)}, f32[512,512]{1,0:T(8,128)S(1)}, f32[512,512]{1,0:T(8,128)S(1)}) custom-call(s32[4]{0:T(128)S(1)} %pad_add_fusion.where, bf16[32,7168]{1,0:T(8,128)(2,1)S(1)} %shard_map.72.refs_0_, bf16[32,7168]{1,0:T(8,128)(2,1)S(1)} %collective-permute-done.16.refs_1_, ...), custom_call_target="tpu_custom_call" | custom-call | flops 1073741824 | bytes 4980752 | tf_op jit(solution)/shard_map/pallas_call | solution.py:45
  73.0 2.6 %collective-permute-done.12 = f32[8,128]{1,0:T(8,128)S(1)} collective-permute-done((f32[8,128]{1,0:T(8,128)S(1)}, f32[8,128]{1,0:T(8,128)S(1)}, u32[]{:S(2)}, u32[]{:S(2)}) %collective-permute-start.12) | collective-permute-done | bytes 4128 | tf_op jit(solution)/shard_map/ppermute | solution.py:31
  75.7 2.0 %shard_map.74 = (bf16[512,512]{1,0:T(8,128)(2,1)S(1)}, f32[512,512]{1,0:T(8,128)S(1)}, f32[512,512]{1,0:T(8,128)S(1)}, f32[8,128]{1,0:T(8,128)S(1)}) custom-call(s32[4]{0:T(128)S(1)} %pad_add_fusion.where, bf16[512,512]{1,0:T(8,128)(2,1)S(1)} %get-tuple-element.41.refs_0_.refs_2_, bf16[512,512]{1,0:T(8,128)(2,1)S(1)} %get-tuple-element.42.refs_1_.refs_3_, ...), custom_call_target="tpu_custom_call" | custom-call | flops 1073741824 | bytes 4198416 | tf_op jit(solution)/shard_map/pallas_call | solution.py:45
  77.7 2.0 %shard_map.75 = (bf16[32,1536]{1,0:T(8,128)(2,1)S(1)}, bf16[32,1536]{1,0:T(8,128)(2,1)S(1)}, bf16[32,1536]{1,0:T(8,128)(2,1)S(1)}, bf16[32,1536]{1,0:T(8,128)(2,1)S(1)}) custom-call(s32[4]{0:T(128)S(1)} %pad_add_fusion.where, f32[8,128]{1,0:T(8,128)S(1)} %add.56.refs_0_, f32[8,128]{1,0:T(8,128)S(1)} %get-tuple-element.44.refs_1_, ...), custom_call_target="tpu_custom_call" | custom-call | flops 1342177280 | bytes 6168592 | tf_op jit(solution)/shard_map/pallas_call | solution.py:45
  80.8 1.7 %collective-permute-start.24 = (bf16[32,1536]{1,0:T(8,128)(2,1)S(1)}, bf16[32,1536]{1,0:T(8,128)(2,1)S(1)}, u32[]{:S(2)}, u32[]{:S(2)}) collective-permute-start(bf16[32,1536]{1,0:T(8,128)(2,1)S(1)} %get-tuple-element.52), channel_id=1, source_target_pairs={{0,16},{2,18},{4,20},{6,22},{8,24},{10,26},{12,28},{14,30},{16,0},... | collective-permute-start | bytes 294920 | tf_op jit(solution)/shard_map/ppermute | solution.py:31
  82.4 1.7 %collective-permute-start.25 = (bf16[32,1536]{1,0:T(8,128)(2,1)S(1)}, bf16[32,1536]{1,0:T(8,128)(2,1)S(1)}, u32[]{:S(2)}, u32[]{:S(2)}) collective-permute-start(bf16[32,1536]{1,0:T(8,128)(2,1)S(1)} %get-tuple-element.53), channel_id=1, source_target_pairs={{0,24},{2,26},{4,28},{6,30},{8,16},{10,18},{12,20},{14,22},{16,8},... | collective-permute-start | bytes 294920 | tf_op jit(solution)/shard_map/ppermute | solution.py:31
  84.1 1.5 %collective-permute-done.23.refs_1_ = bf16[32,1536]{1,0:T(8,128)(2,1)S(1)} collective-permute-done((bf16[32,1536]{1,0:T(8,128)(2,1)S(1)}, bf16[32,1536]{1,0:T(8,128)(2,1)S(1)}, u32[]{:S(2)}, u32[]{:S(2)}) %collective-permute-start.23) | collective-permute-done | bytes 98336 | tf_op jit(solution)/shard_map/ppermute | solution.py:31
  85.6 5.8 %collective-permute-done.24.refs_2_ = bf16[32,1536]{1,0:T(8,128)(2,1)S(1)} collective-permute-done((bf16[32,1536]{1,0:T(8,128)(2,1)S(1)}, bf16[32,1536]{1,0:T(8,128)(2,1)S(1)}, u32[]{:S(2)}, u32[]{:S(2)}) %collective-permute-start.24) | collective-permute-done | bytes 98336 | tf_op jit(solution)/shard_map/ppermute | solution.py:31
  (56 shorter events, 20.8 us)
Async XLA Ops:
  1.9 26.7 %collective-permute-start = (bf16[4,2,2,32,512]{4,3,2,1,0:T(8,128)(2,1)S(1)}, bf16[4,2,2,32,512]{4,3,2,1,0:T(8,128)(2,1)S(1)}, u32[]{:S(2)}, u32[]{:S(2)}) collective-permute-start(bf16[4,2,2,32,512]{4,3,2,1,0:T(8,128)(2,1)S(1)} %dynamic-slice_bitcast_fusion.1), channel_id=1, source_target_pairs={{0,2},{2,0},{4,6},{6,4},{8,10},{10,8},{12,14},{14,12},{16,18},{18,... | collective-permute-start | bytes 1572872 | tf_op jit(solution)/shard_map/ppermute | solution.py:31
  6.8 21.8 %collective-permute-start.1 = (bf16[4,2,2,32,512]{4,3,2,1,0:T(8,128)(2,1)}, bf16[4,2,2,32,512]{4,3,2,1,0:T(8,128)(2,1)S(1)}, u32[]{:S(2)}, u32[]{:S(2)}) collective-permute-start(bf16[4,2,2,32,512]{4,3,2,1,0:T(8,128)(2,1)} %dynamic-slice_bitcast_fusion), channel_id=1, source_target_pairs={{0,4},{2,6},{4,0},{6,2},{8,12},{10,14},{12,8},{14,10},{16,20},{18,... | collective-permute-start | bytes 1572872 | tf_op jit(solution)/shard_map/ppermute | solution.py:31
  9.3 7.6 %collective-permute-start.13 = (bf16[32,2560]{1,0:T(8,128)(2,1)S(1)}, bf16[32,2560]{1,0:T(8,128)(2,1)S(1)}, u32[]{:S(2)}, u32[]{:S(2)}) collective-permute-start(bf16[32,2560]{1,0:T(8,128)(2,1)S(1)} %get-tuple-element.38), channel_id=1, source_target_pairs={{0,8},{2,10},{4,12},{6,14},{8,0},{10,2},{12,4},{14,6},{16,24},{18,... | collective-permute-start | bytes 491528 | tf_op jit(solution)/shard_map/ppermute | solution.py:31
  11.0 14.8 %collective-permute-start.14 = (bf16[32,2560]{1,0:T(8,128)(2,1)S(1)}, bf16[32,2560]{1,0:T(8,128)(2,1)S(1)}, u32[]{:S(2)}, u32[]{:S(2)}) collective-permute-start(bf16[32,2560]{1,0:T(8,128)(2,1)S(1)} %get-tuple-element.39), channel_id=1, source_target_pairs={{0,16},{2,18},{4,20},{6,22},{8,24},{10,26},{12,28},{14,30},{16,0},... | collective-permute-start | bytes 491528 | tf_op jit(solution)/shard_map/ppermute | solution.py:31
  13.5 12.2 %collective-permute-start.15 = (bf16[32,2560]{1,0:T(8,128)(2,1)S(1)}, bf16[32,2560]{1,0:T(8,128)(2,1)S(1)}, u32[]{:S(2)}, u32[]{:S(2)}) collective-permute-start(bf16[32,2560]{1,0:T(8,128)(2,1)S(1)} %get-tuple-element.40), channel_id=1, source_target_pairs={{0,24},{2,26},{4,28},{6,30},{8,16},{10,18},{12,20},{14,22},{16,8},... | collective-permute-start | bytes 491528 | tf_op jit(solution)/shard_map/ppermute | solution.py:31
  26.4 35.2 %collective-permute-start.17 = (bf16[32,7168]{1,0:T(8,128)(2,1)S(1)}, bf16[32,7168]{1,0:T(8,128)(2,1)S(1)}, u32[]{:S(2)}, u32[]{:S(2)}) collective-permute-start(bf16[32,7168]{1,0:T(8,128)(2,1)S(1)} %shard_map.72.refs_0_), channel_id=1, source_target_pairs={{0,4},{2,6},{4,0},{6,2},{8,12},{10,14},{12,8},{14,10},{16,20},{18,... | collective-permute-start | bytes 1376264 | tf_op jit(solution)/shard_map/ppermute | solution.py:31
  27.0 35.2 %collective-permute-start.16 = (bf16[32,7168]{1,0:T(8,128)(2,1)S(1)}, bf16[32,7168]{1,0:T(8,128)(2,1)S(1)}, u32[]{:S(2)}, u32[]{:S(2)}) collective-permute-start(bf16[32,7168]{1,0:T(8,128)(2,1)S(1)} %shard_map.72.refs_0_), channel_id=1, source_target_pairs={{0,2},{2,0},{4,6},{6,4},{8,10},{10,8},{12,14},{14,12},{16,18},{18,... | collective-permute-start | bytes 1376264 | tf_op jit(solution)/shard_map/ppermute | solution.py:31
  29.4 11.6 %collective-permute-start.2 = (bf16[4,2,32,512]{3,2,1,0:T(8,128)(2,1)S(1)}, bf16[4,2,32,512]{3,2,1,0:T(8,128)(2,1)S(1)}, u32[]{:S(2)}, u32[]{:S(2)}) collective-permute-start(bf16[4,2,32,512]{3,2,1,0:T(8,128)(2,1)S(1)} %get-tuple-element.30), channel_id=1, source_target_pairs={{0,4},{2,6},{4,0},{6,2},{8,12},{10,14},{12,8},{14,10},{16,20},{18,... | collective-permute-start | bytes 786440 | tf_op jit(solution)/shard_map/ppermute | solution.py:31
  31.0 10.3 %collective-permute-start.3 = (bf16[4,2,32,512]{3,2,1,0:T(8,128)(2,1)S(1)}, bf16[4,2,32,512]{3,2,1,0:T(8,128)(2,1)S(1)}, u32[]{:S(2)}, u32[]{:S(2)}) collective-permute-start(bf16[4,2,32,512]{3,2,1,0:T(8,128)(2,1)S(1)} %get-tuple-element.31), channel_id=1, source_target_pairs={{0,2},{2,0},{4,6},{6,4},{8,10},{10,8},{12,14},{14,12},{16,18},{18,... | collective-permute-start | bytes 786440 | tf_op jit(solution)/shard_map/ppermute | solution.py:31
  41.9 7.6 %collective-permute-start.4 = (bf16[4,32,512]{2,1,0:T(8,128)(2,1)S(1)}, bf16[4,32,512]{2,1,0:T(8,128)(2,1)S(1)}, u32[]{:S(2)}, u32[]{:S(2)}) collective-permute-start(bf16[4,32,512]{2,1,0:T(8,128)(2,1)S(1)} %get-tuple-element.33), channel_id=1, source_target_pairs={{0,8},{2,10},{4,12},{6,14},{8,0},{10,2},{12,4},{14,6},{16,24},{18,... | collective-permute-start | bytes 393224 | tf_op jit(solution)/shard_map/ppermute | solution.py:31
  45.8 11.1 %collective-permute-start.5 = (bf16[4,32,512]{2,1,0:T(8,128)(2,1)S(1)}, bf16[4,32,512]{2,1,0:T(8,128)(2,1)S(1)}, u32[]{:S(2)}, u32[]{:S(2)}) collective-permute-start(bf16[4,32,512]{2,1,0:T(8,128)(2,1)S(1)} %get-tuple-element.34), channel_id=1, source_target_pairs={{0,16},{2,18},{4,20},{6,22},{8,24},{10,26},{12,28},{14,30},{16,0},... | collective-permute-start | bytes 393224 | tf_op jit(solution)/shard_map/ppermute | solution.py:31
  47.5 9.4 %collective-permute-start.6 = (bf16[4,32,512]{2,1,0:T(8,128)(2,1)S(1)}, bf16[4,32,512]{2,1,0:T(8,128)(2,1)S(1)}, u32[]{:S(2)}, u32[]{:S(2)}) collective-permute-start(bf16[4,32,512]{2,1,0:T(8,128)(2,1)S(1)} %get-tuple-element.35), channel_id=1, source_target_pairs={{0,24},{2,26},{4,28},{6,30},{8,16},{10,18},{12,20},{14,22},{16,8},... | collective-permute-start | bytes 393224 | tf_op jit(solution)/shard_map/ppermute | solution.py:31
  57.1 6.6 %collective-permute-start.9 = (f32[8,128]{1,0:T(8,128)S(1)}, f32[8,128]{1,0:T(8,128)S(1)}, u32[]{:S(2)}, u32[]{:S(2)}) collective-permute-start(f32[8,128]{1,0:T(8,128)S(1)} %get-tuple-element.36), channel_id=1, source_target_pairs={{0,24},{2,26},{4,28},{6,30},{8,16},{10,18},{12,20},{14,22},{16,8},... | collective-permute-start | bytes 12296 | tf_op jit(solution)/shard_map/ppermute | solution.py:31
  59.3 4.5 %collective-permute-start.8 = (f32[8,128]{1,0:T(8,128)S(1)}, f32[8,128]{1,0:T(8,128)S(1)}, u32[]{:S(2)}, u32[]{:S(2)}) collective-permute-start(f32[8,128]{1,0:T(8,128)S(1)} %get-tuple-element.36), channel_id=1, source_target_pairs={{0,16},{2,18},{4,20},{6,22},{8,24},{10,26},{12,28},{14,30},{16,0},... | collective-permute-start | bytes 12296 | tf_op jit(solution)/shard_map/ppermute | solution.py:31
  60.6 3.6 %collective-permute-start.7 = (f32[8,128]{1,0:T(8,128)S(1)}, f32[8,128]{1,0:T(8,128)S(1)}, u32[]{:S(2)}, u32[]{:S(2)}) collective-permute-start(f32[8,128]{1,0:T(8,128)S(1)} %get-tuple-element.36), channel_id=1, source_target_pairs={{0,8},{2,10},{4,12},{6,14},{8,0},{10,2},{12,4},{14,6},{16,24},{18,... | collective-permute-start | bytes 12296 | tf_op jit(solution)/shard_map/ppermute | solution.py:31
  61.6 8.5 %collective-permute-start.19 = (bf16[32,3456]{1,0:T(8,128)(2,1)S(1)}, bf16[32,3456]{1,0:T(8,128)(2,1)S(1)}, u32[]{:S(2)}, u32[]{:S(2)}) collective-permute-start(bf16[32,3456]{1,0:T(8,128)(2,1)S(1)} %slice.9), channel_id=1, source_target_pairs={{0,2},{2,0},{4,6},{6,4},{8,10},{10,8},{12,14},{14,12},{16,18},{18,... | collective-permute-start | bytes 663560 | tf_op jit(solution)/shard_map/ppermute | solution.py:31
  62.2 8.8 %collective-permute-start.18 = (bf16[32,3712]{1,0:T(8,128)(2,1)S(1)}, bf16[32,3712]{1,0:T(8,128)(2,1)S(1)}, u32[]{:S(2)}, u32[]{:S(2)}) collective-permute-start(bf16[32,3712]{1,0:T(8,128)(2,1)S(1)} %slice.8), channel_id=1, source_target_pairs={{0,4},{2,6},{4,0},{6,2},{8,12},{10,14},{12,8},{14,10},{16,20},{18,... | collective-permute-start | bytes 712712 | tf_op jit(solution)/shard_map/ppermute | solution.py:31
  66.5 9.1 %collective-permute-start.22 = (bf16[4,32,512]{2,1,0:T(8,128)(2,1)S(1)}, bf16[4,32,512]{2,1,0:T(8,128)(2,1)S(1)}, u32[]{:S(2)}, u32[]{:S(2)}) collective-permute-start(bf16[4,32,512]{2,1,0:T(8,128)(2,1)S(1)} %get-tuple-element.43.refs_2_), channel_id=1, source_target_pairs={{0,6},{2,4},{4,2},{6,0},{8,14},{10,12},{12,10},{14,8},{16,22},{18,... | collective-permute-start | bytes 393224 | tf_op jit(solution)/shard_map/ppermute | solution.py:31
  68.4 7.3 %collective-permute-start.21 = (bf16[4,32,512]{2,1,0:T(8,128)(2,1)S(1)}, bf16[4,32,512]{2,1,0:T(8,128)(2,1)S(1)}, u32[]{:S(2)}, u32[]{:S(2)}) collective-permute-start(bf16[4,32,512]{2,1,0:T(8,128)(2,1)S(1)} %get-tuple-element.43.refs_2_), channel_id=1, source_target_pairs={{0,4},{2,6},{4,0},{6,2},{8,12},{10,14},{12,8},{14,10},{16,20},{18,... | collective-permute-start | bytes 393224 | tf_op jit(solution)/shard_map/ppermute | solution.py:31
  69.0 6.6 %collective-permute-start.20 = (bf16[4,32,512]{2,1,0:T(8,128)(2,1)S(1)}, bf16[4,32,512]{2,1,0:T(8,128)(2,1)S(1)}, u32[]{:S(2)}, u32[]{:S(2)}) collective-permute-start(bf16[4,32,512]{2,1,0:T(8,128)(2,1)S(1)} %get-tuple-element.43.refs_2_), channel_id=1, source_target_pairs={{0,2},{2,0},{4,6},{6,4},{8,10},{10,8},{12,14},{14,12},{16,18},{18,... | collective-permute-start | bytes 393224 | tf_op jit(solution)/shard_map/ppermute | solution.py:31
  70.1 5.5 %collective-permute-start.12 = (f32[8,128]{1,0:T(8,128)S(1)}, f32[8,128]{1,0:T(8,128)S(1)}, u32[]{:S(2)}, u32[]{:S(2)}) collective-permute-start(f32[8,128]{1,0:T(8,128)S(1)} %add.55), channel_id=1, source_target_pairs={{0,4},{2,6},{4,0},{6,2},{8,12},{10,14},{12,8},{14,10},{16,20},{18,... | collective-permute-start | bytes 12296 | tf_op jit(solution)/shard_map/ppermute | solution.py:31
  79.7 5.9 %collective-permute-start.23 = (bf16[32,1536]{1,0:T(8,128)(2,1)S(1)}, bf16[32,1536]{1,0:T(8,128)(2,1)S(1)}, u32[]{:S(2)}, u32[]{:S(2)}) collective-permute-start(bf16[32,1536]{1,0:T(8,128)(2,1)S(1)} %get-tuple-element.51), channel_id=1, source_target_pairs={{0,8},{2,10},{4,12},{6,14},{8,0},{10,2},{12,4},{14,6},{16,24},{18,... | collective-permute-start | bytes 294920 | tf_op jit(solution)/shard_map/ppermute | solution.py:31
  80.8 10.6 %collective-permute-start.24 = (bf16[32,1536]{1,0:T(8,128)(2,1)S(1)}, bf16[32,1536]{1,0:T(8,128)(2,1)S(1)}, u32[]{:S(2)}, u32[]{:S(2)}) collective-permute-start(bf16[32,1536]{1,0:T(8,128)(2,1)S(1)} %get-tuple-element.52), channel_id=1, source_target_pairs={{0,16},{2,18},{4,20},{6,22},{8,24},{10,26},{12,28},{14,30},{16,0},... | collective-permute-start | bytes 294920 | tf_op jit(solution)/shard_map/ppermute | solution.py:31
  82.4 9.0 %collective-permute-start.25 = (bf16[32,1536]{1,0:T(8,128)(2,1)S(1)}, bf16[32,1536]{1,0:T(8,128)(2,1)S(1)}, u32[]{:S(2)}, u32[]{:S(2)}) collective-permute-start(bf16[32,1536]{1,0:T(8,128)(2,1)S(1)} %get-tuple-element.53), channel_id=1, source_target_pairs={{0,24},{2,26},{4,28},{6,30},{8,16},{10,18},{12,20},{14,22},{16,8},... | collective-permute-start | bytes 294920 | tf_op jit(solution)/shard_map/ppermute | solution.py:31
  (6 other events, 35.8 us)

commit v6 on v5

--- a/solution.py
+++ b/solution.py
@@ -40,7 +40,7 @@
     return jnp.stack([pick(stacked, own ^ k, 0) for k in range(len(pieces))])
 
 
-def call(kernel, out_shape, scratch, flops, smem, *operands, space=pltpu.VMEM):
+def call(kernel, out_shape, scratch, flops, smem, *operands, space=pltpu.VMEM, grant=VMEM_GRANT):
     moved = sum(x.size * x.dtype.itemsize for x in (*operands, *jax.tree.leaves(out_shape)))
     return pl.pallas_call(
         kernel,
@@ -49,7 +49,7 @@
         out_specs=jax.tree.map(lambda _: VMEM_SPEC, out_shape),
         scratch_shapes=scratch,
         cost_estimate=pl.CostEstimate(flops=flops, bytes_accessed=moved, transcendentals=0),
-        compiler_params=pltpu.CompilerParams(vmem_limit_bytes=VMEM_GRANT),
+        compiler_params=pltpu.CompilerParams(vmem_limit_bytes=grant),
     )(*operands)
 
 
@@ -136,6 +136,23 @@
     gram_columns(right_gram, conjugate)
 
 
+def cut_kernel(where, grads, low_out, high_out, done):
+    blocks, middle = low_out.shape[:2]
+    copies = []
+    for block in range(blocks):
+        for z in range(middle):
+            for high in range(2):
+                source = grads.at[block, z, high, 1 - where[2]]
+                copies.append((source, low_out.at[block, z, high]))
+            source = grads.at[block, middle + z, 1 - where[3]]
+            copies.append((source, high_out.at[block, z]))
+    copies = [pltpu.make_async_copy(*pair, done.at[i]) for i, pair in enumerate(copies)]
+    for copy in copies:
+        copy.start()
+    for copy in copies:
+        copy.wait()
+
+
 def relay_kernel(where, own, low_own, low_seen, high_own, high_seen, kept, low_out, high_out):
     middle = own.shape[1] // 2
 
@@ -282,7 +299,8 @@
 def place_kernel(plan, where, slots, old_state, *refs):
     pieces, (precond, new_state) = refs[: plan.blocks], refs[plan.blocks :]
     size = plan.size
-    new_state[...] = old_state[...]
+    if new_state.shape[0] > plan.blocks:
+        new_state[...] = old_state[...]
     for k, piece in enumerate(pieces):
         precond[where[0] ^ k] = piece[:, 2 * size :]
         new_state[slots[where[0] ^ k]] = piece[:, : 2 * size]
@@ -326,8 +344,19 @@
             cut = lax.dynamic_slice(array, [0 if i is None else i for i in start], extent)
             return cut.reshape([n for i, n in enumerate(extent) if n > 1 or i not in (2, 3)])
 
-        low_seen = flip(part(grads, 0, None, 1 - my_low), devices, 1)
-        high_seen = flip(part(grads, 1, 1 - my_high, None), devices, 2)
+        first = call(
+            cut_kernel,
+            (shaped((blocks, middle, 2, rows, columns)),) * 2,
+            [pltpu.SemaphoreType.DMA((3 * blocks * middle,))],
+            0,
+            1,
+            where,
+            grads.reshape(blocks, blocks, 2, 2, rows, columns),
+            space=pltpu.HBM,
+            grant=None,
+        )
+        low_seen = flip(first[0], devices, 1)
+        high_seen = flip(first[1], devices, 2)
         kept, low_sent, high_sent = call(
             relay_kernel,
             (shaped((blocks, blocks, rows, columns), FLOAT),)
@@ -383,6 +412,7 @@
             inverse_factors[0],
             probes[0],
             space=pltpu.HBM,
+            grant=None,
         )
     else:
         wide = jnp.concatenate([old_state, inverse_factors[0], probes[0]], axis=2)

time: 93 us -> 96.8 us (1.041)
  Pallas kernels: 10.4 us -> 15.5 us
  local copies, waits for them, and re-layouts: 5.24 us -> 3.12 us
    pallas_call x9 -> x10, Pallas kernels: 10.4 us -> 15.5 us  [call(): pl.pallas_call(kernel, out_shape=out_shape, in_specs=[SMEM_SPEC] * smem +...]
    reshape x4 -> x2, local copies, waits for them, and re-layouts: 5.19 us -> 2.15 us  [part(): cut.reshape([n for i, n in enumerate(extent) if n > 1 or i not in (2, 3)])]
  transfers between devices with their start and end apart: 26 -> 26, of which waited for: 13 -> 13; matrix products, arithmetic and copies ran while one was open for 4% -> 2% of each run, Pallas kernels for 5% -> 7%
where the time goes in v6:
time: 96.8 us; the launch traced here: 96.4 us
  waiting for transfers between devices  39.6 us (41%)
  starting transfers between devices  36.8 us (38%)
  Pallas kernels  15.5 us (16%)
  local copies, waits for them, and re-layouts  3.12 us (3%)
    ppermute x25, waiting for transfers between devices, flip(): return lax.ppermute(array, 'dp', [(i, i ^ mask) for i in range(devices)])  38.4 us
    ppermute x25, starting transfers between devices, flip(): return lax.ppermute(array, 'dp', [(i, i ^ mask) for i in range(devices)])  36.8 us
    pallas_call x10, Pallas kernels, call(): pl.pallas_call(kernel, out_shape=out_shape, in_specs=[SMEM_SPEC] * smem +...  15.5 us
    reshape x2, local copies, waits for them, and re-layouts, part(): cut.reshape([n for i, n in enumerate(extent) if n > 1 or i not in (2, 3)])  2.15 us
  transfers between devices with their start and end apart: 26, of which 13 were waited for; matrix products, arithmetic and copies ran while one was open for 2% of the time, Pallas kernels for 7%

profile of v6, /device:TPU:0, one launch (start us, length us, event | category | flops | bytes accessed | tf_op | source)
XLA Modules:
  0.0 96.4 jit_solution(2943901441298400093)
XLA Ops:
  1.3 3.2 %shard_map.68 = (bf16[4,2,2,32,512]{4,3,2,1,0:T(8,128)(2,1)}, bf16[4,2,2,32,512]{4,3,2,1,0:T(8,128)(2,1)}) custom-call(s32[4]{0:T(128)} %pad_add_fusion.where, bf16[4,4,2,2,32,512]{5,4,3,2,1,0:T(8,128)(2,1)} %bitcast.21), custom_call_target="tpu_custom_call" | custom-call | bytes 3145744 | tf_op jit(solution)/shard_map/pallas_call | solution.py:45
  4.5 3.0 %collective-permute-start = (bf16[4,2,2,32,512]{4,3,2,1,0:T(8,128)(2,1)}, bf16[4,2,2,32,512]{4,3,2,1,0:T(8,128)(2,1)S(1)}, u32[]{:S(2)}, u32[]{:S(2)}) collective-permute-start(bf16[4,2,2,32,512]{4,3,2,1,0:T(8,128)(2,1)} %get-tuple-element.31), channel_id=1, source_target_pairs={{0,2},{2,0},{4,6},{6,4},{8,10},{10,8},{12,14},{14,12},{16,18},{18,... | collective-permute-start | bytes 1572872 | tf_op jit(solution)/shard_map/ppermute | solution.py:31
  7.5 1.5 %collective-permute-start.1 = (bf16[4,2,2,32,512]{4,3,2,1,0:T(8,128)(2,1)}, bf16[4,2,2,32,512]{4,3,2,1,0:T(8,128)(2,1)S(1)}, u32[]{:S(2)}, u32[]{:S(2)}) collective-permute-start(bf16[4,2,2,32,512]{4,3,2,1,0:T(8,128)(2,1)} %get-tuple-element.32), channel_id=1, source_target_pairs={{0,4},{2,6},{4,0},{6,2},{8,12},{10,14},{12,8},{14,10},{16,20},{18,... | collective-permute-start | bytes 1572872 | tf_op jit(solution)/shard_map/ppermute | solution.py:31
  9.1 2.7 %shard_map.72 = (bf16[32,2560]{1,0:T(8,128)(2,1)}, bf16[32,2560]{1,0:T(8,128)(2,1)}, bf16[32,2560]{1,0:T(8,128)(2,1)}, bf16[32,2560]{1,0:T(8,128)(2,1)}) custom-call(s32[4]{0:T(128)} %pad_add_fusion.where, s32[4]{0:T(128)} %bitcast.19, bf16[4,32,1024]{2,1,0:T(8,128)(2,1)} %bitcast.17, bf16[4,32,1024]{2,1,0:T(8,128)(2,1)} %bitcast.24, ...), custom_call_target="tpu_custom_call" | custom-call | bytes 1310752 | tf_op jit(solution)/shard_map/pallas_call | solution.py:45
  11.8 1.6 %collective-permute-start.13 = (bf16[32,2560]{1,0:T(8,128)(2,1)}, bf16[32,2560]{1,0:T(8,128)(2,1)S(1)}, u32[]{:S(2)}, u32[]{:S(2)}) collective-permute-start(bf16[32,2560]{1,0:T(8,128)(2,1)} %get-tuple-element.42), channel_id=1, source_target_pairs={{0,8},{2,10},{4,12},{6,14},{8,0},{10,2},{12,4},{14,6},{16,24},{18,... | collective-permute-start | bytes 491528 | tf_op jit(solution)/shard_map/ppermute | solution.py:31
  13.4 2.6 %collective-permute-start.14 = (bf16[32,2560]{1,0:T(8,128)(2,1)}, bf16[32,2560]{1,0:T(8,128)(2,1)S(1)}, u32[]{:S(2)}, u32[]{:S(2)}) collective-permute-start(bf16[32,2560]{1,0:T(8,128)(2,1)} %get-tuple-element.43), channel_id=1, source_target_pairs={{0,16},{2,18},{4,20},{6,22},{8,24},{10,26},{12,28},{14,30},{16,0},... | collective-permute-start | bytes 491528 | tf_op jit(solution)/shard_map/ppermute | solution.py:31
  17.3 2.2 %collective-permute-done.13.refs_1_ = bf16[32,2560]{1,0:T(8,128)(2,1)S(1)} collective-permute-done((bf16[32,2560]{1,0:T(8,128)(2,1)}, bf16[32,2560]{1,0:T(8,128)(2,1)S(1)}, u32[]{:S(2)}, u32[]{:S(2)}) %collective-permute-start.13) | collective-permute-done | bytes 163872 | tf_op jit(solution)/shard_map/ppermute | solution.py:31
  19.6 8.9 %collective-permute-done.14.refs_2_ = bf16[32,2560]{1,0:T(8,128)(2,1)S(1)} collective-permute-done((bf16[32,2560]{1,0:T(8,128)(2,1)}, bf16[32,2560]{1,0:T(8,128)(2,1)S(1)}, u32[]{:S(2)}, u32[]{:S(2)}) %collective-permute-start.14) | collective-permute-done | bytes 163872 | tf_op jit(solution)/shard_map/ppermute | solution.py:31
  33.0 1.6 %collective-permute-start.2 = (bf16[4,2,32,512]{3,2,1,0:T(8,128)(2,1)S(1)}, bf16[4,2,32,512]{3,2,1,0:T(8,128)(2,1)S(1)}, u32[]{:S(2)}, u32[]{:S(2)}) collective-permute-start(bf16[4,2,32,512]{3,2,1,0:T(8,128)(2,1)S(1)} %get-tuple-element.34), channel_id=1, source_target_pairs={{0,4},{2,6},{4,0},{6,2},{8,12},{10,14},{12,8},{14,10},{16,20},{18,... | collective-permute-start | bytes 786440 | tf_op jit(solution)/shard_map/ppermute | solution.py:31
  34.6 1.5 %collective-permute-start.3 = (bf16[4,2,32,512]{3,2,1,0:T(8,128)(2,1)S(1)}, bf16[4,2,32,512]{3,2,1,0:T(8,128)(2,1)S(1)}, u32[]{:S(2)}, u32[]{:S(2)}) collective-permute-start(bf16[4,2,32,512]{3,2,1,0:T(8,128)(2,1)S(1)} %get-tuple-element.35), channel_id=1, source_target_pairs={{0,2},{2,0},{4,6},{6,4},{8,10},{10,8},{12,14},{14,12},{16,18},{18,... | collective-permute-start | bytes 786440 | tf_op jit(solution)/shard_map/ppermute | solution.py:31
  36.1 8.5 %collective-permute-done.2.low_last = bf16[4,2,32,512]{3,2,1,0:T(8,128)(2,1)S(1)} collective-permute-done((bf16[4,2,32,512]{3,2,1,0:T(8,128)(2,1)S(1)}, bf16[4,2,32,512]{3,2,1,0:T(8,128)(2,1)S(1)}, u32[]{:S(2)}, u32[]{:S(2)}) %collective-permute-start.2) | collective-permute-done | bytes 262176 | tf_op jit(solution)/shard_map/ppermute | solution.py:31
  45.5 4.0 %collective-permute-start.4 = (bf16[4,32,512]{2,1,0:T(8,128)(2,1)S(1)}, bf16[4,32,512]{2,1,0:T(8,128)(2,1)S(1)}, u32[]{:S(2)}, u32[]{:S(2)}) collective-permute-start(bf16[4,32,512]{2,1,0:T(8,128)(2,1)S(1)} %get-tuple-element.37), channel_id=1, source_target_pairs={{0,8},{2,10},{4,12},{6,14},{8,0},{10,2},{12,4},{14,6},{16,24},{18,... | collective-permute-start | bytes 393224 | tf_op jit(solution)/shard_map/ppermute | solution.py:31
  49.4 1.7 %collective-permute-start.5 = (bf16[4,32,512]{2,1,0:T(8,128)(2,1)S(1)}, bf16[4,32,512]{2,1,0:T(8,128)(2,1)S(1)}, u32[]{:S(2)}, u32[]{:S(2)}) collective-permute-start(bf16[4,32,512]{2,1,0:T(8,128)(2,1)S(1)} %get-tuple-element.38), channel_id=1, source_target_pairs={{0,16},{2,18},{4,20},{6,22},{8,24},{10,26},{12,28},{14,30},{16,0},... | collective-permute-start | bytes 393224 | tf_op jit(solution)/shard_map/ppermute | solution.py:31
  53.0 7.5 %collective-permute-done.5.refs_2_ = bf16[4,32,512]{2,1,0:T(8,128)(2,1)S(1)} collective-permute-done((bf16[4,32,512]{2,1,0:T(8,128)(2,1)S(1)}, bf16[4,32,512]{2,1,0:T(8,128)(2,1)S(1)}, u32[]{:S(2)}, u32[]{:S(2)}) %collective-permute-start.5) | collective-permute-done | bytes 131104 | tf_op jit(solution)/shard_map/ppermute | solution.py:31
  60.7 2.2 %collective-permute-start.9 = (f32[8,128]{1,0:T(8,128)S(1)}, f32[8,128]{1,0:T(8,128)S(1)}, u32[]{:S(2)}, u32[]{:S(2)}) collective-permute-start(f32[8,128]{1,0:T(8,128)S(1)} %get-tuple-element.40), channel_id=1, source_target_pairs={{0,24},{2,26},{4,28},{6,30},{8,16},{10,18},{12,20},{14,22},{16,8},... | collective-permute-start | bytes 12296 | tf_op jit(solution)/shard_map/ppermute | solution.py:31
  65.8 1.5 %collective-permute-start.18 = (bf16[32,3712]{1,0:T(8,128)(2,1)S(1)}, bf16[32,3712]{1,0:T(8,128)(2,1)S(1)}, u32[]{:S(2)}, u32[]{:S(2)}) collective-permute-start(bf16[32,3712]{1,0:T(8,128)(2,1)S(1)} %slice.8), channel_id=1, source_target_pairs={{0,4},{2,6},{4,0},{6,2},{8,12},{10,14},{12,8},{14,10},{16,20},{18,... | collective-permute-start | bytes 712712 | tf_op jit(solution)/shard_map/ppermute | solution.py:31
  70.1 1.9 %collective-permute-start.22 = (bf16[4,32,512]{2,1,0:T(8,128)(2,1)S(1)}, bf16[4,32,512]{2,1,0:T(8,128)(2,1)S(1)}, u32[]{:S(2)}, u32[]{:S(2)}) collective-permute-start(bf16[4,32,512]{2,1,0:T(8,128)(2,1)S(1)} %get-tuple-element.47.refs_2_), channel_id=1, source_target_pairs={{0,6},{2,4},{4,2},{6,0},{8,14},{10,12},{12,10},{14,8},{16,22},{18,... | collective-permute-start | bytes 393224 | tf_op jit(solution)/shard_map/ppermute | solution.py:31
  74.7 2.0 %shard_map.74 = (bf16[512,512]{1,0:T(8,128)(2,1)S(1)}, bf16[512,512]{1,0:T(8,128)(2,1)S(1)}, f32[512,512]{1,0:T(8,128)S(1)}, f32[512,512]{1,0:T(8,128)S(1)}) custom-call(s32[4]{0:T(128)S(1)} %copy-done.2, bf16[32,7168]{1,0:T(8,128)(2,1)S(1)} %shard_map.73.refs_0_, bf16[32,7168]{1,0:T(8,128)(2,1)S(1)} %collective-permute-done.16.refs_1_, ...), custom_call_target="tpu_custom_call" | custom-call | flops 1073741824 | bytes 4980752 | tf_op jit(solution)/shard_map/pallas_call | solution.py:45
  76.6 2.6 %collective-permute-done.12 = f32[8,128]{1,0:T(8,128)S(1)} collective-permute-done((f32[8,128]{1,0:T(8,128)S(1)}, f32[8,128]{1,0:T(8,128)S(1)}, u32[]{:S(2)}, u32[]{:S(2)}) %collective-permute-start.12) | collective-permute-done | bytes 4128 | tf_op jit(solution)/shard_map/ppermute | solution.py:31
  79.3 2.1 %shard_map.75 = (bf16[512,512]{1,0:T(8,128)(2,1)S(1)}, f32[512,512]{1,0:T(8,128)S(1)}, f32[512,512]{1,0:T(8,128)S(1)}, f32[8,128]{1,0:T(8,128)S(1)}) custom-call(s32[4]{0:T(128)S(1)} %copy-done.2, bf16[512,512]{1,0:T(8,128)(2,1)S(1)} %get-tuple-element.45.refs_0_.refs_2_, bf16[512,512]{1,0:T(8,128)(2,1)S(1)} %get-tuple-element.46.refs_1_.refs_3_, ...), custom_call_target="tpu_custom_call" | custom-call | flops 1073741824 | bytes 4198416 | tf_op jit(solution)/shard_map/pallas_call | solution.py:45
  81.3 2.0 %shard_map.76 = (bf16[32,1536]{1,0:T(8,128)(2,1)S(1)}, bf16[32,1536]{1,0:T(8,128)(2,1)S(1)}, bf16[32,1536]{1,0:T(8,128)(2,1)S(1)}, bf16[32,1536]{1,0:T(8,128)(2,1)S(1)}) custom-call(s32[4]{0:T(128)S(1)} %copy-done.2, f32[8,128]{1,0:T(8,128)S(1)} %add.54.refs_0_, f32[8,128]{1,0:T(8,128)S(1)} %get-tuple-element.48.refs_1_, ...), custom_call_target="tpu_custom_call" | custom-call | flops 1342177280 | bytes 6168592 | tf_op jit(solution)/shard_map/pallas_call | solution.py:45
  84.4 1.7 %collective-permute-start.24 = (bf16[32,1536]{1,0:T(8,128)(2,1)S(1)}, bf16[32,1536]{1,0:T(8,128)(2,1)S(1)}, u32[]{:S(2)}, u32[]{:S(2)}) collective-permute-start(bf16[32,1536]{1,0:T(8,128)(2,1)S(1)} %get-tuple-element.56), channel_id=1, source_target_pairs={{0,16},{2,18},{4,20},{6,22},{8,24},{10,26},{12,28},{14,30},{16,0},... | collective-permute-start | bytes 294920 | tf_op jit(solution)/shard_map/ppermute | solution.py:31
  86.1 1.7 %collective-permute-start.25 = (bf16[32,1536]{1,0:T(8,128)(2,1)S(1)}, bf16[32,1536]{1,0:T(8,128)(2,1)S(1)}, u32[]{:S(2)}, u32[]{:S(2)}) collective-permute-start(bf16[32,1536]{1,0:T(8,128)(2,1)S(1)} %get-tuple-element.57), channel_id=1, source_target_pairs={{0,24},{2,26},{4,28},{6,30},{8,16},{10,18},{12,20},{14,22},{16,8},... | collective-permute-start | bytes 294920 | tf_op jit(solution)/shard_map/ppermute | solution.py:31
  89.2 5.8 %collective-permute-done.24.refs_2_ = bf16[32,1536]{1,0:T(8,128)(2,1)S(1)} collective-permute-done((bf16[32,1536]{1,0:T(8,128)(2,1)S(1)}, bf16[32,1536]{1,0:T(8,128)(2,1)S(1)}, u32[]{:S(2)}, u32[]{:S(2)}) %collective-permute-start.24) | collective-permute-done | bytes 98336 | tf_op jit(solution)/shard_map/ppermute | solution.py:31
  (55 shorter events, 21.6 us)
Async XLA Ops:
  4.5 27.7 %collective-permute-start = (bf16[4,2,2,32,512]{4,3,2,1,0:T(8,128)(2,1)}, bf16[4,2,2,32,512]{4,3,2,1,0:T(8,128)(2,1)S(1)}, u32[]{:S(2)}, u32[]{:S(2)}) collective-permute-start(bf16[4,2,2,32,512]{4,3,2,1,0:T(8,128)(2,1)} %get-tuple-element.31), channel_id=1, source_target_pairs={{0,2},{2,0},{4,6},{6,4},{8,10},{10,8},{12,14},{14,12},{16,18},{18,... | collective-permute-start | bytes 1572872 | tf_op jit(solution)/shard_map/ppermute | solution.py:31
  7.5 24.7 %collective-permute-start.1 = (bf16[4,2,2,32,512]{4,3,2,1,0:T(8,128)(2,1)}, bf16[4,2,2,32,512]{4,3,2,1,0:T(8,128)(2,1)S(1)}, u32[]{:S(2)}, u32[]{:S(2)}) collective-permute-start(bf16[4,2,2,32,512]{4,3,2,1,0:T(8,128)(2,1)} %get-tuple-element.32), channel_id=1, source_target_pairs={{0,4},{2,6},{4,0},{6,2},{8,12},{10,14},{12,8},{14,10},{16,20},{18,... | collective-permute-start | bytes 1572872 | tf_op jit(solution)/shard_map/ppermute | solution.py:31
  11.8 7.8 %collective-permute-start.13 = (bf16[32,2560]{1,0:T(8,128)(2,1)}, bf16[32,2560]{1,0:T(8,128)(2,1)S(1)}, u32[]{:S(2)}, u32[]{:S(2)}) collective-permute-start(bf16[32,2560]{1,0:T(8,128)(2,1)} %get-tuple-element.42), channel_id=1, source_target_pairs={{0,8},{2,10},{4,12},{6,14},{8,0},{10,2},{12,4},{14,6},{16,24},{18,... | collective-permute-start | bytes 491528 | tf_op jit(solution)/shard_map/ppermute | solution.py:31
  13.4 15.0 %collective-permute-start.14 = (bf16[32,2560]{1,0:T(8,128)(2,1)}, bf16[32,2560]{1,0:T(8,128)(2,1)S(1)}, u32[]{:S(2)}, u32[]{:S(2)}) collective-permute-start(bf16[32,2560]{1,0:T(8,128)(2,1)} %get-tuple-element.43), channel_id=1, source_target_pairs={{0,16},{2,18},{4,20},{6,22},{8,24},{10,26},{12,28},{14,30},{16,0},... | collective-permute-start | bytes 491528 | tf_op jit(solution)/shard_map/ppermute | solution.py:31
  16.0 12.4 %collective-permute-start.15 = (bf16[32,2560]{1,0:T(8,128)(2,1)}, bf16[32,2560]{1,0:T(8,128)(2,1)S(1)}, u32[]{:S(2)}, u32[]{:S(2)}) collective-permute-start(bf16[32,2560]{1,0:T(8,128)(2,1)} %get-tuple-element.44), channel_id=1, source_target_pairs={{0,24},{2,26},{4,28},{6,30},{8,16},{10,18},{12,20},{14,22},{16,8},... | collective-permute-start | bytes 491528 | tf_op jit(solution)/shard_map/ppermute | solution.py:31
  30.0 35.2 %collective-permute-start.17 = (bf16[32,7168]{1,0:T(8,128)(2,1)S(1)}, bf16[32,7168]{1,0:T(8,128)(2,1)S(1)}, u32[]{:S(2)}, u32[]{:S(2)}) collective-permute-start(bf16[32,7168]{1,0:T(8,128)(2,1)S(1)} %shard_map.73.refs_0_), channel_id=1, source_target_pairs={{0,4},{2,6},{4,0},{6,2},{8,12},{10,14},{12,8},{14,10},{16,20},{18,... | collective-permute-start | bytes 1376264 | tf_op jit(solution)/shard_map/ppermute | solution.py:31
  30.6 35.2 %collective-permute-start.16 = (bf16[32,7168]{1,0:T(8,128)(2,1)S(1)}, bf16[32,7168]{1,0:T(8,128)(2,1)S(1)}, u32[]{:S(2)}, u32[]{:S(2)}) collective-permute-start(bf16[32,7168]{1,0:T(8,128)(2,1)S(1)} %shard_map.73.refs_0_), channel_id=1, source_target_pairs={{0,2},{2,0},{4,6},{6,4},{8,10},{10,8},{12,14},{14,12},{16,18},{18,... | collective-permute-start | bytes 1376264 | tf_op jit(solution)/shard_map/ppermute | solution.py:31
  33.0 11.6 %collective-permute-start.2 = (bf16[4,2,32,512]{3,2,1,0:T(8,128)(2,1)S(1)}, bf16[4,2,32,512]{3,2,1,0:T(8,128)(2,1)S(1)}, u32[]{:S(2)}, u32[]{:S(2)}) collective-permute-start(bf16[4,2,32,512]{3,2,1,0:T(8,128)(2,1)S(1)} %get-tuple-element.34), channel_id=1, source_target_pairs={{0,4},{2,6},{4,0},{6,2},{8,12},{10,14},{12,8},{14,10},{16,20},{18,... | collective-permute-start | bytes 786440 | tf_op jit(solution)/shard_map/ppermute | solution.py:31
  34.6 10.3 %collective-permute-start.3 = (bf16[4,2,32,512]{3,2,1,0:T(8,128)(2,1)S(1)}, bf16[4,2,32,512]{3,2,1,0:T(8,128)(2,1)S(1)}, u32[]{:S(2)}, u32[]{:S(2)}) collective-permute-start(bf16[4,2,32,512]{3,2,1,0:T(8,128)(2,1)S(1)} %get-tuple-element.35), channel_id=1, source_target_pairs={{0,2},{2,0},{4,6},{6,4},{8,10},{10,8},{12,14},{14,12},{16,18},{18,... | collective-permute-start | bytes 786440 | tf_op jit(solution)/shard_map/ppermute | solution.py:31
  45.5 7.6 %collective-permute-start.4 = (bf16[4,32,512]{2,1,0:T(8,128)(2,1)S(1)}, bf16[4,32,512]{2,1,0:T(8,128)(2,1)S(1)}, u32[]{:S(2)}, u32[]{:S(2)}) collective-permute-start(bf16[4,32,512]{2,1,0:T(8,128)(2,1)S(1)} %get-tuple-element.37), channel_id=1, source_target_pairs={{0,8},{2,10},{4,12},{6,14},{8,0},{10,2},{12,4},{14,6},{16,24},{18,... | collective-permute-start | bytes 393224 | tf_op jit(solution)/shard_map/ppermute | solution.py:31
  49.4 11.1 %collective-permute-start.5 = (bf16[4,32,512]{2,1,0:T(8,128)(2,1)S(1)}, bf16[4,32,512]{2,1,0:T(8,128)(2,1)S(1)}, u32[]{:S(2)}, u32[]{:S(2)}) collective-permute-start(bf16[4,32,512]{2,1,0:T(8,128)(2,1)S(1)} %get-tuple-element.38), channel_id=1, source_target_pairs={{0,16},{2,18},{4,20},{6,22},{8,24},{10,26},{12,28},{14,30},{16,0},... | collective-permute-start | bytes 393224 | tf_op jit(solution)/shard_map/ppermute | solution.py:31
  51.1 9.4 %collective-permute-start.6 = (bf16[4,32,512]{2,1,0:T(8,128)(2,1)S(1)}, bf16[4,32,512]{2,1,0:T(8,128)(2,1)S(1)}, u32[]{:S(2)}, u32[]{:S(2)}) collective-permute-start(bf16[4,32,512]{2,1,0:T(8,128)(2,1)S(1)} %get-tuple-element.39), channel_id=1, source_target_pairs={{0,24},{2,26},{4,28},{6,30},{8,16},{10,18},{12,20},{14,22},{16,8},... | collective-permute-start | bytes 393224 | tf_op jit(solution)/shard_map/ppermute | solution.py:31
  60.7 6.6 %collective-permute-start.9 = (f32[8,128]{1,0:T(8,128)S(1)}, f32[8,128]{1,0:T(8,128)S(1)}, u32[]{:S(2)}, u32[]{:S(2)}) collective-permute-start(f32[8,128]{1,0:T(8,128)S(1)} %get-tuple-element.40), channel_id=1, source_target_pairs={{0,24},{2,26},{4,28},{6,30},{8,16},{10,18},{12,20},{14,22},{16,8},... | collective-permute-start | bytes 12296 | tf_op jit(solution)/shard_map/ppermute | solution.py:31
  62.9 4.5 %collective-permute-start.8 = (f32[8,128]{1,0:T(8,128)S(1)}, f32[8,128]{1,0:T(8,128)S(1)}, u32[]{:S(2)}, u32[]{:S(2)}) collective-permute-start(f32[8,128]{1,0:T(8,128)S(1)} %get-tuple-element.40), channel_id=1, source_target_pairs={{0,16},{2,18},{4,20},{6,22},{8,24},{10,26},{12,28},{14,30},{16,0},... | collective-permute-start | bytes 12296 | tf_op jit(solution)/shard_map/ppermute | solution.py:31
  64.2 3.6 %collective-permute-start.7 = (f32[8,128]{1,0:T(8,128)S(1)}, f32[8,128]{1,0:T(8,128)S(1)}, u32[]{:S(2)}, u32[]{:S(2)}) collective-permute-start(f32[8,128]{1,0:T(8,128)S(1)} %get-tuple-element.40), channel_id=1, source_target_pairs={{0,8},{2,10},{4,12},{6,14},{8,0},{10,2},{12,4},{14,6},{16,24},{18,... | collective-permute-start | bytes 12296 | tf_op jit(solution)/shard_map/ppermute | solution.py:31
  65.2 8.5 %collective-permute-start.19 = (bf16[32,3456]{1,0:T(8,128)(2,1)S(1)}, bf16[32,3456]{1,0:T(8,128)(2,1)S(1)}, u32[]{:S(2)}, u32[]{:S(2)}) collective-permute-start(bf16[32,3456]{1,0:T(8,128)(2,1)S(1)} %slice.9), channel_id=1, source_target_pairs={{0,2},{2,0},{4,6},{6,4},{8,10},{10,8},{12,14},{14,12},{16,18},{18,... | collective-permute-start | bytes 663560 | tf_op jit(solution)/shard_map/ppermute | solution.py:31
  65.8 8.8 %collective-permute-start.18 = (bf16[32,3712]{1,0:T(8,128)(2,1)S(1)}, bf16[32,3712]{1,0:T(8,128)(2,1)S(1)}, u32[]{:S(2)}, u32[]{:S(2)}) collective-permute-start(bf16[32,3712]{1,0:T(8,128)(2,1)S(1)} %slice.8), channel_id=1, source_target_pairs={{0,4},{2,6},{4,0},{6,2},{8,12},{10,14},{12,8},{14,10},{16,20},{18,... | collective-permute-start | bytes 712712 | tf_op jit(solution)/shard_map/ppermute | solution.py:31
  70.1 9.1 %collective-permute-start.22 = (bf16[4,32,512]{2,1,0:T(8,128)(2,1)S(1)}, bf16[4,32,512]{2,1,0:T(8,128)(2,1)S(1)}, u32[]{:S(2)}, u32[]{:S(2)}) collective-permute-start(bf16[4,32,512]{2,1,0:T(8,128)(2,1)S(1)} %get-tuple-element.47.refs_2_), channel_id=1, source_target_pairs={{0,6},{2,4},{4,2},{6,0},{8,14},{10,12},{12,10},{14,8},{16,22},{18,... | collective-permute-start | bytes 393224 | tf_op jit(solution)/shard_map/ppermute | solution.py:31
  72.0 7.3 %collective-permute-start.21 = (bf16[4,32,512]{2,1,0:T(8,128)(2,1)S(1)}, bf16[4,32,512]{2,1,0:T(8,128)(2,1)S(1)}, u32[]{:S(2)}, u32[]{:S(2)}) collective-permute-start(bf16[4,32,512]{2,1,0:T(8,128)(2,1)S(1)} %get-tuple-element.47.refs_2_), channel_id=1, source_target_pairs={{0,4},{2,6},{4,0},{6,2},{8,12},{10,14},{12,8},{14,10},{16,20},{18,... | collective-permute-start | bytes 393224 | tf_op jit(solution)/shard_map/ppermute | solution.py:31
  72.6 6.6 %collective-permute-start.20 = (bf16[4,32,512]{2,1,0:T(8,128)(2,1)S(1)}, bf16[4,32,512]{2,1,0:T(8,128)(2,1)S(1)}, u32[]{:S(2)}, u32[]{:S(2)}) collective-permute-start(bf16[4,32,512]{2,1,0:T(8,128)(2,1)S(1)} %get-tuple-element.47.refs_2_), channel_id=1, source_target_pairs={{0,2},{2,0},{4,6},{6,4},{8,10},{10,8},{12,14},{14,12},{16,18},{18,... | collective-permute-start | bytes 393224 | tf_op jit(solution)/shard_map/ppermute | solution.py:31
  73.7 5.5 %collective-permute-start.12 = (f32[8,128]{1,0:T(8,128)S(1)}, f32[8,128]{1,0:T(8,128)S(1)}, u32[]{:S(2)}, u32[]{:S(2)}) collective-permute-start(f32[8,128]{1,0:T(8,128)S(1)} %add.53), channel_id=1, source_target_pairs={{0,4},{2,6},{4,0},{6,2},{8,12},{10,14},{12,8},{14,10},{16,20},{18,... | collective-permute-start | bytes 12296 | tf_op jit(solution)/shard_map/ppermute | solution.py:31
  83.3 5.9 %collective-permute-start.23 = (bf16[32,1536]{1,0:T(8,128)(2,1)S(1)}, bf16[32,1536]{1,0:T(8,128)(2,1)S(1)}, u32[]{:S(2)}, u32[]{:S(2)}) collective-permute-start(bf16[32,1536]{1,0:T(8,128)(2,1)S(1)} %get-tuple-element.55), channel_id=1, source_target_pairs={{0,8},{2,10},{4,12},{6,14},{8,0},{10,2},{12,4},{14,6},{16,24},{18,... | collective-permute-start | bytes 294920 | tf_op jit(solution)/shard_map/ppermute | solution.py:31
  84.4 10.6 %collective-permute-start.24 = (bf16[32,1536]{1,0:T(8,128)(2,1)S(1)}, bf16[32,1536]{1,0:T(8,128)(2,1)S(1)}, u32[]{:S(2)}, u32[]{:S(2)}) collective-permute-start(bf16[32,1536]{1,0:T(8,128)(2,1)S(1)} %get-tuple-element.56), channel_id=1, source_target_pairs={{0,16},{2,18},{4,20},{6,22},{8,24},{10,26},{12,28},{14,30},{16,0},... | collective-permute-start | bytes 294920 | tf_op jit(solution)/shard_map/ppermute | solution.py:31
  86.1 9.0 %collective-permute-start.25 = (bf16[32,1536]{1,0:T(8,128)(2,1)S(1)}, bf16[32,1536]{1,0:T(8,128)(2,1)S(1)}, u32[]{:S(2)}, u32[]{:S(2)}) collective-permute-start(bf16[32,1536]{1,0:T(8,128)(2,1)S(1)} %get-tuple-element.57), channel_id=1, source_target_pairs={{0,24},{2,26},{4,28},{6,30},{8,16},{10,18},{12,20},{14,22},{16,8},... | collective-permute-start | bytes 294920 | tf_op jit(solution)/shard_map/ppermute | solution.py:31
  (6 other events, 60.4 us)

commit v7 on v5

--- a/solution.py
+++ b/solution.py
@@ -28,7 +28,8 @@
 
 
 def flip(array, devices, mask):
-    return lax.ppermute(array, "dp", [(i, i ^ mask) for i in range(devices)])
+    pairs = [(i, i ^ mask) for i in range(devices)]
+    return lax.ppermute(array, "dp", pairs)
 
 
 def pick(array, index, axis):
@@ -326,8 +327,9 @@
             cut = lax.dynamic_slice(array, [0 if i is None else i for i in start], extent)
             return cut.reshape([n for i, n in enumerate(extent) if n > 1 or i not in (2, 3)])
 
-        low_seen = flip(part(grads, 0, None, 1 - my_low), devices, 1)
-        high_seen = flip(part(grads, 1, 1 - my_high, None), devices, 2)
+        first = part(grads, 0, None, 1 - my_low), part(grads, 1, 1 - my_high, None)
+        low_seen = flip(first[0], devices, 1)
+        high_seen = flip(first[1], devices, 2)
         kept, low_sent, high_sent = call(
             relay_kernel,
             (shaped((blocks, blocks, rows, columns), FLOAT),)

time: 93 us -> 93 us (level)
  no operation moved by 1% of the time
where the time goes in v7:
time: 93 us; the launch traced here: 92.8 us
  waiting for transfers between devices  39.4 us (42%)
  starting transfers between devices  36.8 us (40%)
  Pallas kernels  10.4 us (11%)
  local copies, waits for them, and re-layouts  5.24 us (6%)
    ppermute x25, waiting for transfers between devices, flip(): return lax.ppermute(array, 'dp', pairs)  38.2 us
    ppermute x25, starting transfers between devices, flip(): return lax.ppermute(array, 'dp', pairs)  36.8 us
    pallas_call x9, Pallas kernels, call(): pl.pallas_call(kernel, out_shape=out_shape, in_specs=[SMEM_SPEC] * smem +...  10.4 us
    reshape x4, local copies, waits for them, and re-layouts, part(): cut.reshape([n for i, n in enumerate(extent) if n > 1 or i not in (2, 3)])  5.19 us
  transfers between devices with their start and end apart: 26, of which 13 were waited for; matrix products, arithmetic and copies ran while one was open for 4% of the time, Pallas kernels for 5%

profile of v7, /device:TPU:0, one launch (start us, length us, event | category | flops | bytes accessed | tf_op | source)
XLA Modules:
  0.0 92.8 jit_solution(11053137260621691498)
XLA Ops:
  1.9 3.0 %collective-permute-start = (bf16[4,2,2,32,512]{4,3,2,1,0:T(8,128)(2,1)S(1)}, bf16[4,2,2,32,512]{4,3,2,1,0:T(8,128)(2,1)S(1)}, u32[]{:S(2)}, u32[]{:S(2)}) collective-permute-start(bf16[4,2,2,32,512]{4,3,2,1,0:T(8,128)(2,1)S(1)} %dynamic-slice_bitcast_fusion.1), channel_id=1, source_target_pairs={{0,2},{2,0},{4,6},{6,4},{8,10},{10,8},{12,14},{14,12},{16,18},{18,... | collective-permute-start | bytes 1572872 | tf_op jit(solution)/shard_map/ppermute | solution.py:32
  4.9 1.9 %dynamic-slice_bitcast_fusion = bf16[4,2,2,32,512]{4,3,2,1,0:T(8,128)(2,1)} fusion(bf16[4,4,2,2,32,512]{5,4,3,2,1,0:T(8,128)(2,1)} %bitcast.38, s32[]{:T(128)S(6)} %select_n.40), kind=kLoop, calls=%fused_computation | loop fusion | bytes 1048580 | tf_op jit(solution)/shard_map/reshape | solution.py:328
  6.8 1.5 %collective-permute-start.1 = (bf16[4,2,2,32,512]{4,3,2,1,0:T(8,128)(2,1)}, bf16[4,2,2,32,512]{4,3,2,1,0:T(8,128)(2,1)S(1)}, u32[]{:S(2)}, u32[]{:S(2)}) collective-permute-start(bf16[4,2,2,32,512]{4,3,2,1,0:T(8,128)(2,1)} %dynamic-slice_bitcast_fusion), channel_id=1, source_target_pairs={{0,4},{2,6},{4,0},{6,2},{8,12},{10,14},{12,8},{14,10},{16,20},{18,... | collective-permute-start | bytes 1572872 | tf_op jit(solution)/shard_map/ppermute | solution.py:32
  9.3 1.6 %collective-permute-start.13 = (bf16[32,2560]{1,0:T(8,128)(2,1)S(1)}, bf16[32,2560]{1,0:T(8,128)(2,1)S(1)}, u32[]{:S(2)}, u32[]{:S(2)}) collective-permute-start(bf16[32,2560]{1,0:T(8,128)(2,1)S(1)} %get-tuple-element.38), channel_id=1, source_target_pairs={{0,8},{2,10},{4,12},{6,14},{8,0},{10,2},{12,4},{14,6},{16,24},{18,... | collective-permute-start | bytes 491528 | tf_op jit(solution)/shard_map/ppermute | solution.py:32
  11.0 2.6 %collective-permute-start.14 = (bf16[32,2560]{1,0:T(8,128)(2,1)S(1)}, bf16[32,2560]{1,0:T(8,128)(2,1)S(1)}, u32[]{:S(2)}, u32[]{:S(2)}) collective-permute-start(bf16[32,2560]{1,0:T(8,128)(2,1)S(1)} %get-tuple-element.39), channel_id=1, source_target_pairs={{0,16},{2,18},{4,20},{6,22},{8,24},{10,26},{12,28},{14,30},{16,0},... | collective-permute-start | bytes 491528 | tf_op jit(solution)/shard_map/ppermute | solution.py:32
  14.9 2.0 %collective-permute-done.13.refs_1_ = bf16[32,2560]{1,0:T(8,128)(2,1)S(1)} collective-permute-done((bf16[32,2560]{1,0:T(8,128)(2,1)S(1)}, bf16[32,2560]{1,0:T(8,128)(2,1)S(1)}, u32[]{:S(2)}, u32[]{:S(2)}) %collective-permute-start.13) | collective-permute-done | bytes 163872 | tf_op jit(solution)/shard_map/ppermute | solution.py:32
  16.9 8.9 %collective-permute-done.14.refs_2_ = bf16[32,2560]{1,0:T(8,128)(2,1)S(1)} collective-permute-done((bf16[32,2560]{1,0:T(8,128)(2,1)S(1)}, bf16[32,2560]{1,0:T(8,128)(2,1)S(1)}, u32[]{:S(2)}, u32[]{:S(2)}) %collective-permute-start.14) | collective-permute-done | bytes 163872 | tf_op jit(solution)/shard_map/ppermute | solution.py:32
  29.4 1.6 %collective-permute-start.2 = (bf16[4,2,32,512]{3,2,1,0:T(8,128)(2,1)S(1)}, bf16[4,2,32,512]{3,2,1,0:T(8,128)(2,1)S(1)}, u32[]{:S(2)}, u32[]{:S(2)}) collective-permute-start(bf16[4,2,32,512]{3,2,1,0:T(8,128)(2,1)S(1)} %get-tuple-element.30), channel_id=1, source_target_pairs={{0,4},{2,6},{4,0},{6,2},{8,12},{10,14},{12,8},{14,10},{16,20},{18,... | collective-permute-start | bytes 786440 | tf_op jit(solution)/shard_map/ppermute | solution.py:32
  31.0 1.5 %collective-permute-start.3 = (bf16[4,2,32,512]{3,2,1,0:T(8,128)(2,1)S(1)}, bf16[4,2,32,512]{3,2,1,0:T(8,128)(2,1)S(1)}, u32[]{:S(2)}, u32[]{:S(2)}) collective-permute-start(bf16[4,2,32,512]{3,2,1,0:T(8,128)(2,1)S(1)} %get-tuple-element.31), channel_id=1, source_target_pairs={{0,2},{2,0},{4,6},{6,4},{8,10},{10,8},{12,14},{14,12},{16,18},{18,... | collective-permute-start | bytes 786440 | tf_op jit(solution)/shard_map/ppermute | solution.py:32
  32.5 8.5 %collective-permute-done.2.low_last = bf16[4,2,32,512]{3,2,1,0:T(8,128)(2,1)S(1)} collective-permute-done((bf16[4,2,32,512]{3,2,1,0:T(8,128)(2,1)S(1)}, bf16[4,2,32,512]{3,2,1,0:T(8,128)(2,1)S(1)}, u32[]{:S(2)}, u32[]{:S(2)}) %collective-permute-start.2) | collective-permute-done | bytes 262176 | tf_op jit(solution)/shard_map/ppermute | solution.py:32
  41.9 4.0 %collective-permute-start.4 = (bf16[4,32,512]{2,1,0:T(8,128)(2,1)S(1)}, bf16[4,32,512]{2,1,0:T(8,128)(2,1)S(1)}, u32[]{:S(2)}, u32[]{:S(2)}) collective-permute-start(bf16[4,32,512]{2,1,0:T(8,128)(2,1)S(1)} %get-tuple-element.33), channel_id=1, source_target_pairs={{0,8},{2,10},{4,12},{6,14},{8,0},{10,2},{12,4},{14,6},{16,24},{18,... | collective-permute-start | bytes 393224 | tf_op jit(solution)/shard_map/ppermute | solution.py:32
  45.8 1.7 %collective-permute-start.5 = (bf16[4,32,512]{2,1,0:T(8,128)(2,1)S(1)}, bf16[4,32,512]{2,1,0:T(8,128)(2,1)S(1)}, u32[]{:S(2)}, u32[]{:S(2)}) collective-permute-start(bf16[4,32,512]{2,1,0:T(8,128)(2,1)S(1)} %get-tuple-element.34), channel_id=1, source_target_pairs={{0,16},{2,18},{4,20},{6,22},{8,24},{10,26},{12,28},{14,30},{16,0},... | collective-permute-start | bytes 393224 | tf_op jit(solution)/shard_map/ppermute | solution.py:32
  49.4 7.5 %collective-permute-done.5.refs_2_ = bf16[4,32,512]{2,1,0:T(8,128)(2,1)S(1)} collective-permute-done((bf16[4,32,512]{2,1,0:T(8,128)(2,1)S(1)}, bf16[4,32,512]{2,1,0:T(8,128)(2,1)S(1)}, u32[]{:S(2)}, u32[]{:S(2)}) %collective-permute-start.5) | collective-permute-done | bytes 131104 | tf_op jit(solution)/shard_map/ppermute | solution.py:32
  57.1 2.2 %collective-permute-start.9 = (f32[8,128]{1,0:T(8,128)S(1)}, f32[8,128]{1,0:T(8,128)S(1)}, u32[]{:S(2)}, u32[]{:S(2)}) collective-permute-start(f32[8,128]{1,0:T(8,128)S(1)} %get-tuple-element.36), channel_id=1, source_target_pairs={{0,24},{2,26},{4,28},{6,30},{8,16},{10,18},{12,20},{14,22},{16,8},... | collective-permute-start | bytes 12296 | tf_op jit(solution)/shard_map/ppermute | solution.py:32
  62.2 1.5 %collective-permute-start.18 = (bf16[32,3712]{1,0:T(8,128)(2,1)S(1)}, bf16[32,3712]{1,0:T(8,128)(2,1)S(1)}, u32[]{:S(2)}, u32[]{:S(2)}) collective-permute-start(bf16[32,3712]{1,0:T(8,128)(2,1)S(1)} %slice.8), channel_id=1, source_target_pairs={{0,4},{2,6},{4,0},{6,2},{8,12},{10,14},{12,8},{14,10},{16,20},{18,... | collective-permute-start | bytes 712712 | tf_op jit(solution)/shard_map/ppermute | solution.py:32
  66.5 1.9 %collective-permute-start.22 = (bf16[4,32,512]{2,1,0:T(8,128)(2,1)S(1)}, bf16[4,32,512]{2,1,0:T(8,128)(2,1)S(1)}, u32[]{:S(2)}, u32[]{:S(2)}) collective-permute-start(bf16[4,32,512]{2,1,0:T(8,128)(2,1)S(1)} %get-tuple-element.43.refs_2_), channel_id=1, source_target_pairs={{0,6},{2,4},{4,2},{6,0},{8,14},{10,12},{12,10},{14,8},{16,22},{18,... | collective-permute-start | bytes 393224 | tf_op jit(solution)/shard_map/ppermute | solution.py:32
  71.1 1.9 %shard_map.73 = (bf16[512,512]{1,0:T(8,128)(2,1)S(1)}, bf16[512,512]{1,0:T(8,128)(2,1)S(1)}, f32[512,512]{1,0:T(8,128)S(1)}, f32[512,512]{1,0:T(8,128)S(1)}) custom-call(s32[4]{0:T(128)S(1)} %pad_add_fusion.where, bf16[32,7168]{1,0:T(8,128)(2,1)S(1)} %shard_map.72.refs_0_, bf16[32,7168]{1,0:T(8,128)(2,1)S(1)} %collective-permute-done.16.refs_1_, ...), custom_call_target="tpu_custom_call" | custom-call | flops 1073741824 | bytes 4980752 | tf_op jit(solution)/shard_map/pallas_call | solution.py:46
  73.0 2.6 %collective-permute-done.12 = f32[8,128]{1,0:T(8,128)S(1)} collective-permute-done((f32[8,128]{1,0:T(8,128)S(1)}, f32[8,128]{1,0:T(8,128)S(1)}, u32[]{:S(2)}, u32[]{:S(2)}) %collective-permute-start.12) | collective-permute-done | bytes 4128 | tf_op jit(solution)/shard_map/ppermute | solution.py:32
  75.7 2.0 %shard_map.74 = (bf16[512,512]{1,0:T(8,128)(2,1)S(1)}, f32[512,512]{1,0:T(8,128)S(1)}, f32[512,512]{1,0:T(8,128)S(1)}, f32[8,128]{1,0:T(8,128)S(1)}) custom-call(s32[4]{0:T(128)S(1)} %pad_add_fusion.where, bf16[512,512]{1,0:T(8,128)(2,1)S(1)} %get-tuple-element.41.refs_0_.refs_2_, bf16[512,512]{1,0:T(8,128)(2,1)S(1)} %get-tuple-element.42.refs_1_.refs_3_, ...), custom_call_target="tpu_custom_call" | custom-call | flops 1073741824 | bytes 4198416 | tf_op jit(solution)/shard_map/pallas_call | solution.py:46
  77.7 2.0 %shard_map.75 = (bf16[32,1536]{1,0:T(8,128)(2,1)S(1)}, bf16[32,1536]{1,0:T(8,128)(2,1)S(1)}, bf16[32,1536]{1,0:T(8,128)(2,1)S(1)}, bf16[32,1536]{1,0:T(8,128)(2,1)S(1)}) custom-call(s32[4]{0:T(128)S(1)} %pad_add_fusion.where, f32[8,128]{1,0:T(8,128)S(1)} %add.56.refs_0_, f32[8,128]{1,0:T(8,128)S(1)} %get-tuple-element.44.refs_1_, ...), custom_call_target="tpu_custom_call" | custom-call | flops 1342177280 | bytes 6168592 | tf_op jit(solution)/shard_map/pallas_call | solution.py:46
  80.8 1.7 %collective-permute-start.24 = (bf16[32,1536]{1,0:T(8,128)(2,1)S(1)}, bf16[32,1536]{1,0:T(8,128)(2,1)S(1)}, u32[]{:S(2)}, u32[]{:S(2)}) collective-permute-start(bf16[32,1536]{1,0:T(8,128)(2,1)S(1)} %get-tuple-element.52), channel_id=1, source_target_pairs={{0,16},{2,18},{4,20},{6,22},{8,24},{10,26},{12,28},{14,30},{16,0},... | collective-permute-start | bytes 294920 | tf_op jit(solution)/shard_map/ppermute | solution.py:32
  82.4 1.7 %collective-permute-start.25 = (bf16[32,1536]{1,0:T(8,128)(2,1)S(1)}, bf16[32,1536]{1,0:T(8,128)(2,1)S(1)}, u32[]{:S(2)}, u32[]{:S(2)}) collective-permute-start(bf16[32,1536]{1,0:T(8,128)(2,1)S(1)} %get-tuple-element.53), channel_id=1, source_target_pairs={{0,24},{2,26},{4,28},{6,30},{8,16},{10,18},{12,20},{14,22},{16,8},... | collective-permute-start | bytes 294920 | tf_op jit(solution)/shard_map/ppermute | solution.py:32
  84.1 1.5 %collective-permute-done.23.refs_1_ = bf16[32,1536]{1,0:T(8,128)(2,1)S(1)} collective-permute-done((bf16[32,1536]{1,0:T(8,128)(2,1)S(1)}, bf16[32,1536]{1,0:T(8,128)(2,1)S(1)}, u32[]{:S(2)}, u32[]{:S(2)}) %collective-permute-start.23) | collective-permute-done | bytes 98336 | tf_op jit(solution)/shard_map/ppermute | solution.py:32
  85.6 5.8 %collective-permute-done.24.refs_2_ = bf16[32,1536]{1,0:T(8,128)(2,1)S(1)} collective-permute-done((bf16[32,1536]{1,0:T(8,128)(2,1)S(1)}, bf16[32,1536]{1,0:T(8,128)(2,1)S(1)}, u32[]{:S(2)}, u32[]{:S(2)}) %collective-permute-start.24) | collective-permute-done | bytes 98336 | tf_op jit(solution)/shard_map/ppermute | solution.py:32
  (56 shorter events, 20.8 us)
Async XLA Ops:
  1.9 26.7 %collective-permute-start = (bf16[4,2,2,32,512]{4,3,2,1,0:T(8,128)(2,1)S(1)}, bf16[4,2,2,32,512]{4,3,2,1,0:T(8,128)(2,1)S(1)}, u32[]{:S(2)}, u32[]{:S(2)}) collective-permute-start(bf16[4,2,2,32,512]{4,3,2,1,0:T(8,128)(2,1)S(1)} %dynamic-slice_bitcast_fusion.1), channel_id=1, source_target_pairs={{0,2},{2,0},{4,6},{6,4},{8,10},{10,8},{12,14},{14,12},{16,18},{18,... | collective-permute-start | bytes 1572872 | tf_op jit(solution)/shard_map/ppermute | solution.py:32
  6.8 21.8 %collective-permute-start.1 = (bf16[4,2,2,32,512]{4,3,2,1,0:T(8,128)(2,1)}, bf16[4,2,2,32,512]{4,3,2,1,0:T(8,128)(2,1)S(1)}, u32[]{:S(2)}, u32[]{:S(2)}) collective-permute-start(bf16[4,2,2,32,512]{4,3,2,1,0:T(8,128)(2,1)} %dynamic-slice_bitcast_fusion), channel_id=1, source_target_pairs={{0,4},{2,6},{4,0},{6,2},{8,12},{10,14},{12,8},{14,10},{16,20},{18,... | collective-permute-start | bytes 1572872 | tf_op jit(solution)/shard_map/ppermute | solution.py:32
  9.3 7.6 %collective-permute-start.13 = (bf16[32,2560]{1,0:T(8,128)(2,1)S(1)}, bf16[32,2560]{1,0:T(8,128)(2,1)S(1)}, u32[]{:S(2)}, u32[]{:S(2)}) collective-permute-start(bf16[32,2560]{1,0:T(8,128)(2,1)S(1)} %get-tuple-element.38), channel_id=1, source_target_pairs={{0,8},{2,10},{4,12},{6,14},{8,0},{10,2},{12,4},{14,6},{16,24},{18,... | collective-permute-start | bytes 491528 | tf_op jit(solution)/shard_map/ppermute | solution.py:32
  11.0 14.8 %collective-permute-start.14 = (bf16[32,2560]{1,0:T(8,128)(2,1)S(1)}, bf16[32,2560]{1,0:T(8,128)(2,1)S(1)}, u32[]{:S(2)}, u32[]{:S(2)}) collective-permute-start(bf16[32,2560]{1,0:T(8,128)(2,1)S(1)} %get-tuple-element.39), channel_id=1, source_target_pairs={{0,16},{2,18},{4,20},{6,22},{8,24},{10,26},{12,28},{14,30},{16,0},... | collective-permute-start | bytes 491528 | tf_op jit(solution)/shard_map/ppermute | solution.py:32
  13.5 12.2 %collective-permute-start.15 = (bf16[32,2560]{1,0:T(8,128)(2,1)S(1)}, bf16[32,2560]{1,0:T(8,128)(2,1)S(1)}, u32[]{:S(2)}, u32[]{:S(2)}) collective-permute-start(bf16[32,2560]{1,0:T(8,128)(2,1)S(1)} %get-tuple-element.40), channel_id=1, source_target_pairs={{0,24},{2,26},{4,28},{6,30},{8,16},{10,18},{12,20},{14,22},{16,8},... | collective-permute-start | bytes 491528 | tf_op jit(solution)/shard_map/ppermute | solution.py:32
  26.4 35.2 %collective-permute-start.17 = (bf16[32,7168]{1,0:T(8,128)(2,1)S(1)}, bf16[32,7168]{1,0:T(8,128)(2,1)S(1)}, u32[]{:S(2)}, u32[]{:S(2)}) collective-permute-start(bf16[32,7168]{1,0:T(8,128)(2,1)S(1)} %shard_map.72.refs_0_), channel_id=1, source_target_pairs={{0,4},{2,6},{4,0},{6,2},{8,12},{10,14},{12,8},{14,10},{16,20},{18,... | collective-permute-start | bytes 1376264 | tf_op jit(solution)/shard_map/ppermute | solution.py:32
  27.0 35.2 %collective-permute-start.16 = (bf16[32,7168]{1,0:T(8,128)(2,1)S(1)}, bf16[32,7168]{1,0:T(8,128)(2,1)S(1)}, u32[]{:S(2)}, u32[]{:S(2)}) collective-permute-start(bf16[32,7168]{1,0:T(8,128)(2,1)S(1)} %shard_map.72.refs_0_), channel_id=1, source_target_pairs={{0,2},{2,0},{4,6},{6,4},{8,10},{10,8},{12,14},{14,12},{16,18},{18,... | collective-permute-start | bytes 1376264 | tf_op jit(solution)/shard_map/ppermute | solution.py:32
  29.4 11.6 %collective-permute-start.2 = (bf16[4,2,32,512]{3,2,1,0:T(8,128)(2,1)S(1)}, bf16[4,2,32,512]{3,2,1,0:T(8,128)(2,1)S(1)}, u32[]{:S(2)}, u32[]{:S(2)}) collective-permute-start(bf16[4,2,32,512]{3,2,1,0:T(8,128)(2,1)S(1)} %get-tuple-element.30), channel_id=1, source_target_pairs={{0,4},{2,6},{4,0},{6,2},{8,12},{10,14},{12,8},{14,10},{16,20},{18,... | collective-permute-start | bytes 786440 | tf_op jit(solution)/shard_map/ppermute | solution.py:32
  31.0 10.3 %collective-permute-start.3 = (bf16[4,2,32,512]{3,2,1,0:T(8,128)(2,1)S(1)}, bf16[4,2,32,512]{3,2,1,0:T(8,128)(2,1)S(1)}, u32[]{:S(2)}, u32[]{:S(2)}) collective-permute-start(bf16[4,2,32,512]{3,2,1,0:T(8,128)(2,1)S(1)} %get-tuple-element.31), channel_id=1, source_target_pairs={{0,2},{2,0},{4,6},{6,4},{8,10},{10,8},{12,14},{14,12},{16,18},{18,... | collective-permute-start | bytes 786440 | tf_op jit(solution)/shard_map/ppermute | solution.py:32
  41.9 7.6 %collective-permute-start.4 = (bf16[4,32,512]{2,1,0:T(8,128)(2,1)S(1)}, bf16[4,32,512]{2,1,0:T(8,128)(2,1)S(1)}, u32[]{:S(2)}, u32[]{:S(2)}) collective-permute-start(bf16[4,32,512]{2,1,0:T(8,128)(2,1)S(1)} %get-tuple-element.33), channel_id=1, source_target_pairs={{0,8},{2,10},{4,12},{6,14},{8,0},{10,2},{12,4},{14,6},{16,24},{18,... | collective-permute-start | bytes 393224 | tf_op jit(solution)/shard_map/ppermute | solution.py:32
  45.8 11.1 %collective-permute-start.5 = (bf16[4,32,512]{2,1,0:T(8,128)(2,1)S(1)}, bf16[4,32,512]{2,1,0:T(8,128)(2,1)S(1)}, u32[]{:S(2)}, u32[]{:S(2)}) collective-permute-start(bf16[4,32,512]{2,1,0:T(8,128)(2,1)S(1)} %get-tuple-element.34), channel_id=1, source_target_pairs={{0,16},{2,18},{4,20},{6,22},{8,24},{10,26},{12,28},{14,30},{16,0},... | collective-permute-start | bytes 393224 | tf_op jit(solution)/shard_map/ppermute | solution.py:32
  47.5 9.4 %collective-permute-start.6 = (bf16[4,32,512]{2,1,0:T(8,128)(2,1)S(1)}, bf16[4,32,512]{2,1,0:T(8,128)(2,1)S(1)}, u32[]{:S(2)}, u32[]{:S(2)}) collective-permute-start(bf16[4,32,512]{2,1,0:T(8,128)(2,1)S(1)} %get-tuple-element.35), channel_id=1, source_target_pairs={{0,24},{2,26},{4,28},{6,30},{8,16},{10,18},{12,20},{14,22},{16,8},... | collective-permute-start | bytes 393224 | tf_op jit(solution)/shard_map/ppermute | solution.py:32
  57.1 6.6 %collective-permute-start.9 = (f32[8,128]{1,0:T(8,128)S(1)}, f32[8,128]{1,0:T(8,128)S(1)}, u32[]{:S(2)}, u32[]{:S(2)}) collective-permute-start(f32[8,128]{1,0:T(8,128)S(1)} %get-tuple-element.36), channel_id=1, source_target_pairs={{0,24},{2,26},{4,28},{6,30},{8,16},{10,18},{12,20},{14,22},{16,8},... | collective-permute-start | bytes 12296 | tf_op jit(solution)/shard_map/ppermute | solution.py:32
  59.3 4.5 %collective-permute-start.8 = (f32[8,128]{1,0:T(8,128)S(1)}, f32[8,128]{1,0:T(8,128)S(1)}, u32[]{:S(2)}, u32[]{:S(2)}) collective-permute-start(f32[8,128]{1,0:T(8,128)S(1)} %get-tuple-element.36), channel_id=1, source_target_pairs={{0,16},{2,18},{4,20},{6,22},{8,24},{10,26},{12,28},{14,30},{16,0},... | collective-permute-start | bytes 12296 | tf_op jit(solution)/shard_map/ppermute | solution.py:32
  60.6 3.6 %collective-permute-start.7 = (f32[8,128]{1,0:T(8,128)S(1)}, f32[8,128]{1,0:T(8,128)S(1)}, u32[]{:S(2)}, u32[]{:S(2)}) collective-permute-start(f32[8,128]{1,0:T(8,128)S(1)} %get-tuple-element.36), channel_id=1, source_target_pairs={{0,8},{2,10},{4,12},{6,14},{8,0},{10,2},{12,4},{14,6},{16,24},{18,... | collective-permute-start | bytes 12296 | tf_op jit(solution)/shard_map/ppermute | solution.py:32
  61.6 8.5 %collective-permute-start.19 = (bf16[32,3456]{1,0:T(8,128)(2,1)S(1)}, bf16[32,3456]{1,0:T(8,128)(2,1)S(1)}, u32[]{:S(2)}, u32[]{:S(2)}) collective-permute-start(bf16[32,3456]{1,0:T(8,128)(2,1)S(1)} %slice.9), channel_id=1, source_target_pairs={{0,2},{2,0},{4,6},{6,4},{8,10},{10,8},{12,14},{14,12},{16,18},{18,... | collective-permute-start | bytes 663560 | tf_op jit(solution)/shard_map/ppermute | solution.py:32
  62.2 8.8 %collective-permute-start.18 = (bf16[32,3712]{1,0:T(8,128)(2,1)S(1)}, bf16[32,3712]{1,0:T(8,128)(2,1)S(1)}, u32[]{:S(2)}, u32[]{:S(2)}) collective-permute-start(bf16[32,3712]{1,0:T(8,128)(2,1)S(1)} %slice.8), channel_id=1, source_target_pairs={{0,4},{2,6},{4,0},{6,2},{8,12},{10,14},{12,8},{14,10},{16,20},{18,... | collective-permute-start | bytes 712712 | tf_op jit(solution)/shard_map/ppermute | solution.py:32
  66.5 9.1 %collective-permute-start.22 = (bf16[4,32,512]{2,1,0:T(8,128)(2,1)S(1)}, bf16[4,32,512]{2,1,0:T(8,128)(2,1)S(1)}, u32[]{:S(2)}, u32[]{:S(2)}) collective-permute-start(bf16[4,32,512]{2,1,0:T(8,128)(2,1)S(1)} %get-tuple-element.43.refs_2_), channel_id=1, source_target_pairs={{0,6},{2,4},{4,2},{6,0},{8,14},{10,12},{12,10},{14,8},{16,22},{18,... | collective-permute-start | bytes 393224 | tf_op jit(solution)/shard_map/ppermute | solution.py:32
  68.4 7.3 %collective-permute-start.21 = (bf16[4,32,512]{2,1,0:T(8,128)(2,1)S(1)}, bf16[4,32,512]{2,1,0:T(8,128)(2,1)S(1)}, u32[]{:S(2)}, u32[]{:S(2)}) collective-permute-start(bf16[4,32,512]{2,1,0:T(8,128)(2,1)S(1)} %get-tuple-element.43.refs_2_), channel_id=1, source_target_pairs={{0,4},{2,6},{4,0},{6,2},{8,12},{10,14},{12,8},{14,10},{16,20},{18,... | collective-permute-start | bytes 393224 | tf_op jit(solution)/shard_map/ppermute | solution.py:32
  69.0 6.6 %collective-permute-start.20 = (bf16[4,32,512]{2,1,0:T(8,128)(2,1)S(1)}, bf16[4,32,512]{2,1,0:T(8,128)(2,1)S(1)}, u32[]{:S(2)}, u32[]{:S(2)}) collective-permute-start(bf16[4,32,512]{2,1,0:T(8,128)(2,1)S(1)} %get-tuple-element.43.refs_2_), channel_id=1, source_target_pairs={{0,2},{2,0},{4,6},{6,4},{8,10},{10,8},{12,14},{14,12},{16,18},{18,... | collective-permute-start | bytes 393224 | tf_op jit(solution)/shard_map/ppermute | solution.py:32
  70.1 5.5 %collective-permute-start.12 = (f32[8,128]{1,0:T(8,128)S(1)}, f32[8,128]{1,0:T(8,128)S(1)}, u32[]{:S(2)}, u32[]{:S(2)}) collective-permute-start(f32[8,128]{1,0:T(8,128)S(1)} %add.55), channel_id=1, source_target_pairs={{0,4},{2,6},{4,0},{6,2},{8,12},{10,14},{12,8},{14,10},{16,20},{18,... | collective-permute-start | bytes 12296 | tf_op jit(solution)/shard_map/ppermute | solution.py:32
  79.7 5.9 %collective-permute-start.23 = (bf16[32,1536]{1,0:T(8,128)(2,1)S(1)}, bf16[32,1536]{1,0:T(8,128)(2,1)S(1)}, u32[]{:S(2)}, u32[]{:S(2)}) collective-permute-start(bf16[32,1536]{1,0:T(8,128)(2,1)S(1)} %get-tuple-element.51), channel_id=1, source_target_pairs={{0,8},{2,10},{4,12},{6,14},{8,0},{10,2},{12,4},{14,6},{16,24},{18,... | collective-permute-start | bytes 294920 | tf_op jit(solution)/shard_map/ppermute | solution.py:32
  80.8 10.6 %collective-permute-start.24 = (bf16[32,1536]{1,0:T(8,128)(2,1)S(1)}, bf16[32,1536]{1,0:T(8,128)(2,1)S(1)}, u32[]{:S(2)}, u32[]{:S(2)}) collective-permute-start(bf16[32,1536]{1,0:T(8,128)(2,1)S(1)} %get-tuple-element.52), channel_id=1, source_target_pairs={{0,16},{2,18},{4,20},{6,22},{8,24},{10,26},{12,28},{14,30},{16,0},... | collective-permute-start | bytes 294920 | tf_op jit(solution)/shard_map/ppermute | solution.py:32
  82.4 9.0 %collective-permute-start.25 = (bf16[32,1536]{1,0:T(8,128)(2,1)S(1)}, bf16[32,1536]{1,0:T(8,128)(2,1)S(1)}, u32[]{:S(2)}, u32[]{:S(2)}) collective-permute-start(bf16[32,1536]{1,0:T(8,128)(2,1)S(1)} %get-tuple-element.53), channel_id=1, source_target_pairs={{0,24},{2,26},{4,28},{6,30},{8,16},{10,18},{12,20},{14,22},{16,8},... | collective-permute-start | bytes 294920 | tf_op jit(solution)/shard_map/ppermute | solution.py:32
  (6 other events, 35.8 us)
